TPU v7x, 32 devices: a whole 2x2x4 slice. The times are simulated.
32 devices in a mesh: rep: 4 (over y, x), shard: 8 (over z, core).
Axes of the slice: x: 2, y: 2, z: 4, core: 2. Of those that a mesh axis runs over, the one named last changes fastest.
Arguments:
- tokens: bfloat16 [16, 2048, 768], P('shard', 'rep'), may hold values from -6 to 6
- segment_ids: int32 [16, 2048], P('shard'), may hold values from 0 to 7, never falling along the last dimension, each value on 1 to 1024 neighbouring positions
- cotangent: bfloat16 [16, 2048, 768], P('shard', 'rep'), may hold values from -6 to 6
- query_weight: bfloat16 [768, 768], P('shard'), may hold values from -0.3125 to 0.3125
- key_weight: bfloat16 [768, 768], P('shard'), may hold values from -0.3125 to 0.3125
- value_weight: bfloat16 [768, 768], P('shard'), may hold values from -0.21875 to 0.21875
- output_weight: bfloat16 [768, 768], P('shard'), may hold values from -1.5 to 1.5
- expand_weight: bfloat16 [768, 3072], P('shard'), may hold values from -0.21875 to 0.21875
- reduce_weight: bfloat16 [3072, 768], P('shard'), may hold values from -0.109375 to 0.109375
- query_bias: bfloat16 [768], P('shard'), may hold values from -1.5 to 1.5
- value_bias: bfloat16 [768], P('shard'), may hold values from -0.5 to 0.5
- output_bias: bfloat16 [768], P('shard'), may hold values from -1.5 to 1.5
- expand_bias: bfloat16 [3072], P('shard'), may hold values from -1.5 to 1.5
- reduce_bias: bfloat16 [768], P('shard'), may hold values from -1.5 to 1.5
- first_gain: bfloat16 [768], P('shard'), may hold values from 0.099609375 to 1.8984375
- first_shift: bfloat16 [768], P('shard'), may hold values from -1.5 to 1.5
- second_gain: bfloat16 [768], P('shard'), may hold values from 0.099609375 to 1.8984375
- second_shift: bfloat16 [768], P('shard'), may hold values from -1.5 to 1.5
Outputs:
- layer_output: bfloat16 [16, 2048, 768], P('shard', 'rep')
- tokens_gradient: bfloat16 [16, 2048, 768], P('shard', 'rep')
- query_weight_gradient: float32 [768, 768], P('shard')
- key_weight_gradient: float32 [768, 768], P('shard')
- value_weight_gradient: float32 [768, 768], P('shard')
- output_weight_gradient: float32 [768, 768], P('shard')
- expand_weight_gradient: float32 [768, 3072], P('shard')
- reduce_weight_gradient: float32 [3072, 768], P('shard')
- query_bias_gradient: float32 [768], P('shard')
- value_bias_gradient: float32 [768], P('shard')
- output_bias_gradient: float32 [768], P('shard')
- expand_bias_gradient: float32 [3072], P('shard')
- reduce_bias_gradient: float32 [768], P('shard')
- first_gain_gradient: float32 [768], P('shard')
- first_shift_gradient: float32 [768], P('shard')
- second_gain_gradient: float32 [768], P('shard')
- second_shift_gradient: float32 [768], P('shard')
Inputs may be any that keep to these rules, and one draw needn't show every extreme that they name: `segment_ids`: within each sequence the ids never fall; each document holds 1 to 1024 positions and some document of each sequence exactly 1024.
All inputs are finite; a program needn't handle non-finite values.
Results may differ from a plain program's by a relative error of at most 0.017.
The roundings to bfloat16 on the way count: a program that leaves them out, or rounds other values in their place, can miss the bound.
Values may be sent and summed in bfloat16 or wider, within the bound.
A program may use at most 448 MiB of HBM per device.

v0:
```python
from functools import partial

import jax
import jax.numpy as jnp
from jax import lax
from jax.sharding import PartitionSpec as P

HEAD_DIM = 64


masked_value = -1e30
norm_eps = 1e-05


def as_sent(array):
    return jax.tree.map(lambda a: a.astype(jnp.bfloat16) if a.dtype == jnp.float32 else a, array)


def norm_rows(values, gain, shift):
    centre = values - jnp.mean(values, axis=-1, keepdims=True)
    spread = jnp.mean(centre * centre, axis=-1, keepdims=True)
    return centre * lax.rsqrt(spread + norm_eps) * gain + shift


def dense(left, right):
    return jnp.dot(left, right, preferred_element_type=jnp.float32)


def dense_left(left, right):
    return lax.dot_general(
        left, right, (((0,), (0,)), ((), ())), preferred_element_type=jnp.float32
    )


def dense_right(left, right):
    return lax.dot_general(
        left, right, (((1,), (1,)), ((), ())), preferred_element_type=jnp.float32
    )


def column_sum(values):
    return jnp.sum(values.astype(jnp.float32), axis=0)


def unpack(weights):
    matrices = weights[:6]
    vectors = tuple((member.astype(jnp.float32) for member in weights[6:]))
    return (matrices, vectors)


def block_scores(query_block, key_heads, allowed_blocks, block_rows):
    factor = query_block.shape[2] ** (-0.5)
    pieces = []
    for number in range(len(allowed_blocks)):
        allowed = allowed_blocks[number]
        key_block = key_heads[number * block_rows : (number + 1) * block_rows]
        product = partial(
            jnp.einsum, "qhd,khd->hqk", query_block, key_block, preferred_element_type=jnp.float32
        )
        unmasked = product()
        pieces.append(jnp.where(allowed[None, :, :], unmasked * factor, masked_value))
    return jnp.concatenate(pieces, axis=2)


def allowed_for(query_segments, segment_keys, block_rows, key_count):
    return [
        query_segments[:, None]
        == segment_keys[number * block_rows : (number + 1) * block_rows][None, :]
        for number in range(key_count)
    ]


def attend_forward(query_heads, key_heads, value_heads, segment_query, segment_whole):
    local_rows = query_heads.shape[0]
    block_rows = min(512, local_rows)
    key_count = key_heads.shape[0] // block_rows
    allowed_blocks = allowed_for(segment_query, segment_whole, block_rows, key_count)
    scores = block_scores(query_heads, key_heads, allowed_blocks, block_rows)
    largest = jnp.max(scores, axis=2, keepdims=True)
    exponent = jnp.exp(scores - largest)
    row_total = jnp.sum(exponent, axis=2, keepdims=True)
    chances = (exponent / row_total).astype(jnp.bfloat16)
    logsums = [largest[:, :, 0] + jnp.log(row_total[:, :, 0])]
    mixture = jnp.zeros(query_heads.shape, jnp.float32)
    for number in range(key_count):
        chance_slice = chances[:, :, number * block_rows : (number + 1) * block_rows]
        value_block = value_heads[number * block_rows : (number + 1) * block_rows]
        product = partial(
            jnp.einsum,
            "hqk,khd->qhd",
            chance_slice,
            value_block,
            preferred_element_type=jnp.float32,
        )
        mixture = mixture + product()
    mixtures = [mixture]
    return (jnp.concatenate(mixtures, axis=0), jnp.concatenate(logsums, axis=1))


def attend_backward(
    query_heads,
    key_heads,
    value_heads,
    segment_query,
    segment_keys,
    logsums,
    grad_heads,
    block_rows,
):
    query_rows, head_count, head_width = query_heads.shape
    key_count = key_heads.shape[0] // block_rows
    factor = head_width ** (-0.5)
    block_shape = (block_rows, head_count, head_width)
    key_grads = [jnp.zeros(block_shape, jnp.float32) for number in range(key_count)]
    value_grads = [jnp.zeros(block_shape, jnp.float32) for number in range(key_count)]
    allowed_blocks = allowed_for(segment_query, segment_keys, block_rows, key_count)
    scores = block_scores(query_heads, key_heads, allowed_blocks, block_rows)
    chances = jnp.exp(scores - logsums[:, 0:block_rows, None])
    chance_low = chances.astype(jnp.bfloat16)
    pieces = []
    for number in range(key_count):
        value_block = value_heads[number * block_rows : (number + 1) * block_rows]
        product = partial(
            jnp.einsum, "qhd,khd->hqk", grad_heads, value_block, preferred_element_type=jnp.float32
        )
        pieces.append(product())
    grad_chances = jnp.concatenate(pieces, axis=2)
    centre = jnp.sum(chances * grad_chances, axis=2, keepdims=True)
    centres = [centre[:, :, 0]]
    grad_scores = (chances * (grad_chances - centre)).astype(jnp.bfloat16)
    query_grad = jnp.zeros(block_shape, jnp.float32)
    for number in range(key_count):
        key_block = key_heads[number * block_rows : (number + 1) * block_rows]
        score_slice = grad_scores[:, :, number * block_rows : (number + 1) * block_rows]
        chance_slice = chance_low[:, :, number * block_rows : (number + 1) * block_rows]
        query_grad = (
            query_grad
            + partial(
                jnp.einsum,
                "hqk,khd->qhd",
                score_slice,
                key_block,
                preferred_element_type=jnp.float32,
            )()
        )
        key_grads[number] = (
            key_grads[number]
            + partial(
                jnp.einsum,
                "hqk,qhd->khd",
                score_slice,
                query_heads,
                preferred_element_type=jnp.float32,
            )()
        )
        value_grads[number] = (
            value_grads[number]
            + partial(
                jnp.einsum,
                "hqk,qhd->khd",
                chance_slice,
                grad_heads,
                preferred_element_type=jnp.float32,
            )()
        )
    query_grads = [query_grad * factor]
    key_whole = jnp.concatenate(key_grads, axis=0) * factor
    return (
        jnp.concatenate(query_grads, axis=0),
        key_whole,
        jnp.concatenate(value_grads, axis=0),
        jnp.concatenate(centres, axis=1),
    )


def local(
    tokens,
    segment_ids,
    cotangent,
    query_weight,
    key_weight,
    value_weight,
    output_weight,
    expand_weight,
    reduce_weight,
    query_bias,
    value_bias,
    output_bias,
    expand_bias,
    reduce_bias,
    first_gain,
    first_shift,
    second_gain,
    second_shift,
):
    shards = (
        query_weight,
        key_weight,
        value_weight,
        output_weight,
        expand_weight,
        reduce_weight,
        query_bias,
        value_bias,
        output_bias,
        expand_bias,
        reduce_bias,
        first_gain,
        first_shift,
        second_gain,
        second_shift,
    )
    micro_count = tokens.shape[0]
    local_rows = tokens.shape[1]
    model_width = tokens.shape[2]
    head_count = model_width // HEAD_DIM
    block_rows = min(512, local_rows)
    offset = lax.axis_index("rep") * local_rows
    totals = tuple(
        (
            jnp.zeros((lax.axis_size("shard") * member.shape[0],) + member.shape[1:], jnp.float32)
            for member in shards
        )
    )
    outputs = []
    input_grads = []

    def heads_of(array):
        return array.reshape(array.shape[0], head_count, HEAD_DIM)

    for micro_index in range(micro_count):
        weights_now = (
            lax.all_gather(shards[0], "shard", axis=0, tiled=True),
            lax.all_gather(shards[1], "shard", axis=0, tiled=True),
            lax.all_gather(shards[2], "shard", axis=0, tiled=True),
            lax.all_gather(shards[3], "shard", axis=0, tiled=True),
            lax.all_gather(shards[4], "shard", axis=0, tiled=True),
            lax.all_gather(shards[5], "shard", axis=0, tiled=True),
            lax.all_gather(shards[6], "shard", axis=0, tiled=True),
            lax.all_gather(shards[7], "shard", axis=0, tiled=True),
            lax.all_gather(shards[8], "shard", axis=0, tiled=True),
            lax.all_gather(shards[9], "shard", axis=0, tiled=True),
            lax.all_gather(shards[10], "shard", axis=0, tiled=True),
            lax.all_gather(shards[11], "shard", axis=0, tiled=True),
            lax.all_gather(shards[12], "shard", axis=0, tiled=True),
            lax.all_gather(shards[13], "shard", axis=0, tiled=True),
            lax.all_gather(shards[14], "shard", axis=0, tiled=True),
        )
        matrices, vectors = unpack(weights_now)
        query_matrix, key_matrix, value_matrix, output_matrix, expand_matrix, reduce_matrix = (
            matrices
        )
        (
            query_vector,
            value_vector,
            output_vector,
            expand_vector,
            reduce_vector,
            first_gain_vec,
            first_shift_vec,
            second_gain_vec,
            second_shift_vec,
        ) = vectors
        inputs_now = tokens[micro_index]
        segment_whole = segment_ids[micro_index]
        segment_query = lax.dynamic_slice_in_dim(segment_whole, offset, local_rows)
        queries = (dense(inputs_now, query_matrix) + query_vector).astype(jnp.bfloat16)
        keys_local = dense(inputs_now, key_matrix).astype(jnp.bfloat16)
        values_local = (dense(inputs_now, value_matrix) + value_vector).astype(jnp.bfloat16)
        keys_whole, values_whole = (
            lax.all_gather(keys_local, "rep", axis=0, tiled=True),
            lax.all_gather(values_local, "rep", axis=0, tiled=True),
        )
        mixture, logsums = attend_forward(
            heads_of(queries),
            heads_of(keys_whole),
            heads_of(values_whole),
            segment_query,
            segment_whole,
        )
        attended = mixture.reshape(local_rows, model_width).astype(jnp.bfloat16)
        branch = dense(attended, output_matrix) + output_vector
        first, first_back = jax.vjp(
            norm_rows, inputs_now.astype(jnp.float32) + branch, first_gain_vec, first_shift_vec
        )
        first_low = first.astype(jnp.bfloat16)
        expanded = dense(first_low, expand_matrix) + expand_vector
        activated, gelu_back = jax.vjp(jax.nn.gelu, expanded)
        activated_low = activated.astype(jnp.bfloat16)
        reduced = dense(activated_low, reduce_matrix) + reduce_vector
        result, second_back = jax.vjp(norm_rows, first + reduced, second_gain_vec, second_shift_vec)
        outputs.append(result.astype(jnp.bfloat16))
        weights_now = (
            lax.all_gather(shards[0], "shard", axis=0, tiled=True),
            lax.all_gather(shards[1], "shard", axis=0, tiled=True),
            lax.all_gather(shards[2], "shard", axis=0, tiled=True),
            lax.all_gather(shards[3], "shard", axis=0, tiled=True),
            lax.all_gather(shards[4], "shard", axis=0, tiled=True),
            lax.all_gather(shards[5], "shard", axis=0, tiled=True),
            lax.all_gather(shards[6], "shard", axis=0, tiled=True),
            lax.all_gather(shards[7], "shard", axis=0, tiled=True),
            lax.all_gather(shards[8], "shard", axis=0, tiled=True),
            lax.all_gather(shards[9], "shard", axis=0, tiled=True),
            lax.all_gather(shards[10], "shard", axis=0, tiled=True),
            lax.all_gather(shards[11], "shard", axis=0, tiled=True),
            lax.all_gather(shards[12], "shard", axis=0, tiled=True),
            lax.all_gather(shards[13], "shard", axis=0, tiled=True),
            lax.all_gather(shards[14], "shard", axis=0, tiled=True),
        )
        matrices, vectors = unpack(weights_now)
        query_matrix, key_matrix, value_matrix, output_matrix, expand_matrix, reduce_matrix = (
            matrices
        )
        grad_second, grad_second_gain, grad_second_shift = second_back(
            cotangent[micro_index].astype(jnp.float32)
        )
        grad_reduced = grad_second.astype(jnp.bfloat16)
        reduce_matrix_grad = dense_left(activated_low, grad_reduced)
        (grad_expanded_full,) = gelu_back(dense_right(grad_reduced, reduce_matrix))
        grad_expanded = grad_expanded_full.astype(jnp.bfloat16)
        expand_matrix_grad = dense_left(first_low, grad_expanded)
        grad_first = grad_second + dense_right(grad_expanded, expand_matrix)
        grad_residual, grad_first_gain, grad_first_shift = first_back(grad_first)
        grad_branch = grad_residual.astype(jnp.bfloat16)
        output_matrix_grad = dense_left(attended, grad_branch)
        grad_attended = dense_right(grad_branch, output_matrix).astype(jnp.bfloat16)
        query_side = attend_backward(
            heads_of(queries),
            heads_of(keys_whole),
            heads_of(values_whole),
            segment_query,
            segment_whole,
            logsums,
            heads_of(grad_attended),
            block_rows,
        )
        grad_query_heads = query_side[0]
        key_terms = query_side[1]
        value_terms = query_side[2]
        sequence_rows = key_terms.shape[0]
        grad_keys_full, grad_values_full = (
            lax.psum_scatter(
                key_terms.reshape(sequence_rows, model_width),
                "rep",
                scatter_dimension=0,
                tiled=True,
            ),
            lax.psum_scatter(
                value_terms.reshape(sequence_rows, model_width),
                "rep",
                scatter_dimension=0,
                tiled=True,
            ),
        )
        grad_queries = grad_query_heads.reshape(local_rows, model_width).astype(jnp.bfloat16)
        grad_keys = grad_keys_full.astype(jnp.bfloat16)
        grad_values = grad_values_full.astype(jnp.bfloat16)
        grad_inputs = (
            grad_residual
            + dense_right(grad_queries, query_matrix)
            + dense_right(grad_keys, key_matrix)
            + dense_right(grad_values, value_matrix)
        )
        input_grads.append(grad_inputs.astype(jnp.bfloat16))
        changes = (
            dense_left(inputs_now, grad_queries),
            dense_left(inputs_now, grad_keys),
            dense_left(inputs_now, grad_values),
            output_matrix_grad,
            expand_matrix_grad,
            reduce_matrix_grad,
            column_sum(grad_queries),
            column_sum(grad_values),
            column_sum(grad_branch),
            column_sum(grad_expanded),
            column_sum(grad_reduced),
            grad_first_gain,
            grad_first_shift,
            grad_second_gain,
            grad_second_shift,
        )
        totals = tuple((total + change for total, change in zip(totals, changes)))
    summed = lax.psum_scatter(totals, "shard", scatter_dimension=0, tiled=True)
    final = jax.tree.map(lambda part: part.astype(jnp.float32), lax.psum(as_sent(summed), "rep"))
    return (jnp.stack(outputs), jnp.stack(input_grads)) + tuple(final)


def solution(mesh):
    in_specs = (
        P("shard", "rep", None),
        P("shard", None),
        P("shard", "rep", None),
        P("shard", None),
        P("shard", None),
        P("shard", None),
        P("shard", None),
        P("shard", None),
        P("shard", None),
        P("shard"),
        P("shard"),
        P("shard"),
        P("shard"),
        P("shard"),
        P("shard"),
        P("shard"),
        P("shard"),
        P("shard"),
    )
    out_specs = (
        P("shard", "rep", None),
        P("shard", "rep", None),
        P("shard", None),
        P("shard", None),
        P("shard", None),
        P("shard", None),
        P("shard", None),
        P("shard", None),
        P("shard"),
        P("shard"),
        P("shard"),
        P("shard"),
        P("shard"),
        P("shard"),
        P("shard"),
        P("shard"),
        P("shard"),
    )
    return jax.shard_map(local, mesh=mesh, in_specs=in_specs, out_specs=out_specs, check_vma=False)
```

profile of v0, /device:TPU:0, one launch (start us, length us, event | category | flops | bytes accessed | tf_op | source)
XLA Modules:
  0.0 1376.7 jit_solution(11595395446563708483)
XLA Ops:
  18.2 30.6 %all-reduce.18 = (bf16[768]{0:T(1024)(128)(2,1)S(1)}, bf16[768]{0:T(1024)(128)(2,1)S(1)}, bf16[768]{0:T(1024)(128)(2,1)S(1)}, bf16[768]{0:T(1024)(128)(2,1)S(1)}...) all-reduce(bf16[768]{0:T(1024)(128)(2,1)S(1)} %dynamic-update-slice, ...), channel_id=1, replica_groups=mesh['rep'=4,'shard'=8] {'shard'}, use_global_device_ids=true, to_apply=%add | all-reduce | flops 6144 | bytes 24576
  70.3 12.7 all-gather
  93.8 35.4 %all-gather.28.cloned.1.call-done = bf16[2048,768]{1,0:T(8,128)(2,1)} async-done(((bf16[512,768]{1,0:T(8,128)(2,1)}), bf16[2048,768]{1,0:T(8,128)(2,1)}) %all-gather.28.cloned.1.call-update) | async-done | bytes 3145744 | tf_op jit(solution)/shard_map/all_gather | solution.py:272
  135.1 40.4 %all-gather.14.cloned.1.call-done = bf16[2048,768]{1,0:T(8,128)(2,1)} async-done(((bf16[512,768]{1,0:T(8,128)(2,1)}), bf16[2048,768]{1,0:T(8,128)(2,1)}) %all-gather.14.cloned.1.call-update) | async-done | bytes 3145744 | tf_op jit(solution)/shard_map/all_gather | solution.py:272
  195.3 25.8 %all-gather.30.cloned.1.call-done = bf16[2048,768]{1,0:T(8,128)(2,1)} async-done(((bf16[512,768]{1,0:T(8,128)(2,1)}), bf16[2048,768]{1,0:T(8,128)(2,1)}) %all-gather.30.cloned.1.call-update) | async-done | bytes 3145744 | tf_op jit(solution)/shard_map/all_gather | solution.py:271
  234.0 33.0 %all-gather.20.cloned.1.call-done = bf16[2048,768]{1,0:T(8,128)(2,1)} async-done(((bf16[512,768]{1,0:T(8,128)(2,1)}), bf16[2048,768]{1,0:T(8,128)(2,1)}) %all-gather.20.cloned.1.call-update) | async-done | bytes 3145744 | tf_op jit(solution)/shard_map/all_gather | solution.py:271
  279.8 7.9 fusion.215
  287.7 6.7 fusion.212
  294.4 7.5 fusion.213
  308.6 17.5 %fusion.5 = f32[12,512]{1,0:T(8,128)S(1)} fusion(f32[12,512]{1,0:T(8,128)S(1)} %maximum_maximum_fusion, f32[12,512,512]{1,2,0:T(8,128)} %get-tuple-element.199, f32[12,512,512]{1,2,0:T(8,128)} %get-tuple-element.201, f32[12,512,512]{1,2,0:T(8,128)} %get-tuple-element.205, f32[12,512,512]{1,2,0:T(8,128)} %get-tuple-element.203), kind=kLoop, calls=%fused_computation.19 | loop fusion | flops 62908416 | bytes 50380800 | tf_op jit(solution)/shard_map/reduce_sum | solution.py:81
  326.2 7.6 fusion.209
  340.4 6.6 fusion.207
  347.1 7.1 fusion.208
  354.2 17.3 %fusion.4 = f32[12,512]{1,0:T(8,128)S(1)} fusion(f32[12,512]{1,0:T(8,128)S(1)} %maximum_maximum_fusion.1, f32[12,512,512]{1,2,0:T(8,128)} %get-tuple-element.187, f32[12,512,512]{1,2,0:T(8,128)} %get-tuple-element.189, f32[12,512,512]{1,2,0:T(8,128)} %get-tuple-element.193, f32[12,512,512]{1,2,0:T(8,128)} %get-tuple-element.191), kind=kLoop, calls=%fused_computation.18 | loop fusion | flops 62908416 | bytes 50380800 | tf_op jit(solution)/shard_map/reduce_sum | solution.py:81
  371.5 39.4 %fusion.6 = (bf16[12,512,2048]{1,2,0:T(8,128)(2,1)}, bf16[12,512,2048]{1,2,0:T(8,128)(2,1)}) fusion(f32[12,512]{1,0:T(8,128)S(1)} %log_add_fusion.1, f32[12,512,512]{1,2,0:T(8,128)} %get-tuple-element.187, f32[12,512,512]{1,2,0:T(8,128)} %get-tuple-element.189, f32[12,512,512]{1,2,0:T(8,128)} %get-tuple-element.193, f32[12,512,512]{1,2,0:T(8,128)} %get-tuple-element.191, ...), kind=kLoop, calls=%fused_computation.20 | loop fusion | flops 100663296 | bytes 100737024 | tf_op jit(solution)/shard_map/convert_element_type | solution.py:119
  431.1 39.2 %fusion.9 = (bf16[12,512,2048]{1,2,0:T(8,128)(2,1)}, bf16[12,512,2048]{1,2,0:T(8,128)(2,1)}) fusion(f32[12,512]{1,0:T(8,128)S(1)} %log_add_fusion, f32[12,512,512]{1,2,0:T(8,128)} %get-tuple-element.199, f32[12,512,512]{1,2,0:T(8,128)} %get-tuple-element.201, f32[12,512,512]{1,2,0:T(8,128)} %get-tuple-element.205, f32[12,512,512]{1,2,0:T(8,128)} %get-tuple-element.203, ...), kind=kLoop, calls=%fused_computation.21 | loop fusion | flops 100663296 | bytes 100737024 | tf_op jit(solution)/shard_map/convert_element_type | solution.py:119
  488.1 8.4 fusion.190
  496.5 7.9 fusion.211
  522.8 18.1 %convert_reduce_fusion.1 = (f32[3072]{0:T(1024)}, bf16[512,3072]{1,0:T(8,128)(2,1)}, f32[3072]{0:T(1024)}, bf16[512,3072]{1,0:T(8,128)(2,1)S(1)}) fusion(f32[512,3072]{1,0:T(8,128)} %fusion.190, f32[3072]{0:T(1024)S(1)} %bitcast.362, f32[512,3072]{1,0:T(8,128)} %fusion.223, f32[512,3072]{1,0:T(8,128)} %copy-done.124, ...), kind=kOutput, calls=%fused_computation.87 | convolution fusion | flops 2488264704 | bytes 30707712 | tf_op jit(solution)/shard_map/dot_general | solution.py:36
  621.4 7.0 fusion.218
  629.2 76.6 %multiply_convert_fusion.1 = bf16[12,512,2048]{1,2,0:T(8,128)(2,1)} fusion(f32[12,512,512]{1,2,0:T(8,128)} %fusion.221, f32[12,512,512]{1,2,0:T(8,128)} %fusion.220, f32[12,512,512]{1,2,0:T(8,128)} %fusion.219, f32[12,512,512]{1,2,0:T(8,128)} %fusion.218, f32[12,512]{1,0:T(8,128)S(1)} %copy-done.86, f32[12,512,512]{1,2,0:T(8,128)} %get-tuple-element.187, ...), kind=kOutput, calls=%fused_computation.10 | output fusion | flops 226500608 | bytes 125853696 | tf_op jit(solution)/shard_map/sub | solution.py:130
  754.2 87.6 %multiply_convert_fusion = bf16[12,512,2048]{1,2,0:T(8,128)(2,1)} fusion(f32[12,512,512]{1,2,0:T(8,128)} %fusion.227, f32[12,512,512]{1,2,0:T(8,128)} %fusion.226, f32[12,512,512]{1,2,0:T(8,128)} %fusion.225, f32[12,512,512]{1,2,0:T(8,128)} %fusion.224, f32[12,512]{1,0:T(8,128)S(1)} %copy-done.84, f32[12,512,512]{1,2,0:T(8,128)} %get-tuple-element.199, ...), kind=kOutput, calls=%fused_computation.6 | output fusion | flops 226500608 | bytes 125853696 | tf_op jit(solution)/shard_map/sub | solution.py:130
  921.2 13.1 reduce-scatter.21.cloned.1.call-done
  948.2 10.2 convolution_add_fusion
  983.1 27.4 %reduce-scatter.31.cloned.1.call-done = f32[96,768]{1,0:T(8,128)} async-done(((f32[768,768]{1,0:T(8,128)}), f32[96,768]{1,0:T(8,128)}) %reduce-scatter.31.cloned.1.call-update) | async-done | bytes 294928
  1012.4 35.7 %reduce-scatter.35.cloned.1.call-done = f32[96,768]{1,0:T(8,128)} async-done(((f32[768,768]{1,0:T(8,128)}), f32[96,768]{1,0:T(8,128)}) %reduce-scatter.35.cloned.1.call-update) | async-done | bytes 294928
  1049.9 35.8 %reduce-scatter.33.cloned.1.call-done = f32[96,768]{1,0:T(8,128)} async-done(((f32[768,768]{1,0:T(8,128)}), f32[96,768]{1,0:T(8,128)}) %reduce-scatter.33.cloned.1.call-update) | async-done | bytes 294928
  1087.5 99.2 %reduce-scatter.29.cloned.1.call-done = f32[384,768]{1,0:T(8,128)} async-done(((f32[3072,768]{1,0:T(8,128)}), f32[384,768]{1,0:T(8,128)}) %reduce-scatter.29.cloned.1.call-update) | async-done | bytes 1179664 | tf_op jit(solution)/shard_map/reduce_scatter | solution.py:383
  1188.9 97.9 %reduce-scatter.27.cloned.1.call-done = f32[96,3072]{1,0:T(8,128)} async-done(((f32[768,3072]{1,0:T(8,128)}), f32[96,3072]{1,0:T(8,128)}) %reduce-scatter.27.cloned.1.call-update) | async-done | bytes 1179664 | tf_op jit(solution)/shard_map/reduce_scatter | solution.py:383
  1289.2 26.4 %all-reduce.17 = (bf16[768]{0:T(1024)(128)(2,1)S(1)}, bf16[768]{0:T(1024)(128)(2,1)S(1)}, bf16[768]{0:T(1024)(128)(2,1)S(1)}, bf16[3072]{0:T(1024)(128)(2,1)S(1)...) all-reduce(f32[768]{0:T(1024)S(1)} %add.445, ...), channel_id=12, replica_groups=mesh['rep'=4,'shard'=8] {'shard'}, use_global_device_ids=true, to_apply=%region_46.47.clone | all-reduce | flops 9216 | bytes 55296
  1316.3 10.0 all-reduce.19
  1340.1 18.0 %all-reduce.23.cloned.1.call-done = (bf16[96,768]{0,1:T(8,128)(2,1)}, bf16[96,768]{0,1:T(8,128)(2,1)}, bf16[96,768]{0,1:T(8,128)(2,1)}, bf16[96,768]{1,0:T(8,128...) async-done(((bf16[96,768]{0,1:T(8,128)(2,1)}, bf16[96,768]{0,1:T(8,128)(2,1)}, bf16[96,768]{0,1:T(8,128)(2,1)}, bf16[96,768]{1,0:T(8,128)(2,1)}, ...) | async-done | bytes 1769488 | tf_op jit(solution)/shard_map/psum | solution.py:384
  (534 shorter events, 443.5 us)
Async XLA Ops:
  7.2 41.5 %all-gather.12.cloned.1.call-start = ((), (), s32[]{:S(2)}) async-start(), calls=%async_computation.10 | async-start | bytes 1327104 | tf_op jit(solution)/shard_map/all_gather | solution.py:235
  7.9 51.3 %all-gather.18.cloned.1.call-start = ((), (), s32[]{:S(2)}) async-start(), calls=%async_computation.13 | async-start | bytes 1327104 | tf_op jit(solution)/shard_map/all_gather | solution.py:234
  8.7 78.0 %all-gather.16.cloned.1.call-start = ((), (), s32[]{:S(2)}) async-start(), calls=%async_computation.12 | async-start | bytes 1327104 | tf_op jit(solution)/shard_map/all_gather | solution.py:233
  9.4 119.8 %all-gather.28.cloned.1.call-start = ((), (), s32[]{:S(2)}) async-start(), calls=%async_computation.18 | async-start | bytes 3932160 | tf_op jit(solution)/shard_map/all_gather | solution.py:272
  52.1 123.4 %all-gather.14.cloned.1.call-start = ((), (), s32[]{:S(2)}) async-start(), calls=%async_computation.11 | async-start | bytes 3932160 | tf_op jit(solution)/shard_map/all_gather | solution.py:272
  53.8 167.3 %all-gather.30.cloned.1.call-start = ((), (), s32[]{:S(2)}) async-start(), calls=%async_computation.19 | async-start | bytes 3932160 | tf_op jit(solution)/shard_map/all_gather | solution.py:271
  62.2 204.8 %all-gather.20.cloned.1.call-start = ((), (), s32[]{:S(2)}) async-start(), calls=%async_computation.14 | async-start | bytes 3932160 | tf_op jit(solution)/shard_map/all_gather | solution.py:271
  65.2 362.0 %all-gather.22.cloned.1.call-start = ((), (), s32[]{:S(2)}) async-start(), calls=%async_computation.15 | async-start | bytes 1327104 | tf_op jit(solution)/shard_map/all_gather | solution.py:236
  65.9 422.2 %all-gather.24.cloned.1.call-start = ((), (), s32[]{:S(2)}) async-start(), calls=%async_computation.16 | async-start | bytes 5308416 | tf_op jit(solution)/shard_map/all_gather | solution.py:237
  66.7 429.8 %all-gather.26.cloned.1.call-start = ((), (), s32[]{:S(2)}) async-start(), calls=%async_computation.17 | async-start | bytes 5308416 | tf_op jit(solution)/shard_map/all_gather | solution.py:238
  67.3 838.9 %reduce-scatter.19.cloned.1.call-start = ((), (), s32[]{:S(2)}) async-start(), calls=%async_computation.21 | async-start | bytes 7864320 | tf_op jit(solution)/shard_map/reduce_scatter | solution.py:348
  89.1 212.9 %copy-start = (bf16[512,768]{0,1:T(8,128)(2,1)}, bf16[512,768]{0,1:T(8,128)(2,1)S(1)}, u32[]{:S(2)}) copy-start(bf16[512,768]{0,1:T(8,128)(2,1)S(1)} %copy.203) | copy-start | bytes 2359300
  93.8 253.3 %copy-start.2 = (bf16[512,768]{0,1:T(8,128)(2,1)}, bf16[512,768]{0,1:T(8,128)(2,1)S(1)}, u32[]{:S(2)}) copy-start(bf16[512,768]{0,1:T(8,128)(2,1)S(1)} %copy.190) | copy-start | bytes 2359300
  326.1 105.0 %copy-start.83 = (f32[12,512]{1,0:T(8,128)}, f32[12,512]{1,0:T(8,128)S(1)}, u32[]{:S(2)}) copy-start(f32[12,512]{1,0:T(8,128)S(1)} %log_add_fusion) | copy-start | bytes 73732
  429.7 118.3 %copy-start.95 = (f32[512]{0:T(512)}, f32[512]{0:T(512)S(1)}, u32[]{:S(2)}) copy-start(f32[512]{0:T(512)S(1)} %broadcast_multiply_fusion.3) | copy-start | bytes 6148
  487.7 60.4 %copy-start.6 = (f32[512,768]{1,0:T(8,128)}, f32[512,768]{1,0:T(8,128)S(1)}, u32[]{:S(2)}) copy-start(f32[512,768]{1,0:T(8,128)S(1)} %get-tuple-element.207) | copy-start | bytes 4718596
  487.7 60.4 %copy-start.90 = (f32[512]{0:T(512)}, f32[512]{0:T(512)S(1)}, u32[]{:S(2)}) copy-start(f32[512]{0:T(512)S(1)} %broadcast_multiply_fusion.1) | copy-start | bytes 6148
  488.0 60.0 %copy-start.112 = (f32[512]{0:T(512)}, f32[512]{0:T(512)S(1)}, u32[]{:S(2)}) copy-start(f32[512]{0:T(512)S(1)} %fusion.175) | copy-start | bytes 6148
  488.0 60.0 %copy-start.93 = (f32[512]{0:T(512)}, f32[512]{0:T(512)S(1)}, u32[]{:S(2)}) copy-start(f32[512]{0:T(512)S(1)} %fusion.177) | copy-start | bytes 6148
  574.7 335.0 %reduce-scatter.23.cloned.1.call-start = ((), (), s32[]{:S(2)}) async-start(), calls=%async_computation.23 | async-start | bytes 7864320 | tf_op jit(solution)/shard_map/reduce_scatter | solution.py:348
  628.5 77.3 %copy-start.3 = (bf16[512,768]{0,1:T(8,128)(2,1)S(1)}, bf16[512,768]{0,1:T(8,128)(2,1)}, u32[]{:S(2)}) copy-start(bf16[512,768]{0,1:T(8,128)(2,1)} %copy-done.2) | copy-start | bytes 2359300
  628.5 289.1 %reduce-scatter.17.cloned.1.call-start = ((), (), s32[]{:S(2)}) async-start(), calls=%async_computation.20 | async-start | bytes 7864320 | tf_op jit(solution)/shard_map/reduce_scatter | solution.py:342
  753.5 88.3 %copy-start.1 = (bf16[512,768]{0,1:T(8,128)(2,1)S(1)}, bf16[512,768]{0,1:T(8,128)(2,1)}, u32[]{:S(2)}) copy-start(bf16[512,768]{0,1:T(8,128)(2,1)} %copy-done) | copy-start | bytes 2359300
  753.5 180.9 %reduce-scatter.21.cloned.1.call-start = ((), (), s32[]{:S(2)}) async-start(), calls=%async_computation.22 | async-start | bytes 7864320 | tf_op jit(solution)/shard_map/reduce_scatter | solution.py:342
  864.0 117.3 %reduce-scatter.25.cloned.1.call-start = ((), (), s32[]{:S(2)}) async-start(), calls=%async_computation.24 | async-start | bytes 2654208 | tf_op jit(solution)/shard_map/reduce_scatter | solution.py:383
  868.4 142.1 %reduce-scatter.31.cloned.1.call-start = ((), (), s32[]{:S(2)}) async-start(), calls=%async_computation.27 | async-start | bytes 2654208
  906.1 142.1 %reduce-scatter.35.cloned.1.call-start = ((), (), s32[]{:S(2)}) async-start(), calls=%async_computation.29 | async-start | bytes 2654208
  917.5 168.2 %reduce-scatter.33.cloned.1.call-start = ((), (), s32[]{:S(2)}) async-start(), calls=%async_computation.28 | async-start | bytes 2654208
  941.9 244.9 %reduce-scatter.29.cloned.1.call-start = ((), (), s32[]{:S(2)}) async-start(), calls=%async_computation.26 | async-start | bytes 10616832 | tf_op jit(solution)/shard_map/reduce_scatter | solution.py:383
  958.4 328.4 %reduce-scatter.27.cloned.1.call-start = ((), (), s32[]{:S(2)}) async-start(), calls=%async_computation.25 | async-start | bytes 10616832 | tf_op jit(solution)/shard_map/reduce_scatter | solution.py:383
  970.9 387.3 %all-reduce.23.cloned.1.call-start = ((), (), s32[]{:S(2)}) async-start(), calls=%async_computation.30 | async-start | bytes 3833856 | tf_op jit(solution)/shard_map/psum | solution.py:384
  981.3 307.7 %copy-start.8 = (f32[512,768]{0,1:T(8,128)S(1)}, f32[512,768]{0,1:T(8,128)}, u32[]{:S(2)}) copy-start(f32[512,768]{0,1:T(8,128)} %reduce-scatter.23.cloned.1.call-done) | copy-start | bytes 4718596
  (123 other events, 895.7 us)
Sparse Core Ops, SparseCore 0:
  9.7 25.5 all-gather.11
  36.9 22.3 all-gather.17
  60.9 22.3 all-gather.15
  85.5 43.6 all-gather.27
  131.4 43.9 all-gather.13
  177.2 43.9 all-gather.29
  223.0 43.9 all-gather.19
  268.7 22.6 all-gather.21
  293.0 51.4 all-gather.23
  346.0 50.5 all-gather.25
  574.8 70.3 reduce-scatter.18
  648.1 70.1 reduce-scatter.22
  753.6 70.1 reduce-scatter.16
  864.1 70.2 reduce-scatter.20
  936.5 36.3 reduce-scatter.24
  975.1 35.3 reduce-scatter.30
  1012.6 35.4 reduce-scatter.34
  1050.3 35.3 reduce-scatter.32
  1088.1 98.6 reduce-scatter.28
  1188.9 97.8 reduce-scatter.26
  1291.3 66.8 all-reduce.22
where the time goes:
time: 1380 us
  waiting for transfers between devices  472 us (34%)
  matrix products  385 us (28%)
  other arithmetic  327 us (24%)
  local copies, waits for them, and re-layouts  93.1 us (7%)
  blocking collectives  79.7 us (6%)
  between operations  19 us (1%)
    reduce_scatter x3, waiting for transfers between devices, local(): summed = lax.psum_scatter(totals, 'shard', scatter_dimension=0, tiled=True)  197 us
    sub x2, other arithmetic, attend_backward(): grad_scores = (chances * (grad_chances - centre)).astype(jnp.bfloat16)  164 us
    unnamed x24, waiting for transfers between devices  103 us
    convert_element_type x2, other arithmetic, attend_backward(): chance_low = chances.astype(jnp.bfloat16)  78.5 us
    all_gather x2, waiting for transfers between devices, local(): lax.all_gather(values_local, 'rep', axis=0, tiled=True)  75.8 us
    all_gather x2, waiting for transfers between devices, local(): lax.all_gather(keys_local, 'rep', axis=0, tiled=True)  58.8 us
    unnamed x2, blocking collectives  57 us
    dot_general x8, matrix products, block_scores(): unmasked = product()  56.7 us
  transfers between devices with their start and end apart: 21, of which 12 were waited for; matrix products, arithmetic and copies ran while one was open for 51% of the time, Pallas kernels for 0%

commit v1 on v0

v1 whole, which is shorter than its diff:
```python
import functools
import math

import jax
import jax.numpy as jnp
from jax import lax
from jax.experimental import pallas as pl
from jax.experimental.pallas import tpu as pltpu
from jax.sharding import PartitionSpec as P

HEAD_DIM = 64
BLOCK = 256
ROWS = 256
MASKED = -1e30
EPS = 1e-05
SCALE = HEAD_DIM**-0.5
SCALE2 = SCALE * math.log2(math.e)
GELU_A = math.sqrt(2.0 / math.pi)
GELU_B = 0.044715
F32 = jnp.float32
BF16 = jnp.bfloat16
VMEM_LIMIT = 60 * 1024 * 1024


def dot(left, right):
    return jnp.dot(left, right, preferred_element_type=F32)


def dot_right(left, right):
    return lax.dot_general(left, right, (((1,), (1,)), ((), ())), preferred_element_type=F32)


def dot_left(left, right):
    return lax.dot_general(left, right, (((0,), (0,)), ((), ())), preferred_element_type=F32)


def params(**more):
    return pltpu.CompilerParams(vmem_limit_bytes=VMEM_LIMIT, **more)


def qkv_kernel(core, own, other, wq, wk, wv, bq, bv, q_out, k_out, v_out):
    per_core = pl.num_programs(0) // 2
    mine = pl.program_id(0) // per_core == core[0]
    rows = jnp.where(mine, own[...], other[...])
    q_out[...] = (dot(rows, wq[...]) + bq[...]).astype(BF16)
    k_out[...] = dot(rows, wk[...]).astype(BF16)
    v_out[...] = (dot(rows, wv[...]) + bv[...]).astype(BF16)


def project(core, own, other, wq, wk, wv, bq, bv):
    rows, width = own.shape
    half = width // 2
    steps = rows // ROWS

    def side(flip):
        def index(i, core):
            first = jnp.where(core[0] == flip, 0, steps)
            return (jnp.clip(i - first, 0, steps - 1), 0)

        return index

    weight = pl.BlockSpec((width, half), lambda i, core: (0, core[0]))
    bias = pl.BlockSpec((1, half), lambda i, core: (0, core[0]))
    result = pl.BlockSpec((ROWS, half), lambda i, core: (i, 0))
    return pl.pallas_call(
        qkv_kernel,
        out_shape=[jax.ShapeDtypeStruct((2 * rows, half), BF16)] * 3,
        grid_spec=pltpu.PrefetchScalarGridSpec(
            num_scalar_prefetch=1,
            grid=(2 * steps,),
            in_specs=[
                pl.BlockSpec((ROWS, width), side(0)),
                pl.BlockSpec((ROWS, width), side(1)),
                weight,
                weight,
                weight,
                bias,
                bias,
            ],
            out_specs=[result] * 3,
        ),
        compiler_params=params(),
        cost_estimate=pl.CostEstimate(
            flops=2 * 2 * rows * width * 3 * half, bytes_accessed=10 << 20, transcendentals=0
        ),
        name="project",
    )(core, own, other, wq, wk, wv, bq, bv)


def halves(pair):
    lane = lax.broadcasted_iota(jnp.int32, pair.shape, 1)
    zero = jnp.zeros_like(pair)
    return jnp.where(lane < HEAD_DIM, pair, zero), jnp.where(lane < HEAD_DIM, zero, pair)


def attend_kernel(low, high, q_ref, k_ref, v_ref, seg_row, seg_col, out, lse, v_turned, top, total, mix):
    rows, width = q_ref.shape
    heads = width // HEAD_DIM
    pairs = heads // 2
    v_turned[...] = v_ref[...].T

    @pl.loop(0, rows // BLOCK)
    def _(qb):
        q_rows = pl.ds(pl.multiple_of(qb * BLOCK, BLOCK), BLOCK)
        seg_q = seg_row[:, q_rows]
        top[...] = jnp.full_like(top, MASKED)
        total[...] = jnp.zeros_like(total)
        mix[...] = jnp.zeros_like(mix)

        def step(kb, carry):
            k_rows = pl.ds(pl.multiple_of(kb * BLOCK, BLOCK), BLOCK)
            same = seg_col[k_rows, :] == seg_q
            for pair in range(pairs):
                cols = pl.ds(pair * 2 * HEAD_DIM, 2 * HEAD_DIM)
                keys = k_ref[k_rows, cols]
                for side, queries in enumerate(halves(q_ref[q_rows, cols])):
                    h = 2 * pair + side
                    head = pl.ds(h * HEAD_DIM, HEAD_DIM)
                    scores = jnp.where(same, dot_right(keys, queries) * SCALE2, MASKED)
                    before = top[pl.ds(h, 1), :]
                    now = jnp.maximum(before, jnp.max(scores, axis=0, keepdims=True))
                    weight = jnp.exp2(scores - now)
                    fade = jnp.exp2(before - now)
                    top[pl.ds(h, 1), :] = now
                    total[pl.ds(h, 1), :] = total[pl.ds(h, 1), :] * fade + jnp.sum(
                        weight, axis=0, keepdims=True
                    )
                    mix[head, :] = mix[head, :] * fade + dot(
                        v_turned[head, k_rows], weight.astype(BF16)
                    )
            return carry

        lax.fori_loop(low[qb], high[qb], step, 0)
        lse[:, q_rows] = top[...] + jnp.log2(total[...])
        for h in range(heads):
            head = pl.ds(h * HEAD_DIM, HEAD_DIM)
            mix[head, :] = mix[head, :] / total[pl.ds(h, 1), :]
        out[q_rows, :] = mix[...].T.astype(BF16)


def attend(low, high, q, k, v, seg_row, seg_col):
    rows, width = q.shape
    heads = width // HEAD_DIM
    whole = lambda shape: pl.BlockSpec(shape, lambda i, *_: (0,) * len(shape))
    return pl.pallas_call(
        attend_kernel,
        out_shape=[
            jax.ShapeDtypeStruct((rows, width), BF16),
            jax.ShapeDtypeStruct((heads, rows), F32),
        ],
        grid_spec=pltpu.PrefetchScalarGridSpec(
            num_scalar_prefetch=2,
            grid=(1,),
            in_specs=[whole((rows, width))] * 3 + [whole((1, rows)), whole((rows, 1))],
            out_specs=[whole((rows, width)), whole((heads, rows))],
            scratch_shapes=[
                pltpu.VMEM((width, rows), BF16),
                pltpu.VMEM((heads, BLOCK), F32),
                pltpu.VMEM((heads, BLOCK), F32),
                pltpu.VMEM((width, BLOCK), F32),
            ],
        ),
        compiler_params=params(),
        cost_estimate=pl.CostEstimate(
            flops=4 * rows * rows * width * 2,
            bytes_accessed=8 << 20,
            transcendentals=rows * rows * heads // 2,
        ),
        name="attend",
    )(low, high, q, k, v, seg_row, seg_col)


def attend_back_kernel(
    core, low, high, q_ref, k_ref, v_ref, out_ref, own, other, lse, seg_row, seg_col,
    dq_out, dk_out, dv_out, grad, k_turned, delta, dq, dk, dv,
):
    rows, width = q_ref.shape
    heads = width // HEAD_DIM
    pairs = heads // 2
    per_core = own.shape[0]
    mine = pl.multiple_of(core[0] * per_core, per_core)
    theirs = pl.multiple_of((1 - core[0]) * per_core, per_core)
    grad[pl.ds(mine, per_core), :] = own[...]
    grad[pl.ds(theirs, per_core), :] = other[...]
    k_turned[...] = k_ref[...].T
    picks = (
        lax.broadcasted_iota(jnp.int32, (8, width), 1) // HEAD_DIM
        == lax.broadcasted_iota(jnp.int32, (8, width), 0)
    ).astype(BF16)

    @pl.loop(0, rows // BLOCK)
    def _(qb):
        q_rows = pl.ds(pl.multiple_of(qb * BLOCK, BLOCK), BLOCK)
        both = grad[q_rows, :].astype(F32) * out_ref[q_rows, :].astype(F32)
        coarse = both.astype(BF16)
        fine = (both - coarse.astype(F32)).astype(BF16)
        delta[:, q_rows] = dot_right(picks, coarse) + dot_right(picks, fine)

    dq[...] = jnp.zeros_like(dq)

    @pl.loop(0, rows // BLOCK)
    def _(kb):
        k_rows = pl.ds(pl.multiple_of(kb * BLOCK, BLOCK), BLOCK)
        seg_k = seg_col[k_rows, :]
        dk[...] = jnp.zeros_like(dk)
        dv[...] = jnp.zeros_like(dv)

        def step(qb, carry):
            q_rows = pl.ds(pl.multiple_of(qb * BLOCK, BLOCK), BLOCK)
            same = seg_k == seg_row[:, q_rows]
            for pair in range(pairs):
                cols = pl.ds(pair * 2 * HEAD_DIM, 2 * HEAD_DIM)
                keys, values = k_ref[k_rows, cols], v_ref[k_rows, cols]
                q_sides, grad_sides = halves(q_ref[q_rows, cols]), halves(grad[q_rows, cols])
                lows, slopes = [], []
                for side in range(2):
                    h = 2 * pair + side
                    scores = jnp.where(same, dot_right(keys, q_sides[side]) * SCALE2, MASKED)
                    probs = jnp.exp2(scores - lse[pl.ds(h, 1), q_rows])
                    grad_probs = dot_right(values, grad_sides[side])
                    slope = (probs * (grad_probs - delta[pl.ds(h, 1), q_rows])).astype(BF16)
                    lows.append(probs.astype(BF16))
                    slopes.append(slope)
                    head = pl.ds(h * HEAD_DIM, HEAD_DIM)
                    dq[head, q_rows] += dot(k_turned[head, k_rows], slope)
                dv[:, cols] += dot(jnp.concatenate(lows, 1), jnp.concatenate(grad_sides, 0))
                dk[:, cols] += dot(jnp.concatenate(slopes, 1), jnp.concatenate(q_sides, 0))
            return carry

        lax.fori_loop(low[kb], high[kb], step, 0)
        dk_out[k_rows, :] = (dk[...] * SCALE).astype(BF16)
        dv_out[k_rows, :] = dv[...].astype(BF16)

    @pl.loop(0, rows // BLOCK)
    def _(qb):
        q_rows = pl.ds(pl.multiple_of(qb * BLOCK, BLOCK), BLOCK)
        dq_out[q_rows, :] = (dq[:, q_rows] * SCALE).T.astype(BF16)


def attend_back(core, low, high, q, k, v, out, own, other, lse, seg_row, seg_col):
    rows, width = q.shape
    heads = width // HEAD_DIM
    whole = lambda shape: pl.BlockSpec(shape, lambda i, *_: (0,) * len(shape))
    return pl.pallas_call(
        attend_back_kernel,
        out_shape=[jax.ShapeDtypeStruct((rows, width), BF16)] * 3,
        grid_spec=pltpu.PrefetchScalarGridSpec(
            num_scalar_prefetch=3,
            grid=(1,),
            in_specs=[whole((rows, width))] * 4
            + [whole((rows // 2, width))] * 2
            + [whole((heads, rows)), whole((1, rows)), whole((rows, 1))],
            out_specs=[whole((rows, width))] * 3,
            scratch_shapes=[
                pltpu.VMEM((rows, width), BF16),
                pltpu.VMEM((width, rows), BF16),
                pltpu.VMEM((8, rows), F32),
                pltpu.VMEM((width, rows), F32),
                pltpu.VMEM((BLOCK, width), F32),
                pltpu.VMEM((BLOCK, width), F32),
            ],
        ),
        compiler_params=params(),
        cost_estimate=pl.CostEstimate(
            flops=10 * rows * rows * width * 2,
            bytes_accessed=16 << 20,
            transcendentals=rows * rows * heads // 2,
        ),
        name="attend_back",
    )(core, low, high, q, k, v, out, own, other, lse, seg_row, seg_col)


def row_mean(values):
    return jnp.mean(values, axis=-1, keepdims=True)


def norm(values):
    centre = values - row_mean(values)
    scale = lax.rsqrt(row_mean(centre * centre) + EPS)
    return centre * scale, scale


def norm_back(normed, scale, gain, grad):
    inner = grad * gain
    return scale * (inner - row_mean(inner) - normed * row_mean(inner * normed))


def column_sum(values):
    return jnp.sum(values.astype(F32), axis=0, keepdims=True)


def rows_kernel(
    core, x_ref, mine, theirs, cot, wo, we, wr, vectors, be,
    out, ga_mine, ga_theirs, residual, act, ge, low_out, gr_out, gb_out, sums, sum_e, slope,
):
    width = x_ref.shape[1]
    half = width // 2
    chunks = we.shape[1] // width
    bo, br = vectors[0:1, :], vectors[1:2, :]
    gain1, shift1, gain2, shift2 = [vectors[n : n + 1, :] for n in range(2, 6)]
    at_mine = pl.multiple_of(core[0] * half, half)
    at_theirs = pl.multiple_of((1 - core[0]) * half, half)
    wo_mine, wo_theirs = wo[pl.ds(at_mine, half), :], wo[pl.ds(at_theirs, half), :]

    @pl.when(pl.program_id(0) == 0)
    def _():
        sums[...] = jnp.zeros_like(sums)
        sum_e[...] = jnp.zeros_like(sum_e)

    branch = dot(mine[...], wo_mine) + dot(theirs[...], wo_theirs) + bo
    normed1, scale1 = norm(x_ref[...].astype(F32) + branch)
    first = normed1 * gain1 + shift1
    first_low = first.astype(BF16)
    low_out[...] = first_low
    reduced = jnp.zeros_like(first)
    for j in range(chunks):
        cols = slice(j * width, (j + 1) * width)
        u = dot(first_low, we[:, cols]) + be[:, cols]
        square = u * u
        curve = jnp.tanh(GELU_A * (u + GELU_B * (square * u)))
        cdf = 0.5 * (1.0 + curve)
        slope[:, cols] = cdf + (0.5 * GELU_A) * u * (1.0 - curve * curve) * (
            1.0 + (3.0 * GELU_B) * square
        )
        activated = (u * cdf).astype(BF16)
        act[:, cols] = activated
        reduced += dot(activated, wr[cols, :])
    normed2, scale2 = norm(first + (reduced + br))
    out[...] = (normed2 * gain2 + shift2).astype(BF16)

    incoming = cot[...].astype(F32)
    grad_second = norm_back(normed2, scale2, gain2, incoming)
    grad_reduced = grad_second.astype(BF16)
    gr_out[...] = grad_reduced
    grad_first = grad_second
    for j in range(chunks):
        cols = slice(j * width, (j + 1) * width)
        grad_expanded = (dot_right(grad_reduced, wr[cols, :]) * slope[:, cols]).astype(BF16)
        ge[:, cols] = grad_expanded
        sum_e[:, cols] += column_sum(grad_expanded)
        grad_first += dot_right(grad_expanded, we[:, cols])
    grad_residual = norm_back(normed1, scale1, gain1, grad_first)
    residual[...] = grad_residual
    grad_branch = grad_residual.astype(BF16)
    gb_out[...] = grad_branch
    ga_mine[...] = dot_right(grad_branch, wo_mine).astype(BF16)
    ga_theirs[...] = dot_right(grad_branch, wo_theirs).astype(BF16)
    sums[0:1, :] += column_sum(grad_branch)
    sums[1:2, :] += column_sum(grad_reduced)
    sums[2:3, :] += column_sum(grad_first * normed1)
    sums[3:4, :] += column_sum(grad_first)
    sums[4:5, :] += column_sum(incoming * normed2)
    sums[5:6, :] += column_sum(incoming)


def row_local(core, x, mine, theirs, cot, wo, we, wr, vectors, be):
    rows, width = x.shape
    half, wide = width // 2, we.shape[1]
    block = lambda cols: pl.BlockSpec((ROWS, cols), lambda i, *_: (i, 0))
    fixed = lambda a: pl.BlockSpec(a.shape, lambda i, *_: (0, 0), pipeline_mode=pl.Buffered(1))
    shape = lambda cols, kind: jax.ShapeDtypeStruct((rows, cols), kind)
    resident = lambda r, cols: pl.BlockSpec((r, cols), lambda i, *_: (0, 0))
    return pl.pallas_call(
        rows_kernel,
        out_shape=[
            shape(width, BF16),
            shape(half, BF16),
            shape(half, BF16),
            shape(width, F32),
            shape(wide, BF16),
            shape(wide, BF16),
            shape(width, BF16),
            shape(width, BF16),
            shape(width, BF16),
            jax.ShapeDtypeStruct((8, width), F32),
            jax.ShapeDtypeStruct((1, wide), F32),
        ],
        grid_spec=pltpu.PrefetchScalarGridSpec(
            num_scalar_prefetch=1,
            grid=(rows // ROWS,),
            in_specs=[
                block(width),
                block(half),
                block(half),
                block(width),
                fixed(wo),
                fixed(we),
                fixed(wr),
                fixed(vectors),
                fixed(be),
            ],
            out_specs=[
                block(width),
                block(half),
                block(half),
                block(width),
                block(wide),
                block(wide),
                block(width),
                block(width),
                block(width),
                resident(8, width),
                resident(1, wide),
            ],
            scratch_shapes=[pltpu.VMEM((ROWS, wide), F32)],
        ),
        compiler_params=params(),
        cost_estimate=pl.CostEstimate(
            flops=2 * 2 * rows * width * (width + 2 * wide),
            bytes_accessed=40 << 20,
            transcendentals=rows * wide,
        ),
        name="row_local",
    )(core, x, mine, theirs, cot, wo, we, wr, vectors, be)


def weight_grad_kernel(left, right, out):
    out[...] = dot_left(left[...], right[...]).astype(out.dtype)


def weight_grad(left, right, kind):
    rows, m = left.shape
    n = right.shape[1]
    tm, tn = min(m, 768), min(n, 768)
    return pl.pallas_call(
        weight_grad_kernel,
        out_shape=jax.ShapeDtypeStruct((m, n), kind),
        grid=(m // tm, n // tn),
        in_specs=[
            pl.BlockSpec((rows, tm), lambda i, j: (0, i)),
            pl.BlockSpec((rows, tn), lambda i, j: (0, j)),
        ],
        out_specs=pl.BlockSpec((tm, tn), lambda i, j: (i, j)),
        compiler_params=params(),
        cost_estimate=pl.CostEstimate(
            flops=2 * rows * m * n, bytes_accessed=16 << 20, transcendentals=0
        ),
        name="weight_grad",
    )(left, right)


def input_grad_kernel(core, own, other, d_ref, w_ref, dw, sums, dx_own, dx_other):
    part = pl.program_id(0)
    rows = own.shape[0]
    mine = pl.multiple_of(core[0] * rows, rows)
    theirs = pl.multiple_of((1 - core[0]) * rows, rows)
    d_own, d_other = d_ref[0, pl.ds(mine, rows), :], d_ref[0, pl.ds(theirs, rows), :]
    dw[0] = (dot_left(own[...], d_own) + dot_left(other[...], d_other)).astype(dw.dtype)
    sums[0] = jnp.broadcast_to(column_sum(d_own) + column_sum(d_other), sums.shape[1:])
    to_own, to_other = dot_right(d_own, w_ref[0]), dot_right(d_other, w_ref[0])

    @pl.when(part == 0)
    def _():
        dx_own[...] = to_own
        dx_other[...] = to_other

    @pl.when(part > 0)
    def _():
        dx_own[...] += to_own
        dx_other[...] += to_other


def input_grad(core, own, other, grads, weights, kind):
    rows, width = own.shape
    half = width // 2
    whole = lambda shape: pl.BlockSpec(shape, lambda i, *_: (0,) * len(shape))
    return pl.pallas_call(
        input_grad_kernel,
        out_shape=[
            jax.ShapeDtypeStruct((3, width, half), kind),
            jax.ShapeDtypeStruct((3, 8, half), F32),
            jax.ShapeDtypeStruct((rows, width), F32),
            jax.ShapeDtypeStruct((rows, width), F32),
        ],
        grid_spec=pltpu.PrefetchScalarGridSpec(
            num_scalar_prefetch=1,
            grid=(3,),
            in_specs=[
                whole((rows, width)),
                whole((rows, width)),
                pl.BlockSpec((1, 2 * rows, half), lambda i, core: (i, 0, 0)),
                pl.BlockSpec((1, width, half), lambda i, core: (i, 0, core[0])),
            ],
            out_specs=[
                pl.BlockSpec((1, width, half), lambda i, core: (i, 0, 0)),
                pl.BlockSpec((1, 8, half), lambda i, core: (i, 0, 0)),
                whole((rows, width)),
                whole((rows, width)),
            ],
        ),
        compiler_params=params(),
        cost_estimate=pl.CostEstimate(
            flops=2 * 2 * 2 * rows * width * 3 * half, bytes_accessed=20 << 20, transcendentals=0
        ),
        name="input_grad",
    )(core, own, other, grads, weights)


def local(tokens, segment_ids, cotangent, *shards):
    rep_size, shard_size = lax.axis_size("rep"), lax.axis_size("shard")
    rep, shard = lax.axis_index("rep"), lax.axis_index("shard")
    core = shard % 2
    core_arg = core.reshape(1).astype(jnp.int32)
    width = tokens.shape[2]
    half = width // 2
    both = ("rep", "shard")

    def flat(r, s):
        return r * shard_size + s

    def route(k, back=False):
        pairs = []
        for r in range(rep_size):
            for s in range(shard_size):
                there = (flat(r, s), flat(2 * (s % 2) + (r + k) % 2, s - s % 2 + r // 2))
                pairs.append(there[::-1] if back else there)
        return pairs

    swap_pairs = [(flat(r, s), flat(r, s ^ 1)) for r in range(rep_size) for s in range(shard_size)]

    def swap(array):
        return lax.ppermute(array, both, swap_pairs)

    odd = rep % 2

    def to_sequences(array):
        a, b = array[0], array[1]
        even_part = lax.ppermute(jnp.where(odd == 0, a, b), both, route(0))
        odd_part = lax.ppermute(jnp.where(odd == 0, b, a), both, route(1))
        return jnp.concatenate(
            [jnp.where(odd == 0, even_part, odd_part), jnp.where(odd == 0, odd_part, even_part)]
        )

    def from_sequences(array):
        rows = array.shape[0] // 2
        a, b = array[:rows], array[rows:]
        even_part = lax.ppermute(jnp.where(odd == 0, a, b), both, route(0, True))
        odd_part = lax.ppermute(jnp.where(odd == 0, b, a), both, route(1, True))
        return jnp.stack(
            [jnp.where(odd == 0, even_part, odd_part), jnp.where(odd == 0, odd_part, even_part)]
        )

    matrices = [lax.all_gather(m, "shard", axis=0, tiled=True) for m in shards[:6]]
    wq, wk, wv, wo, we, wr = matrices
    small = jnp.concatenate(shards[6:])
    small = lax.all_gather(small[None], "shard", axis=0, tiled=True)
    vectors, at = [], 0
    for member in shards[6:]:
        n = member.shape[0]
        vectors.append(small[:, at : at + n].reshape(1, n * shard_size).astype(F32))
        at += n
    bq, bv, bo, be, br, gain1, shift1, gain2, shift2 = vectors

    own = to_sequences(tokens)
    cot = to_sequences(cotangent)
    other = swap(own)
    swapped_ids = swap(segment_ids)
    ids = jnp.where(rep // 2 == core, segment_ids, swapped_ids)
    segments = lax.dynamic_index_in_dim(ids, odd, 0, keepdims=False)
    blocks = segments.reshape(-1, BLOCK)
    begin = jnp.sum((segments[None, :] < blocks[:, :1]).astype(jnp.int32), axis=1)
    end = jnp.sum((segments[None, :] <= blocks[:, -1:]).astype(jnp.int32), axis=1)
    low, high = begin // BLOCK, (end + BLOCK - 1) // BLOCK
    seg_row, seg_col = segments[None, :], segments[:, None]

    q, k, v = project(core_arg, own, other, wq, wk, wv, bq, bv)
    attended, lse = attend(low, high, q, k, v, seg_row, seg_col)
    rows = own.shape[0]
    mine = lax.dynamic_slice_in_dim(attended, core * rows, rows)
    theirs = swap(lax.dynamic_slice_in_dim(attended, (1 - core) * rows, rows))
    table = jnp.concatenate([bo, br, gain1, shift1, gain2, shift2, bo, bo])
    out, ga_mine, ga_theirs, residual, act, ge, first_low, gr, gb, sums, sum_e = row_local(
        core_arg, own, mine, theirs, cot, wo, we, wr, table, be
    )
    ga_other = swap(ga_theirs)
    kind = F32
    dwr = weight_grad(act, gr, kind)
    dwe = weight_grad(first_low, ge, kind)
    dwo_mine, dwo_theirs = weight_grad(mine, gb, kind), weight_grad(theirs, gb, kind)
    dq, dk, dv = attend_back(
        core_arg, low, high, q, k, v, attended, ga_mine, ga_other, lse, seg_row, seg_col
    )
    dw, sum_qkv, dx_own, dx_other = input_grad(
        core_arg, own, other, jnp.stack([dq, dk, dv]), jnp.stack([wq, wk, wv]), kind
    )
    dx = (residual + dx_own + swap(dx_other.astype(BF16)).astype(F32)).astype(BF16)

    def place(part, dim):
        zero = jnp.zeros_like(part)
        return jnp.where(
            core == 0,
            jnp.concatenate([part, zero], axis=dim),
            jnp.concatenate([zero, part], axis=dim),
        )

    dwo = jnp.where(
        core == 0,
        jnp.concatenate([dwo_mine, dwo_theirs]),
        jnp.concatenate([dwo_theirs, dwo_mine]),
    )
    totals = (
        place(dw[0], 1),
        place(dw[1], 1),
        place(dw[2], 1),
        dwo,
        dwe,
        dwr,
        place(sum_qkv[0, 0], 0),
        place(sum_qkv[2, 0], 0),
        sums[0],
        sum_e[0],
        sums[1],
        sums[2],
        sums[3],
        sums[4],
        sums[5],
    )
    summed = lax.psum_scatter(totals, "shard", scatter_dimension=0, tiled=True)
    final = [part.astype(F32) for part in lax.psum([p.astype(BF16) for p in summed], "rep")]
    return (from_sequences(out), from_sequences(dx)) + tuple(final)


def solution(mesh):
    row = P("shard", "rep", None)
    in_specs = (row, P("shard", None), row) + (P("shard", None),) * 6 + (P("shard"),) * 9
    out_specs = (row, row) + (P("shard", None),) * 6 + (P("shard"),) * 9
    return jax.shard_map(local, mesh=mesh, in_specs=in_specs, out_specs=out_specs, check_vma=False)
```

time: 1380 us -> 778 us (0.56)
  matrix products: 385 us -> 0 us
  other arithmetic: 327 us -> 54.2 us
  Pallas kernels: 0 us -> 216 us
  waiting for transfers between devices: 472 us -> 388 us
  local copies, waits for them, and re-layouts: 93.1 us -> 14.9 us
  starting transfers between devices: 1.32 us -> 34.6 us
  blocking collectives: 79.7 us -> 54.8 us
    dot_general x84 -> x0, matrix products: 385 us -> none  [the longest x8 56.7 us: block_scores(): unmasked = product()]
    pallas_call x0 -> x9, Pallas kernels: none -> 216 us  [the longest x1 64.3 us: attend_back(): pl.pallas_call(attend_back_kernel, out_shape=[jax.ShapeDtypeStruct((rows,...]
    sub x2 -> x0, other arithmetic: 164 us -> none  [attend_backward(): grad_scores = (chances * (grad_chances - centre)).astype(jnp.bfloat16)]
    unnamed x24 -> x13, waiting for transfers between devices: 103 us -> 3.75 us
    convert_element_type x26 -> x23, other arithmetic: 98.8 us -> 26 us  [the longest x15 11 us: local(): part.astype(F32)]
    reduce_scatter x3 -> x6, waiting for transfers between devices: 197 us -> 265 us  [local(): summed = lax.psum_scatter(totals, 'shard', scatter_dimension=0, tiled=True)]
    all_gather x10 -> x6, waiting for transfers between devices: 140 us -> 77.3 us  [local(): lax.all_gather(m, 'shard', axis=0, tiled=True)]
    slice x22 -> x3, local copies, waits for them, and re-layouts: 51.4 us -> 0.99 us  [the longest x1 0.76 us: local(): sum_qkv[2, 0]]
  transfers between devices with their start and end apart: 21 -> 26, of which waited for: 12 -> 9; matrix products, arithmetic and copies ran while one was open for 51% -> 8% of each run, Pallas kernels for 0% -> 23%
where the time goes in v1:
time: 778 us
  waiting for transfers between devices  388 us (50%)
  Pallas kernels  216 us (28%)
  blocking collectives  54.8 us (7%)
  other arithmetic  54.2 us (7%)
  starting transfers between devices  34.6 us (4%)
  between operations  15.6 us (2%)
  local copies, waits for them, and re-layouts  14.9 us (2%)
    reduce_scatter x6, waiting for transfers between devices, local(): summed = lax.psum_scatter(totals, 'shard', scatter_dimension=0, tiled=True)  265 us
    all_gather x6, waiting for transfers between devices, local(): lax.all_gather(m, 'shard', axis=0, tiled=True)  77.3 us
    pallas_call x1, Pallas kernels, attend_back(): pl.pallas_call(attend_back_kernel, out_shape=[jax.ShapeDtypeStruct((rows,...  64.3 us
    pallas_call x1, Pallas kernels, attend(): pl.pallas_call(attend_kernel, out_shape=[jax.ShapeDtypeStruct((rows, widt...  57.2 us
    pallas_call x1, Pallas kernels, row_local(): pl.pallas_call(rows_kernel, out_shape=[shape(width, BF16), shape(half, BF...  40.1 us
    unnamed x1, blocking collectives  28.8 us
    pallas_call x4, Pallas kernels, weight_grad(): pl.pallas_call(weight_grad_kernel, out_shape=jax.ShapeDtypeStruct((m, n),...  27.4 us
    psum x1, waiting for transfers between devices, local(): lax.psum([p.astype(BF16) for p in summed], 'rep')  25.4 us
  transfers between devices with their start and end apart: 26, of which 9 were waited for; matrix products, arithmetic and copies ran while one was open for 8% of the time, Pallas kernels for 23%

profile of v1, /device:TPU:0, one launch (start us, length us, event | category | flops | bytes accessed | tf_op | source)
XLA Modules:
  0.0 778.0 jit_solution(5691548814465940563)
XLA Ops:
  12.1 3.0 collective-permute-start.1
  15.1 16.3 %collective-permute-done.1 = bf16[512,768]{1,0:T(8,128)(2,1)S(1)} collective-permute-done((bf16[512,768]{1,0:T(8,128)(2,1)S(1)}, bf16[512,768]{1,0:T(8,128)(2,1)S(1)}, u32[]{:S(2)}, u32[]{:S(2)}) %collective-permute-start.1) | collective-permute-done | bytes 786464 | tf_op jit(solution)/shard_map/ppermute | solution.py:529
  31.7 3.2 collective-permute-start.3
  39.7 16.5 %all-gather.1 = bf16[8,1,1152]{2,1,0:T(2,128)(2,1)S(1)} all-gather(bf16[1,1,1152]{2,1,0:T(2,128)(2,1)S(1)} %reshape.191), channel_id=2, replica_groups=mesh['rep'=4,'shard'=8] {'shard'}, dimensions={0}, use_global_device_ids=true | all-gather | bytes 20736 | tf_op jit(solution)/shard_map/all_gather | solution.py:546
  61.1 22.2 %all-gather.9.cloned.1.call-done.wq = bf16[768,768]{1,0:T(8,128)(2,1)} async-done(((bf16[96,768]{1,0:T(8,128)(2,1)}), bf16[768,768]{1,0:T(8,128)(2,1)}) %all-gather.9.cloned.1.call-update) | async-done | bytes 1179664 | tf_op jit(solution)/shard_map/all_gather | solution.py:543
  83.3 9.6 %project.1 = (bf16[2048,384]{1,0:T(8,128)(2,1)}, bf16[2048,384]{1,0:T(8,128)(2,1)}, bf16[2048,384]{1,0:T(8,128)(2,1)}) custom-call(s32[1]{0:T(128)} %bitcast.core, bf16[1024,768]{1,0:T(8,128)(2,1)} %copy-done.3, bf16[1024,768]{1,0:T(8,128)(2,1)} %collective-permute-done.3.other, bf16[768,768]{1,0:T(8,128)(2,1)} %all-gather.9.cloned.1.call-done.wq, ...), custom_call_target="tpu_custom_call" | custom-call | flops 3623878656 | bytes 10485760 | tf_op jit(solution)/shard_map/project/pallas_call | solution.py:65
  93.0 57.2 %attend.1 = (bf16[2048,384]{1,0:T(8,128)(2,1)}, f32[6,2048]{1,0:T(8,128)}) custom-call(s32[8]{0:T(128)} %get-tuple-element.131.low, s32[8]{0:T(128)} %get-tuple-element.130.high, bf16[2048,384]{1,0:T(8,128)(2,1)} %get-tuple-element.40.q_ref, bf16[2048,384]{1,0:T(8,128)(2,1)} %get-tuple-element.41.k_ref, bf16[2048,384]{1,0:T(8,128)(2,1)} %get-tuple-element.42.v_ref, ...), custom_call_target="tpu_custom_call" | custom-call | flops 12884901888 | bytes 8388608 | tf_op jit(solution)/shard_map/attend/pallas_call | solution.py:145
  150.2 2.4 constant_dynamic-slice_fusion
  157.3 3.0 all-gather.17.cloned.1.call-done.we
  160.3 52.1 %all-gather.19.cloned.1.call-done.wr = bf16[3072,768]{1,0:T(8,128)(2,1)} async-done(((bf16[384,768]{1,0:T(8,128)(2,1)}), bf16[3072,768]{1,0:T(8,128)(2,1)}) %all-gather.19.cloned.1.call-update) | async-done | bytes 4718608 | tf_op jit(solution)/shard_map/all_gather | solution.py:543
  212.4 40.1 %row_local.1 = (bf16[1024,768]{1,0:T(8,128)(2,1)}, bf16[1024,384]{1,0:T(8,128)(2,1)}, bf16[1024,384]{1,0:T(8,128)(2,1)}, f32[1024,768]{1,0:T(8,128)}, bf16[1024,...) custom-call(s32[1]{0:T(128)} %bitcast.core, ...), custom_call_target="tpu_custom_call" | custom-call | flops 21743271936 | bytes 41943040 | tf_op jit(solution)/shard_map/row_local/pallas_call | solution.py:363
  252.8 3.5 weight_grad.4
  256.3 3.6 weight_grad.5
  259.9 3.4 maximum_select_fusion
  266.8 64.3 %attend_back.1 = (bf16[2048,384]{1,0:T(8,128)(2,1)}, bf16[2048,384]{1,0:T(8,128)(2,1)}, bf16[2048,384]{1,0:T(8,128)(2,1)}) custom-call(s32[1]{0:T(128)} %bitcast.core, s32[8]{0:T(128)} %get-tuple-element.131.low, s32[8]{0:T(128)} %get-tuple-element.130.high, bf16[2048,384]{1,0:T(8,128)(2,1)} %get-tuple-element.40.q_ref, ...), custom_call_target="tpu_custom_call" | custom-call | flops 32212254720 | bytes 16777216 | tf_op jit(solution)/shard_map/attend_back/pallas_call | solution.py:244
  331.1 5.1 pad_maximum_fusion.d_ref
  336.2 17.7 %input_grad.1 = (f32[3,768,384]{2,1,0:T(8,128)}, f32[3,8,384]{2,1,0:T(8,128)}, f32[1024,768]{1,0:T(8,128)}, f32[1024,768]{1,0:T(8,128)}) custom-call(s32[1]{0:T(128)} %bitcast.core, bf16[1024,768]{1,0:T(8,128)(2,1)} %copy-done.3, bf16[1024,768]{1,0:T(8,128)(2,1)} %collective-permute-done.3.other, bf16[3,2048,384]{2,1,0:T(8,128)(2,1)} %pad_maximum_fusion.d_ref, ...), custom_call_target="tpu_custom_call" | custom-call | flops 7247757312 | bytes 20971520 | tf_op jit(solution)/shard_map/input_grad/pallas_call | solution.py:467
  353.9 2.2 slice_bitcast_fusion
  361.2 10.1 %weight_grad.6 = f32[768,3072]{1,0:T(8,128)} custom-call(bf16[1024,768]{1,0:T(8,128)(2,1)} %get-tuple-element.56.left, bf16[1024,3072]{1,0:T(8,128)(2,1)} %get-tuple-element.57.right), custom_call_target="tpu_custom_call" | custom-call | flops 4831838208 | bytes 16777216 | tf_op jit(solution)/shard_map/weight_grad/pallas_call | solution.py:425
  371.4 10.3 %weight_grad.7 = f32[3072,768]{1,0:T(8,128)} custom-call(bf16[1024,3072]{1,0:T(8,128)(2,1)} %get-tuple-element.58.left, bf16[1024,768]{1,0:T(8,128)(2,1)} %get-tuple-element.59.right), custom_call_target="tpu_custom_call" | custom-call | flops 4831838208 | bytes 16777216 | tf_op jit(solution)/shard_map/weight_grad/pallas_call | solution.py:425
  387.0 2.6 broadcast_select_fusion.3
  389.6 7.4 collective-permute-start.7
  397.1 13.0 %collective-permute-start.8 = (bf16[512,768]{1,0:T(8,128)(2,1)}, bf16[512,768]{1,0:T(8,128)(2,1)}, u32[]{:S(2)}, u32[]{:S(2)}) collective-permute-start(bf16[512,768]{1,0:T(8,128)(2,1)} %get-tuple-element.111), channel_id=1, source_target_pairs={{8,0},{24,1},{10,2},{26,3},{12,4},{28,5},{14,6},{30,7},{0,8},{16,9... | collective-permute-start | bytes 2359304 | tf_op jit(solution)/shard_map/ppermute | solution.py:538
  413.5 31.3 %reduce-scatter.9.cloned.1.call-done = f32[96,768]{1,0:T(8,128)} async-done(((f32[768,768]{1,0:T(8,128)}), f32[96,768]{1,0:T(8,128)}) %reduce-scatter.9.cloned.1.call-update) | async-done | bytes 294928 | tf_op jit(solution)/shard_map/reduce_scatter | solution.py:618
  446.4 36.0 %reduce-scatter.11.cloned.1.call-done = f32[96,768]{1,0:T(8,128)} async-done(((f32[768,768]{1,0:T(8,128)}), f32[96,768]{1,0:T(8,128)}) %reduce-scatter.11.cloned.1.call-update) | async-done | bytes 294928 | tf_op jit(solution)/shard_map/reduce_scatter | solution.py:618
  484.1 99.5 %reduce-scatter.15.cloned.1.call-done = f32[96,3072]{1,0:T(8,128)} async-done(((f32[768,3072]{1,0:T(8,128)}), f32[96,3072]{1,0:T(8,128)}) %reduce-scatter.15.cloned.1.call-update) | async-done | bytes 1179664 | tf_op jit(solution)/shard_map/reduce_scatter | solution.py:618
  585.8 97.9 %reduce-scatter.17.cloned.1.call-done = f32[384,768]{1,0:T(8,128)} async-done(((f32[3072,768]{1,0:T(8,128)}), f32[384,768]{1,0:T(8,128)}) %reduce-scatter.17.cloned.1.call-update) | async-done | bytes 1179664 | tf_op jit(solution)/shard_map/reduce_scatter | solution.py:618
  685.9 2.9 add_convert_fusion
  692.0 28.8 %all-reduce.19 = (bf16[768]{0:T(1024)(128)(2,1)S(1)}, bf16[768]{0:T(1024)(128)(2,1)S(1)}, bf16[768]{0:T(1024)(128)(2,1)S(1)}, bf16[3072]{0:T(1024)(128)(2,1)S(1)...) all-reduce(f32[768]{0:T(1024)S(1)} %pad_select_fusion.4, ...), channel_id=9, replica_groups=mesh['rep'=4,'shard'=8] {'shard'}, use_global_device_ids=true, to_apply=%region_14.15.clone | all-reduce | flops 9216 | bytes 55296
  721.5 9.5 %all-reduce.20 = (bf16[96]{0:T(256)(128)(2,1)S(1)}, bf16[96]{0:T(256)(128)(2,1)S(1)}, bf16[96]{0:T(256)(128)(2,1)S(1)}, bf16[384]{0:T(512)(128)(2,1)S(1)}, bf16[...) all-reduce(bf16[96]{0:T(256)(128)(2,1)S(1)} %dynamic-slice.35, ...), channel_id=1, replica_groups=mesh['rep'=4,'shard'=8] {'rep'}, use_global_device_ids=true, to_apply=%region_15.16 | all-reduce | flops 1152 | bytes 4608 | tf_op jit(solution)/shard_map/psum | solution.py:619
  739.8 25.4 %all-reduce.24.cloned.1.call-done = (bf16[96,768]{1,0:T(8,128)(2,1)}, bf16[96,768]{1,0:T(8,128)(2,1)}, bf16[96,768]{1,0:T(8,128)(2,1)}, bf16[96,768]{1,0:T(8,128...) async-done(((bf16[96,768]{1,0:T(8,128)(2,1)}, bf16[96,768]{1,0:T(8,128)(2,1)}, bf16[96,768]{1,0:T(8,128)(2,1)}, bf16[96,768]{1,0:T(8,128)(2,1)}, ...) | async-done | bytes 1769488 | tf_op jit(solution)/shard_map/psum | solution.py:619
  765.2 2.3 convert_element_type.218
  (183 shorter events, 59.9 us)
Async XLA Ops:
  7.2 53.9 %all-gather.11.cloned.1.call-start = ((), (), s32[]{:S(2)}) async-start(), calls=%async_computation.7 | async-start | bytes 1327104 | tf_op jit(solution)/shard_map/all_gather | solution.py:543
  7.9 53.2 %all-gather.13.cloned.1.call-start = ((), (), s32[]{:S(2)}) async-start(), calls=%async_computation.8 | async-start | bytes 1327104 | tf_op jit(solution)/shard_map/all_gather | solution.py:543
  8.7 74.6 %all-gather.9.cloned.1.call-start = ((), (), s32[]{:S(2)}) async-start(), calls=%async_computation.6 | async-start | bytes 1327104 | tf_op jit(solution)/shard_map/all_gather | solution.py:543
  9.4 147.8 %all-gather.15.cloned.1.call-start = ((), (), s32[]{:S(2)}) async-start(), calls=%async_computation.9 | async-start | bytes 1327104 | tf_op jit(solution)/shard_map/all_gather | solution.py:543
  10.0 150.3 %all-gather.17.cloned.1.call-start = ((), (), s32[]{:S(2)}) async-start(), calls=%async_computation.10 | async-start | bytes 5308416 | tf_op jit(solution)/shard_map/all_gather | solution.py:543
  10.6 201.8 %all-gather.19.cloned.1.call-start = ((), (), s32[]{:S(2)}) async-start(), calls=%async_computation.11 | async-start | bytes 5308416 | tf_op jit(solution)/shard_map/all_gather | solution.py:543
  11.2 399.0 %reduce-scatter.13.cloned.1.call-start = ((), (), s32[]{:S(2)}) async-start(), calls=%async_computation.15 | async-start | bytes 2654208 | tf_op jit(solution)/shard_map/reduce_scatter | solution.py:618
  11.3 3.7 collective-permute-start
  12.1 19.3 %collective-permute-start.1 = (bf16[512,768]{1,0:T(8,128)(2,1)S(1)}, bf16[512,768]{1,0:T(8,128)(2,1)S(1)}, u32[]{:S(2)}, u32[]{:S(2)}) collective-permute-start(bf16[512,768]{1,0:T(8,128)(2,1)S(1)} %get-tuple-element.121), channel_id=1, source_target_pairs={{0,8},{1,24},{2,10},{3,26},{4,12},{5,28},{6,14},{7,30},{8,0},{9,16... | collective-permute-start | bytes 2359304 | tf_op jit(solution)/shard_map/ppermute | solution.py:529
  31.6 7.9 %copy-start.19 = (bf16[384]{0:T(512)(128)(2,1)S(1)}, bf16[384]{0:T(512)(128)(2,1)}, u32[]{:S(2)}) copy-start(bf16[384]{0:T(512)(128)(2,1)} %param.30) | copy-start | bytes 2308
  31.6 7.9 %copy-start.20 = (bf16[96]{0:T(256)(128)(2,1)S(1)}, bf16[96]{0:T(256)(128)(2,1)}, u32[]{:S(2)}) copy-start(bf16[96]{0:T(256)(128)(2,1)} %param.27) | copy-start | bytes 580
  31.7 51.6 %collective-permute-start.3 = (bf16[1024,768]{1,0:T(8,128)(2,1)S(1)}, bf16[1024,768]{1,0:T(8,128)(2,1)}, u32[]{:S(2)}, u32[]{:S(2)}) collective-permute-start(bf16[1024,768]{1,0:T(8,128)(2,1)S(1)} %pad_maximum_fusion.2.own.x_ref), channel_id=1, source_target_pairs={{0,1},{1,0},{2,3},{3,2},{4,5},{5,4},{6,7},{7,6},{8,9},{9,8},{10,11... | collective-permute-start | bytes 4718600 | tf_op jit(solution)/shard_map/ppermute | solution.py:522
  34.9 22.8 %collective-permute-start.2 = (s32[2,2048]{1,0:T(2,128)S(1)}, s32[2,2048]{1,0:T(2,128)S(1)}, u32[]{:S(2)}, u32[]{:S(2)}) collective-permute-start(s32[2,2048]{1,0:T(2,128)S(1)} %copy-done.18), channel_id=1, source_target_pairs={{0,1},{1,0},{2,3},{3,2},{4,5},{5,4},{6,7},{7,6},{8,9},{9,8},{10,11... | collective-permute-start | bytes 49160 | tf_op jit(solution)/shard_map/ppermute | solution.py:522
  36.3 118.5 %collective-permute-start.5 = (bf16[512,768]{1,0:T(8,128)(2,1)}, bf16[512,768]{1,0:T(8,128)(2,1)S(1)}, u32[]{:S(2)}, u32[]{:S(2)}) collective-permute-start(bf16[512,768]{1,0:T(8,128)(2,1)} %get-tuple-element.114), channel_id=1, source_target_pairs={{0,0},{1,16},{2,2},{3,18},{4,4},{5,20},{6,6},{7,22},{8,8},{9,24},{... | collective-permute-start | bytes 2359304 | tf_op jit(solution)/shard_map/ppermute | solution.py:528
  38.0 116.7 %collective-permute-start.6 = (bf16[512,768]{1,0:T(8,128)(2,1)S(1)}, bf16[512,768]{1,0:T(8,128)(2,1)}, u32[]{:S(2)}, u32[]{:S(2)}) collective-permute-start(bf16[512,768]{1,0:T(8,128)(2,1)S(1)} %get-tuple-element.115), channel_id=1, source_target_pairs={{0,8},{1,24},{2,10},{3,26},{4,12},{5,28},{6,14},{7,30},{8,0},{9,16... | collective-permute-start | bytes 2359304 | tf_op jit(solution)/shard_map/ppermute | solution.py:529
  58.8 34.1 %copy-start.15 = (s32[1,2048]{1,0:T(1,128)}, s32[1,2048]{1,0:T(1,128)S(1)}, u32[]{:S(2)}) copy-start(s32[1,2048]{1,0:T(1,128)S(1)} %get-tuple-element.100.seg_row) | copy-start | bytes 24580
  152.6 4.6 collective-permute-start.4
  157.3 55.1 %copy-start.9 = (bf16[1024,384]{1,0:T(8,128)(2,1)}, bf16[1024,384]{1,0:T(8,128)(2,1)S(1)}, u32[]{:S(2)}) copy-start(bf16[1024,384]{1,0:T(8,128)(2,1)S(1)} %collective-permute-done.4.theirs.left) | copy-start | bytes 2359300
  252.5 14.4 %collective-permute-start.9 = (bf16[1024,384]{1,0:T(8,128)(2,1)}, bf16[1024,384]{1,0:T(8,128)(2,1)}, u32[]{:S(2)}, u32[]{:S(2)}) collective-permute-start(bf16[1024,384]{1,0:T(8,128)(2,1)} %get-tuple-element.47), channel_id=1, source_target_pairs={{0,1},{1,0},{2,3},{3,2},{4,5},{5,4},{6,7},{7,6},{8,9},{9,8},{10,11... | collective-permute-start | bytes 2359304 | tf_op jit(solution)/shard_map/ppermute | solution.py:522
  263.2 148.6 %reduce-scatter.7.cloned.1.call-start = ((), (), s32[]{:S(2)}) async-start(), calls=%async_computation.12 | async-start | bytes 2654208 | tf_op jit(solution)/shard_map/reduce_scatter | solution.py:618
  357.8 87.0 %reduce-scatter.9.cloned.1.call-start = ((), (), s32[]{:S(2)}) async-start(), calls=%async_computation.13 | async-start | bytes 2654208 | tf_op jit(solution)/shard_map/reduce_scatter | solution.py:618
  359.5 123.0 %reduce-scatter.11.cloned.1.call-start = ((), (), s32[]{:S(2)}) async-start(), calls=%async_computation.14 | async-start | bytes 2654208 | tf_op jit(solution)/shard_map/reduce_scatter | solution.py:618
  361.1 222.5 %reduce-scatter.15.cloned.1.call-start = ((), (), s32[]{:S(2)}) async-start(), calls=%async_computation.16 | async-start | bytes 10616832 | tf_op jit(solution)/shard_map/reduce_scatter | solution.py:618
  371.3 312.4 %reduce-scatter.17.cloned.1.call-start = ((), (), s32[]{:S(2)}) async-start(), calls=%async_computation.17 | async-start | bytes 10616832 | tf_op jit(solution)/shard_map/reduce_scatter | solution.py:618
  381.6 383.6 %all-reduce.24.cloned.1.call-start = ((), (), s32[]{:S(2)}) async-start(), calls=%async_computation.18 | async-start | bytes 3538944 | tf_op jit(solution)/shard_map/psum | solution.py:619
  384.8 301.0 %collective-permute-start.10 = (bf16[1024,768]{1,0:T(8,128)(2,1)}, bf16[1024,768]{1,0:T(8,128)(2,1)}, u32[]{:S(2)}, u32[]{:S(2)}) collective-permute-start(bf16[1024,768]{1,0:T(8,128)(2,1)} %convert_element_type.206), channel_id=1, source_target_pairs={{0,1},{1,0},{2,3},{3,2},{4,5},{5,4},{6,7},{7,6},{8,9},{9,8},{10,11... | collective-permute-start | bytes 4718600 | tf_op jit(solution)/shard_map/ppermute | solution.py:522
  387.0 23.1 %copy-start.16 = (f32[8,768]{1,0:T(8,128)S(1)}, f32[8,768]{1,0:T(8,128)}, u32[]{:S(2)}) copy-start(f32[8,768]{1,0:T(8,128)} %get-tuple-element.61) | copy-start | bytes 73732
  389.6 346.0 %collective-permute-start.7 = (bf16[512,768]{1,0:T(8,128)(2,1)}, bf16[512,768]{1,0:T(8,128)(2,1)}, u32[]{:S(2)}, u32[]{:S(2)}) collective-permute-start(bf16[512,768]{1,0:T(8,128)(2,1)} %get-tuple-element.110), channel_id=1, source_target_pairs={{0,0},{16,1},{2,2},{18,3},{4,4},{20,5},{6,6},{22,7},{8,8},{24,9},{... | collective-permute-start | bytes 2359304 | tf_op jit(solution)/shard_map/ppermute | solution.py:537
  397.1 338.6 %collective-permute-start.8 = (bf16[512,768]{1,0:T(8,128)(2,1)}, bf16[512,768]{1,0:T(8,128)(2,1)}, u32[]{:S(2)}, u32[]{:S(2)}) collective-permute-start(bf16[512,768]{1,0:T(8,128)(2,1)} %get-tuple-element.111), channel_id=1, source_target_pairs={{8,0},{24,1},{10,2},{26,3},{12,4},{28,5},{14,6},{30,7},{0,8},{16,9... | collective-permute-start | bytes 2359304 | tf_op jit(solution)/shard_map/ppermute | solution.py:538
  585.8 100.1 %copy-start.2 = (f32[1024,768]{1,0:T(8,128)S(1)}, f32[1024,768]{1,0:T(8,128)}, u32[]{:S(2)}) copy-start(f32[1024,768]{1,0:T(8,128)} %get-tuple-element.45) | copy-start | bytes 9437188
  688.9 49.5 %collective-permute-start.11 = (bf16[512,768]{1,0:T(8,128)(2,1)S(1)}, bf16[512,768]{1,0:T(8,128)(2,1)S(1)}, u32[]{:S(2)}, u32[]{:S(2)}) collective-permute-start(bf16[512,768]{1,0:T(8,128)(2,1)S(1)} %get-tuple-element.106), channel_id=1, source_target_pairs={{0,0},{16,1},{2,2},{18,3},{4,4},{20,5},{6,6},{22,7},{8,8},{24,9},{... | collective-permute-start | bytes 2359304 | tf_op jit(solution)/shard_map/ppermute | solution.py:537
  689.6 48.8 %collective-permute-start.12 = (bf16[512,768]{1,0:T(8,128)(2,1)S(1)}, bf16[512,768]{1,0:T(8,128)(2,1)S(1)}, u32[]{:S(2)}, u32[]{:S(2)}) collective-permute-start(bf16[512,768]{1,0:T(8,128)(2,1)S(1)} %get-tuple-element.107), channel_id=1, source_target_pairs={{8,0},{24,1},{10,2},{26,3},{12,4},{28,5},{14,6},{30,7},{0,8},{16,9... | collective-permute-start | bytes 2359304 | tf_op jit(solution)/shard_map/ppermute | solution.py:538
  (23 other events, 103.3 us)
Sparse Core Ops, SparseCore 0:
  9.7 25.3 all-gather.10
  36.7 22.5 all-gather.12
  60.9 22.3 all-gather.8
  84.8 22.4 all-gather.14
  108.8 51.4 all-gather.16
  161.8 50.5 all-gather.18
  263.4 35.0 reduce-scatter.12
  357.9 49.3 reduce-scatter.6
  409.6 35.1 reduce-scatter.8
  447.0 35.4 reduce-scatter.10
  484.8 98.8 reduce-scatter.14
  585.8 97.8 reduce-scatter.16
  688.1 77.0 all-reduce.23

commit v2 on v1

v2 whole, which is shorter than its diff:
```python
import functools
import math

import jax
import jax.numpy as jnp
from jax import lax
from jax.experimental import pallas as pl
from jax.experimental.pallas import tpu as pltpu
from jax.sharding import PartitionSpec as P

HEAD_DIM = 64
BLOCK = 256
KEYS = 512
PREPARE = 512
DOCS = 8
ROWS = 256
MASKED = -1e30
EPS = 1e-05
UNITS = 8
EXTRA = 8
SCALE = HEAD_DIM**-0.5
SCALE2 = SCALE * math.log2(math.e)
GELU_A = math.sqrt(2.0 / math.pi)
GELU_B = 0.044715
F32 = jnp.float32
BF16 = jnp.bfloat16
VMEM_LIMIT = 60 * 1024 * 1024


def dot(left, right):
    return jnp.dot(left, right, preferred_element_type=F32)


def dot_right(left, right):
    return lax.dot_general(left, right, (((1,), (1,)), ((), ())), preferred_element_type=F32)


def dot_left(left, right):
    return lax.dot_general(left, right, (((0,), (0,)), ((), ())), preferred_element_type=F32)


def params(**more):
    return pltpu.CompilerParams(vmem_limit_bytes=VMEM_LIMIT, **more)


def stacked(ref):
    return ref[...].reshape(-1, ref.shape[-1])


def gather_kernel(
    nz, square, wide, square_all, wide_all,
    z_send, z_recv, p_send, p_recv, c_send, c_recv, own_send, own_recv, copied,
):
    r, s = lax.axis_index("rep"), lax.axis_index("shard")
    z = s // 2
    twin = (r, s ^ 1)
    barrier = pltpu.get_barrier_semaphore()

    def greet(device):
        pl.semaphore_signal(barrier, 1, device_id=device, device_id_type=pl.DeviceIdType.MESH)

    greet(twin)
    for k in (1, 2, 3):
        greet((r ^ k, s))
    for step in (1, -1):

        @pl.when((z + step >= 0) & (z + step < nz))
        def _(step=step):
            greet((r, s + 2 * step))

    pl.semaphore_wait(barrier, 4 + jnp.where(z > 0, 1, 0) + jnp.where(z < nz - 1, 1, 0))

    def copy(source, target, sent, got, device):
        return pltpu.make_async_remote_copy(
            source, target, sent, got, device_id=device, device_id_type=pl.DeviceIdType.MESH
        )

    kept = [
        pltpu.make_async_copy(square, square_all.at[s], copied.at[0]),
        pltpu.make_async_copy(wide, wide_all.at[s], copied.at[1]),
    ]
    own = [
        copy(square, square_all.at[s], own_send.at[0], own_recv.at[0], twin),
        copy(wide, wide_all.at[s], own_send.at[1], own_recv.at[1], twin),
    ]

    def onward(n, d, part):
        step = 1 - 2 * n
        at = s - 2 * step * d
        if part == 0:
            source = square if d == 0 else square_all.at[at]
            target = square_all.at[at]
        else:
            source = wide.at[r] if d == 0 else wide_all.at[at, r]
            target = wide_all.at[at, r]
        return copy(source, target, z_send.at[n, d, part], z_recv.at[n, d, part], (r, s + 2 * step))

    def sideways(n, d, k):
        at = s - 2 * (1 - 2 * n) * d
        part = wide_all.at[at, r]
        return copy(part, part, p_send.at[n, d - 1, k - 1], p_recv.at[n, d - 1, k - 1], (r ^ k, s))

    def across(n, d, k):
        at = s - 2 * (1 - 2 * n) * d
        part = square_all.at[at] if k == 4 else wide_all.at[at, r ^ k]
        return copy(part, part, c_send.at[n, d - 1, k], c_recv.at[n, d - 1, k], twin)

    def has(n, d):
        at = z - (1 - 2 * n) * d
        return (at >= 0) & (at < nz)

    def goes(n):
        at = z + 1 - 2 * n
        return (at >= 0) & (at < nz)

    for n in (0, 1):

        @pl.when(goes(n))
        def _(n=n):
            onward(n, 0, 1).start()
            onward(n, 0, 0).start()

    for c in own + kept:
        c.start()
    for d in range(1, nz):
        for n in (0, 1):

            @pl.when(has(n, d))
            def _(n=n, d=d):
                onward(n, d - 1, 1).wait_recv()
                if d < nz - 1:

                    @pl.when(goes(n))
                    def _():
                        onward(n, d, 1).start()

                for k in (1, 2, 3):
                    sideways(n, d, k).start()
                across(n, d, 0).start()
                onward(n, d - 1, 0).wait_recv()
                if d < nz - 1:

                    @pl.when(goes(n))
                    def _():
                        onward(n, d, 0).start()

                across(n, d, 4).start()

    for d in range(1, nz):
        for n in (0, 1):

            @pl.when(has(n, d))
            def _(n=n, d=d):
                for k in (1, 2, 3):
                    sideways(n, d, k).wait_recv()
                    across(n, d, k).start()

    for c in own + kept:
        c.wait()
    for n in (0, 1):

        @pl.when(goes(n))
        def _(n=n):
            onward(n, 0, 1).wait_send()
            onward(n, 0, 0).wait_send()

    for d in range(1, nz):
        for n in (0, 1):

            @pl.when(has(n, d))
            def _(n=n, d=d):
                for k in (1, 2, 3):
                    sideways(n, d, k).wait_send()
                for k in range(5):
                    across(n, d, k).wait()
                if d < nz - 1:

                    @pl.when(goes(n))
                    def _():
                        onward(n, d, 1).wait_send()
                        onward(n, d, 0).wait_send()


def gather_weights(square, wide, nz):
    anywhere = pl.BlockSpec(memory_space=pl.ANY)
    sems = lambda *shape: pltpu.SemaphoreType.DMA(shape)
    return pl.pallas_call(
        functools.partial(gather_kernel, nz),
        out_shape=[
            jax.ShapeDtypeStruct((2 * nz,) + square.shape, BF16),
            jax.ShapeDtypeStruct((2 * nz,) + wide.shape, BF16),
        ],
        in_specs=[anywhere] * 2,
        out_specs=[anywhere] * 2,
        scratch_shapes=[
            sems(2, nz - 1, 2),
            sems(2, nz - 1, 2),
            sems(2, nz - 1, 3),
            sems(2, nz - 1, 3),
            sems(2, nz - 1, 5),
            sems(2, nz - 1, 5),
            sems(2),
            sems(2),
            sems(2),
        ],
        compiler_params=params(collective_id=0, has_side_effects=True),
        cost_estimate=pl.CostEstimate(flops=0, bytes_accessed=150 << 20, transcendentals=0),
        name="gather_weights",
    )(square, wide)


def qkv_kernel(core, own, other, wq, wk, wv, bq, bv, q_out, k_out, v_out):
    per_core = pl.num_programs(0) // 2
    mine = pl.program_id(0) // per_core == core[0]
    rows = jnp.where(mine, own[...], other[...])
    q_out[...] = (dot(rows, stacked(wq)) + bq[...]).astype(BF16)
    k_out[...] = dot(rows, stacked(wk)).astype(BF16)
    v_out[...] = (dot(rows, stacked(wv)) + bv[...]).astype(BF16)


def project(core, own, other, square, bq, bv):
    rows, width = own.shape
    half = width // 2
    steps = rows // ROWS

    def side(flip):
        def index(i, core):
            first = jnp.where(core[0] == flip, 0, steps)
            return (jnp.clip(i - first, 0, steps - 1), 0)

        return index

    weight = lambda m: pl.BlockSpec(
        (UNITS, width // UNITS, half), lambda i, core: (0, m, core[0])
    )
    bias = pl.BlockSpec((1, half), lambda i, core: (0, core[0]))
    result = pl.BlockSpec((ROWS, half), lambda i, core: (i, 0))
    return pl.pallas_call(
        qkv_kernel,
        out_shape=[jax.ShapeDtypeStruct((2 * rows, half), BF16)] * 3,
        grid_spec=pltpu.PrefetchScalarGridSpec(
            num_scalar_prefetch=1,
            grid=(2 * steps,),
            in_specs=[
                pl.BlockSpec((ROWS, width), side(0)),
                pl.BlockSpec((ROWS, width), side(1)),
                weight(0),
                weight(1),
                weight(2),
                bias,
                bias,
            ],
            out_specs=[result] * 3,
        ),
        compiler_params=params(),
        cost_estimate=pl.CostEstimate(
            flops=2 * 2 * rows * width * 3 * half, bytes_accessed=10 << 20, transcendentals=0
        ),
        name="project",
    )(core, own, other, square, square, square, bq, bv)


def halves(pair):
    lane = lax.broadcasted_iota(jnp.int32, pair.shape, 1)
    zero = jnp.zeros_like(pair)
    return jnp.where(lane < HEAD_DIM, pair, zero), jnp.where(lane < HEAD_DIM, zero, pair)


def rows_at(n, size):
    return pl.ds(pl.multiple_of(n * size, size), size)


def widen(pair, extra):
    lane = lax.broadcasted_iota(jnp.int32, pair.shape, 1)
    return jnp.where(lane < HEAD_DIM, pair, extra[0]), jnp.where(lane < HEAD_DIM, extra[1], pair)


def same_document(ids, extra_lanes):
    slot = lax.broadcasted_iota(jnp.int32, (ids.shape[0], 2 * HEAD_DIM), 1) % HEAD_DIM
    hit = slot == ids
    for_keys = jnp.where(
        (slot < DOCS) & ~hit,
        MASKED,
        jnp.where((slot >= DOCS) & (slot < DOCS + extra_lanes), 1.0, 0.0),
    )
    return jnp.where(hit, 1.0, 0.0), for_keys.astype(BF16)


def attend_kernel(low, high, q_ref, k_ref, v_ref, seg_col, out, lse, qx, kx, v_turned, top, mix, kept):
    rows, width = q_ref.shape
    heads = width // HEAD_DIM
    pairs = heads // 2
    for at in range(0, rows, PREPARE):
        part = pl.ds(at, PREPARE)
        for_queries, for_keys = same_document(seg_col[part, :], 0)
        for_queries = for_queries.astype(BF16)
        for pair in range(pairs):
            cols = pl.ds(pair * 2 * HEAD_DIM, 2 * HEAD_DIM)
            both = slice(2 * pair, 2 * pair + 2)
            qx[both, part, :] = jnp.stack(widen(q_ref[part, cols], (for_queries, for_queries)))
            kx[both, part, :] = jnp.stack(widen(k_ref[part, cols], (for_keys, for_keys)))
            v_turned[both, :HEAD_DIM, part] = v_ref[part, cols].T.reshape(2, HEAD_DIM, PREPARE)
    v_turned[:, HEAD_DIM:, :] = jnp.ones_like(v_turned[:, HEAD_DIM:, :])

    @pl.loop(0, rows // BLOCK)
    def _(qb):
        q_rows = rows_at(qb, BLOCK)
        top[...] = jnp.full_like(top, MASKED)
        mix[...] = jnp.zeros_like(mix)

        def score(kb, carry):
            k_rows = rows_at(kb, KEYS)
            for h in range(heads):
                scores = dot_right(kx[h, k_rows, :], qx[h, q_rows, :])
                kept[h, k_rows, :] = scores
                top[h] = jnp.maximum(top[h], jnp.max(scores.reshape(KEYS // 8, 8, BLOCK), axis=0))
            return carry

        lax.fori_loop(low[qb], high[qb], score, 0)
        tops = [jnp.max(top[h], axis=0, keepdims=True) * SCALE2 for h in range(heads)]

        def weigh(kb, carry):
            k_rows = rows_at(kb, KEYS)
            for h in range(heads):
                weight = jnp.exp2(kept[h, k_rows, :] * SCALE2 - tops[h]).astype(BF16)
                mix[h] += dot(v_turned[h, :, k_rows], weight)
            return carry

        lax.fori_loop(low[qb], high[qb], weigh, 0)
        for h in range(heads):
            total = mix[h, HEAD_DIM : HEAD_DIM + 1, :]
            lse[pl.ds(h, 1), q_rows] = tops[h] + jnp.log2(total)
            mix[h, :HEAD_DIM, :] = mix[h, :HEAD_DIM, :] / total
        for pair in range(pairs):
            both = mix[2 * pair : 2 * pair + 2, :HEAD_DIM, :].reshape(2 * HEAD_DIM, BLOCK)
            out[q_rows, pl.ds(pair * 2 * HEAD_DIM, 2 * HEAD_DIM)] = both.T.astype(BF16)


def spans(begin, end, size):
    return begin // size, (end + size - 1) // size


def attend(begin, end, q, k, v, seg_col):
    rows, width = q.shape
    heads = width // HEAD_DIM
    whole = lambda shape: pl.BlockSpec(shape, lambda i, *_: (0,) * len(shape))
    wide = pltpu.VMEM((heads, rows, 2 * HEAD_DIM), BF16)
    return pl.pallas_call(
        attend_kernel,
        out_shape=[
            jax.ShapeDtypeStruct((rows, width), BF16),
            jax.ShapeDtypeStruct((heads, rows), F32),
        ],
        grid_spec=pltpu.PrefetchScalarGridSpec(
            num_scalar_prefetch=2,
            grid=(1,),
            in_specs=[whole((rows, width))] * 3 + [whole((rows, 1))],
            out_specs=[whole((rows, width)), whole((heads, rows))],
            scratch_shapes=[
                wide,
                wide,
                pltpu.VMEM((heads, HEAD_DIM + 16, rows), BF16),
                pltpu.VMEM((heads, 8, BLOCK), F32),
                pltpu.VMEM((heads, HEAD_DIM + 16, BLOCK), F32),
                pltpu.VMEM((heads, rows, BLOCK), F32),
            ],
        ),
        compiler_params=params(),
        cost_estimate=pl.CostEstimate(
            flops=4 * rows * rows * width,
            bytes_accessed=8 << 20,
            transcendentals=rows * rows * heads // 2,
        ),
        name="attend",
    )(*spans(begin, end, KEYS), q, k, v, seg_col)


def three_parts(values):
    first = values.astype(BF16)
    rest = values - first.astype(F32)
    second = rest.astype(BF16)
    return first, second, (rest - second.astype(F32)).astype(BF16)


def attend_back_kernel(
    core, low, high, q_ref, k_ref, v_ref, out_ref, own, other, lse, seg_col,
    dq_out, dk_out, dv_out, grad, qx, kx, vx, gx, dq, dk, dv, weights, slopes,
):
    rows, width = q_ref.shape
    heads = width // HEAD_DIM
    pairs = heads // 2
    lanes = 2 * HEAD_DIM
    per_core = own.shape[0]
    grad[rows_at(core[0], per_core), :] = own[...]
    grad[rows_at(1 - core[0], per_core), :] = other[...]
    source = lax.broadcasted_iota(jnp.int32, (24, heads * lanes), 0)
    lane = lax.broadcasted_iota(jnp.int32, (24, heads * lanes), 1)
    place = jnp.where(
        (source % 8 == lane // lanes)
        & (lane % HEAD_DIM == DOCS + source // 8)
        & ((lane % lanes) // HEAD_DIM != (lane // lanes) % 2),
        1.0,
        0.0,
    ).astype(BF16)
    picks = jnp.where(
        lax.broadcasted_iota(jnp.int32, (width, 8), 0) // HEAD_DIM
        == lax.broadcasted_iota(jnp.int32, (width, 8), 1),
        1.0,
        0.0,
    ).astype(BF16)
    for at in range(0, rows, PREPARE):
        part = pl.ds(at, PREPARE)
        for_queries, for_keys = same_document(seg_col[part, :], 3)
        ones = jnp.where(for_keys == 1.0, for_keys, jnp.zeros_like(for_keys))
        level = jnp.concatenate(
            [lse[:, part] * (-1.0 / SCALE2), jnp.zeros((8 - heads, PREPARE), F32)]
        )
        levels = dot_left(jnp.concatenate(three_parts(level)), place)
        both = grad[part, :].astype(F32) * out_ref[part, :].astype(F32)
        coarse = both.astype(BF16)
        fine = (both - coarse.astype(F32)).astype(BF16)
        delta = dot(coarse, picks) + dot(fine, picks)
        deltas = dot(jnp.concatenate(three_parts(-delta), 1), place).astype(BF16)
        for pair in range(pairs):
            cols = pl.ds(pair * lanes, lanes)
            sides = slice(2 * pair, 2 * pair + 2)
            one, two = [slice((2 * pair + e) * lanes, (2 * pair + e + 1) * lanes) for e in (0, 1)]
            marks = [(for_queries + levels[:, side]).astype(BF16) for side in (one, two)]
            qx[sides, part, :] = jnp.stack(widen(q_ref[part, cols], marks))
            kx[sides, part, :] = jnp.stack(widen(k_ref[part, cols], (for_keys, for_keys)))
            vx[sides, part, :] = jnp.stack(widen(v_ref[part, cols], (ones, ones)))
            gx[sides, part, :] = jnp.stack(widen(grad[part, cols], (deltas[:, one], deltas[:, two])))

    dq[...] = jnp.zeros_like(dq)

    @pl.loop(0, rows // BLOCK)
    def _(kb):
        k_rows = rows_at(kb, BLOCK)
        dk[...] = jnp.zeros_like(dk)
        dv[...] = jnp.zeros_like(dv)

        def step(qb, carry):
            q_rows = rows_at(qb, BLOCK)
            for h in range(heads):
                probs = jnp.exp2(dot_right(kx[h, k_rows, :], qx[h, q_rows, :]) * SCALE2)
                weights[h] = probs.astype(BF16)
                centred = dot_right(vx[h, k_rows, :], gx[h, q_rows, :])
                slopes[h] = (probs * centred).astype(BF16)
            for pair in range(pairs):
                cols = pl.ds(pair * lanes, lanes)
                slope = [slopes[2 * pair], slopes[2 * pair + 1]]
                weight = [weights[2 * pair], weights[2 * pair + 1]]
                dq[q_rows, cols] += dot_left(
                    jnp.concatenate(slope, 0), jnp.concatenate(halves(k_ref[k_rows, cols]), 0)
                )
                dk[:, cols] += dot(
                    jnp.concatenate(slope, 1), jnp.concatenate(halves(q_ref[q_rows, cols]), 0)
                )
                dv[:, cols] += dot(
                    jnp.concatenate(weight, 1), jnp.concatenate(halves(grad[q_rows, cols]), 0)
                )
            return carry

        lax.fori_loop(low[kb], high[kb], step, 0)
        dk_out[k_rows, :] = (dk[...] * SCALE).astype(BF16)
        dv_out[k_rows, :] = dv[...].astype(BF16)

    dq_out[...] = (dq[...] * SCALE).astype(BF16)


def attend_back(core, begin, end, q, k, v, out, own, other, lse, seg_col):
    rows, width = q.shape
    heads = width // HEAD_DIM
    whole = lambda shape: pl.BlockSpec(shape, lambda i, *_: (0,) * len(shape))
    wide = pltpu.VMEM((heads, rows, 2 * HEAD_DIM), BF16)
    return pl.pallas_call(
        attend_back_kernel,
        out_shape=[jax.ShapeDtypeStruct((rows, width), BF16)] * 3,
        grid_spec=pltpu.PrefetchScalarGridSpec(
            num_scalar_prefetch=3,
            grid=(1,),
            in_specs=[whole((rows, width))] * 4
            + [whole((rows // 2, width))] * 2
            + [whole((heads, rows)), whole((rows, 1))],
            out_specs=[whole((rows, width))] * 3,
            scratch_shapes=[
                pltpu.VMEM((rows, width), BF16),
                wide,
                wide,
                wide,
                wide,
                pltpu.VMEM((rows, width), F32),
                pltpu.VMEM((BLOCK, width), F32),
                pltpu.VMEM((BLOCK, width), F32),
                pltpu.VMEM((heads, BLOCK, BLOCK), BF16),
                pltpu.VMEM((heads, BLOCK, BLOCK), BF16),
            ],
        ),
        compiler_params=params(),
        cost_estimate=pl.CostEstimate(
            flops=10 * rows * rows * width,
            bytes_accessed=16 << 20,
            transcendentals=rows * rows * heads // 2,
        ),
        name="attend_back",
    )(core, *spans(begin, end, BLOCK), q, k, v, out, own, other, lse, seg_col)


def row_mean(values):
    return jnp.mean(values, axis=-1, keepdims=True)


def norm(values):
    centre = values - row_mean(values)
    scale = lax.rsqrt(row_mean(centre * centre) + EPS)
    return centre * scale, scale


def norm_back(normed, scale, gain, grad):
    inner = grad * gain
    return scale * (inner - row_mean(inner) - normed * row_mean(inner * normed))


def column_sum(values):
    return jnp.sum(values.astype(F32), axis=0, keepdims=True)


def rows_kernel(
    core, x_ref, mine, theirs, cot, wo_mine_ref, wo_theirs_ref, wide_ref, vectors, be,
    out, ga_mine, ga_theirs, residual, act, ge, low_out, gr_out, gb_out, sums, sum_e, slope,
):
    width = x_ref.shape[1]
    chunks = slope.shape[1] // width
    unit = width // UNITS
    each = UNITS // chunks
    we = lambda j: wide_ref[:, j, :unit, :].reshape(width, width)
    wr = lambda j: wide_ref[each * j : each * (j + 1), :, unit:, :].reshape(width, width)
    bo, br = vectors[0:1, :], vectors[1:2, :]
    gain1, shift1, gain2, shift2 = [vectors[n : n + 1, :] for n in range(2, 6)]
    wo_mine, wo_theirs = stacked(wo_mine_ref), stacked(wo_theirs_ref)

    @pl.when(pl.program_id(0) == 0)
    def _():
        sums[...] = jnp.zeros_like(sums)
        sum_e[...] = jnp.zeros_like(sum_e)

    branch = dot(mine[...], wo_mine) + dot(theirs[...], wo_theirs) + bo
    normed1, scale1 = norm(x_ref[...].astype(F32) + branch)
    first = normed1 * gain1 + shift1
    first_low = first.astype(BF16)
    low_out[...] = first_low
    reduced = jnp.zeros_like(first)
    for j in range(chunks):
        cols = slice(j * width, (j + 1) * width)
        u = dot(first_low, we(j)) + be[:, cols]
        square = u * u
        curve = jnp.tanh(GELU_A * (u + GELU_B * (square * u)))
        cdf = 0.5 * (1.0 + curve)
        slope[:, cols] = cdf + (0.5 * GELU_A) * u * (1.0 - curve * curve) * (
            1.0 + (3.0 * GELU_B) * square
        )
        activated = (u * cdf).astype(BF16)
        act[:, cols] = activated
        reduced += dot(activated, wr(j))
    normed2, scale2 = norm(first + (reduced + br))
    out[...] = (normed2 * gain2 + shift2).astype(BF16)

    incoming = cot[...].astype(F32)
    grad_second = norm_back(normed2, scale2, gain2, incoming)
    grad_reduced = grad_second.astype(BF16)
    gr_out[...] = grad_reduced
    grad_first = grad_second
    for j in range(chunks):
        cols = slice(j * width, (j + 1) * width)
        grad_expanded = (dot_right(grad_reduced, wr(j)) * slope[:, cols]).astype(BF16)
        ge[:, cols] = grad_expanded
        sum_e[:, cols] += column_sum(grad_expanded)
        grad_first += dot_right(grad_expanded, we(j))
    grad_residual = norm_back(normed1, scale1, gain1, grad_first)
    residual[...] = grad_residual
    grad_branch = grad_residual.astype(BF16)
    gb_out[...] = grad_branch
    ga_mine[...] = dot_right(grad_branch, wo_mine).astype(BF16)
    ga_theirs[...] = dot_right(grad_branch, wo_theirs).astype(BF16)
    sums[0:1, :] += column_sum(grad_branch)
    sums[1:2, :] += column_sum(grad_reduced)
    sums[2:3, :] += column_sum(grad_first * normed1)
    sums[3:4, :] += column_sum(grad_first)
    sums[4:5, :] += column_sum(incoming * normed2)
    sums[5:6, :] += column_sum(incoming)


def row_local(core, x, mine, theirs, cot, square, wide_all, vectors, be):
    rows, width = x.shape
    half, wide = width // 2, be.shape[1]
    side = lambda flip: pl.BlockSpec(
        (UNITS // 2, width // UNITS, width),
        lambda i, core: (core[0] ^ flip, 3, 0),
        pipeline_mode=pl.Buffered(1),
    )
    block = lambda cols: pl.BlockSpec((ROWS, cols), lambda i, *_: (i, 0))
    fixed = lambda a: pl.BlockSpec(
        a.shape, lambda i, *_: (0,) * a.ndim, pipeline_mode=pl.Buffered(1)
    )
    shape = lambda cols, kind: jax.ShapeDtypeStruct((rows, cols), kind)
    resident = lambda r, cols: pl.BlockSpec((r, cols), lambda i, *_: (0, 0))
    return pl.pallas_call(
        rows_kernel,
        out_shape=[
            shape(width, BF16),
            shape(half, BF16),
            shape(half, BF16),
            shape(width, F32),
            shape(wide, BF16),
            shape(wide, BF16),
            shape(width, BF16),
            shape(width, BF16),
            shape(width, BF16),
            jax.ShapeDtypeStruct((8, width), F32),
            jax.ShapeDtypeStruct((1, wide), F32),
        ],
        grid_spec=pltpu.PrefetchScalarGridSpec(
            num_scalar_prefetch=1,
            grid=(rows // ROWS,),
            in_specs=[
                block(width),
                block(half),
                block(half),
                block(width),
                side(0),
                side(1),
                fixed(wide_all),
                fixed(vectors),
                fixed(be),
            ],
            out_specs=[
                block(width),
                block(half),
                block(half),
                block(width),
                block(wide),
                block(wide),
                block(width),
                block(width),
                block(width),
                resident(8, width),
                resident(1, wide),
            ],
            scratch_shapes=[pltpu.VMEM((ROWS, wide), F32)],
        ),
        compiler_params=params(),
        cost_estimate=pl.CostEstimate(
            flops=2 * 2 * rows * width * (width + 2 * wide),
            bytes_accessed=40 << 20,
            transcendentals=rows * wide,
        ),
        name="row_local",
    )(core, x, mine, theirs, cot, square, square, wide_all, vectors, be)


def weight_grad_kernel(left, right, out):
    out[...] = dot_left(left[...], right[...]).astype(out.dtype)


def weight_grad(left, right, kind):
    rows, m = left.shape
    n = right.shape[1]
    tm, tn = min(m, 768), min(n, 768)
    return pl.pallas_call(
        weight_grad_kernel,
        out_shape=jax.ShapeDtypeStruct((m, n), kind),
        grid=(m // tm, n // tn),
        in_specs=[
            pl.BlockSpec((rows, tm), lambda i, j: (0, i)),
            pl.BlockSpec((rows, tn), lambda i, j: (0, j)),
        ],
        out_specs=pl.BlockSpec((tm, tn), lambda i, j: (i, j)),
        compiler_params=params(),
        cost_estimate=pl.CostEstimate(
            flops=2 * rows * m * n, bytes_accessed=16 << 20, transcendentals=0
        ),
        name="weight_grad",
    )(left, right)


def split_cores(core, both, axis):
    first, second = jnp.split(both, 2, axis=axis)
    keep = jnp.where(core == 0, first, second)
    send = jnp.where(core == 0, second, first)
    return keep.astype(BF16), send.astype(BF16)


def expand_grad_kernel(core, low, ge, keep, send):
    nz, unit = keep.shape[1], keep.shape[3]
    whole = dot_left(low[...], ge[...]).reshape(nz, 2, unit, -1)
    kept, sent = split_cores(core[0], whole, 1)
    keep[...] = kept.reshape(keep.shape)
    send[...] = sent.reshape(send.shape)


def reduce_grad_kernel(core, act, gr, keep_in, send_in, keep, send):
    unit = keep.shape[3]
    whole = dot_left(act[...], gr[...]).reshape(2, 4, unit, -1)
    kept, sent = split_cores(core[0], whole, 0)
    keep[...] = kept.reshape(keep.shape)
    send[...] = sent.reshape(send.shape)


def feed_grads(core, low, ge, act, gr):
    rows, width = low.shape
    wide = ge.shape[1]
    chunks = wide // width
    unit = width // 8
    shape = jax.ShapeDtypeStruct((4, 4, 2, unit, width), BF16)
    flops = 2 * rows * width * wide
    keep, send = pl.pallas_call(
        expand_grad_kernel,
        out_shape=[shape, shape],
        grid_spec=pltpu.PrefetchScalarGridSpec(
            num_scalar_prefetch=1,
            grid=(chunks,),
            in_specs=[
                pl.BlockSpec((rows, width), lambda i, *_: (0, 0)),
                pl.BlockSpec((rows, width), lambda i, *_: (0, i)),
            ],
            out_specs=[pl.BlockSpec((1, 4, 1, unit, width), lambda i, *_: (i, 0, 0, 0, 0))] * 2,
        ),
        compiler_params=params(),
        cost_estimate=pl.CostEstimate(flops=flops, bytes_accessed=14 << 20, transcendentals=0),
        name="expand_grad",
    )(core, low, ge)
    return pl.pallas_call(
        reduce_grad_kernel,
        out_shape=[shape, shape],
        grid_spec=pltpu.PrefetchScalarGridSpec(
            num_scalar_prefetch=1,
            grid=(chunks,),
            in_specs=[
                pl.BlockSpec((rows, width), lambda i, *_: (0, i)),
                pl.BlockSpec((rows, width), lambda i, *_: (0, 0)),
                pl.BlockSpec(memory_space=pl.ANY),
                pl.BlockSpec(memory_space=pl.ANY),
            ],
            out_specs=[pl.BlockSpec((4, 1, 1, unit, width), lambda i, *_: (0, i, 1, 0, 0))] * 2,
        ),
        input_output_aliases={3: 0, 4: 1},
        compiler_params=params(),
        cost_estimate=pl.CostEstimate(flops=flops, bytes_accessed=14 << 20, transcendentals=0),
        name="reduce_grad",
    )(core, act, gr, keep, send)


def output_grad_kernel(core, mine, theirs, gb, keep, send):
    nz, unit = keep.shape[:2]
    from_mine, from_theirs = dot_left(mine[...], gb[...]), dot_left(theirs[...], gb[...])
    first = jnp.where(core[0] == 0, from_mine, from_theirs)
    second = jnp.where(core[0] == 0, from_theirs, from_mine)
    whole = jnp.concatenate([first, second]).reshape(nz, 2, unit, -1)
    kept, sent = split_cores(core[0], whole, 1)
    keep[...] = kept.reshape(keep.shape)
    send[...] = sent.reshape(send.shape)


def output_grad(core, mine, theirs, gb):
    rows = mine.shape[0]
    width = gb.shape[1]
    shape = jax.ShapeDtypeStruct((4, width // 8, width), BF16)
    whole = lambda a: pl.BlockSpec(a.shape, lambda i, *_: (0,) * a.ndim)
    return pl.pallas_call(
        output_grad_kernel,
        out_shape=[shape, shape],
        grid_spec=pltpu.PrefetchScalarGridSpec(
            num_scalar_prefetch=1,
            grid=(1,),
            in_specs=[whole(mine), whole(theirs), whole(gb)],
            out_specs=[whole(shape)] * 2,
        ),
        compiler_params=params(),
        cost_estimate=pl.CostEstimate(
            flops=2 * rows * width * width, bytes_accessed=5 << 20, transcendentals=0
        ),
        name="output_grad",
    )(core, mine, theirs, gb)


def packed_input_grad_kernel(
    core, own, other, d_ref, w_ref, keep, send, sums, dx_own, dx_other
):
    part = pl.program_id(0)
    rows = own.shape[0]
    nz, unit = keep.shape[1], keep.shape[2]
    mine = pl.multiple_of(core[0] * rows, rows)
    theirs = pl.multiple_of((1 - core[0]) * rows, rows)
    d_own, d_other = d_ref[0, pl.ds(mine, rows), :], d_ref[0, pl.ds(theirs, rows), :]
    whole = (dot_left(own[...], d_own) + dot_left(other[...], d_other)).reshape(nz, 2, unit, -1)
    kept, sent = split_cores(core[0], whole, 1)
    keep[...] = kept.reshape(keep.shape)
    send[...] = sent.reshape(send.shape)
    sums[0] = jnp.broadcast_to(column_sum(d_own) + column_sum(d_other), sums.shape[1:])
    to_own, to_other = dot_right(d_own, stacked(w_ref)), dot_right(d_other, stacked(w_ref))

    @pl.when(part == 0)
    def _():
        dx_own[...] = to_own
        dx_other[...] = to_other

    @pl.when(part > 0)
    def _():
        dx_own[...] += to_own
        dx_other[...] += to_other


def packed_input_grad(core, own, other, grads, weights):
    rows, width = own.shape
    half = width // 2
    unit = width // 8
    shape = jax.ShapeDtypeStruct((3, 4, unit, half), BF16)
    whole = lambda shape: pl.BlockSpec(shape, lambda i, *_: (0,) * len(shape))
    packed = pl.BlockSpec((1, 4, unit, half), lambda i, core: (i, 0, 0, 0))
    return pl.pallas_call(
        packed_input_grad_kernel,
        out_shape=[
            shape,
            shape,
            jax.ShapeDtypeStruct((3, 8, half), F32),
            jax.ShapeDtypeStruct((rows, width), F32),
            jax.ShapeDtypeStruct((rows, width), F32),
        ],
        grid_spec=pltpu.PrefetchScalarGridSpec(
            num_scalar_prefetch=1,
            grid=(3,),
            in_specs=[
                whole((rows, width)),
                whole((rows, width)),
                pl.BlockSpec((1, 2 * rows, half), lambda i, core: (i, 0, 0)),
                pl.BlockSpec((UNITS, width // UNITS, half), lambda i, core: (0, i, core[0])),
            ],
            out_specs=[
                packed,
                packed,
                pl.BlockSpec((1, 8, half), lambda i, core: (i, 0, 0)),
                whole((rows, width)),
                whole((rows, width)),
            ],
        ),
        compiler_params=params(),
        cost_estimate=pl.CostEstimate(
            flops=2 * 2 * 2 * rows * width * 3 * half, bytes_accessed=20 << 20, transcendentals=0
        ),
        name="input_grad",
    )(core, own, other, grads, weights)


def input_grad_kernel(core, own, other, d_ref, w_ref, dw, sums, dx_own, dx_other):
    part = pl.program_id(0)
    rows = own.shape[0]
    mine = pl.multiple_of(core[0] * rows, rows)
    theirs = pl.multiple_of((1 - core[0]) * rows, rows)
    d_own, d_other = d_ref[0, pl.ds(mine, rows), :], d_ref[0, pl.ds(theirs, rows), :]
    dw[0] = (dot_left(own[...], d_own) + dot_left(other[...], d_other)).astype(dw.dtype)
    sums[0] = jnp.broadcast_to(column_sum(d_own) + column_sum(d_other), sums.shape[1:])
    to_own, to_other = dot_right(d_own, stacked(w_ref)), dot_right(d_other, stacked(w_ref))

    @pl.when(part == 0)
    def _():
        dx_own[...] = to_own
        dx_other[...] = to_other

    @pl.when(part > 0)
    def _():
        dx_own[...] += to_own
        dx_other[...] += to_other


def input_grad(core, own, other, grads, weights, kind):
    rows, width = own.shape
    half = width // 2
    whole = lambda shape: pl.BlockSpec(shape, lambda i, *_: (0,) * len(shape))
    return pl.pallas_call(
        input_grad_kernel,
        out_shape=[
            jax.ShapeDtypeStruct((3, width, half), kind),
            jax.ShapeDtypeStruct((3, 8, half), F32),
            jax.ShapeDtypeStruct((rows, width), F32),
            jax.ShapeDtypeStruct((rows, width), F32),
        ],
        grid_spec=pltpu.PrefetchScalarGridSpec(
            num_scalar_prefetch=1,
            grid=(3,),
            in_specs=[
                whole((rows, width)),
                whole((rows, width)),
                pl.BlockSpec((1, 2 * rows, half), lambda i, core: (i, 0, 0)),
                pl.BlockSpec((UNITS, width // UNITS, half), lambda i, core: (0, i, core[0])),
            ],
            out_specs=[
                pl.BlockSpec((1, width, half), lambda i, core: (i, 0, 0)),
                pl.BlockSpec((1, 8, half), lambda i, core: (i, 0, 0)),
                whole((rows, width)),
                whole((rows, width)),
            ],
        ),
        compiler_params=params(),
        cost_estimate=pl.CostEstimate(
            flops=2 * 2 * 2 * rows * width * 3 * half, bytes_accessed=20 << 20, transcendentals=0
        ),
        name="input_grad",
    )(core, own, other, grads, weights)


def local(tokens, segment_ids, cotangent, *shards):
    rep_size, shard_size = lax.axis_size("rep"), lax.axis_size("shard")
    rep, shard = lax.axis_index("rep"), lax.axis_index("shard")
    core = shard % 2
    core_arg = core.reshape(1).astype(jnp.int32)
    width = tokens.shape[2]
    half = width // 2
    both = ("rep", "shard")

    def flat(r, s):
        return r * shard_size + s

    def route(k, back=False):
        pairs = []
        for r in range(rep_size):
            for s in range(shard_size):
                there = (flat(r, s), flat(2 * (s % 2) + (r + k) % 2, s - s % 2 + r // 2))
                pairs.append(there[::-1] if back else there)
        return pairs

    swap_pairs = [(flat(r, s), flat(r, s ^ 1)) for r in range(rep_size) for s in range(shard_size)]

    def swap(array):
        return lax.ppermute(array, both, swap_pairs)

    odd = rep % 2

    def to_sequences(array):
        a, b = array[0], array[1]
        even_part = lax.ppermute(jnp.where(odd == 0, a, b), both, route(0))
        odd_part = lax.ppermute(jnp.where(odd == 0, b, a), both, route(1))
        return jnp.concatenate(
            [jnp.where(odd == 0, even_part, odd_part), jnp.where(odd == 0, odd_part, even_part)]
        )

    def from_sequences(array):
        rows = array.shape[0] // 2
        a, b = array[:rows], array[rows:]
        even_part = lax.ppermute(jnp.where(odd == 0, a, b), both, route(0, True))
        odd_part = lax.ppermute(jnp.where(odd == 0, b, a), both, route(1, True))
        return jnp.stack(
            [jnp.where(odd == 0, even_part, odd_part), jnp.where(odd == 0, odd_part, even_part)]
        )

    tuned = rep_size == 4 and shard_size == UNITS
    rows_at = width // UNITS
    chunks = shards[4].shape[1] // width
    small = jnp.concatenate(shards[6:])
    if tuned:
        small_rows = jnp.concatenate([small, jnp.zeros((EXTRA * width - small.shape[0],), BF16)])
        square_own = jnp.concatenate(list(shards[:4]) + [small_rows.reshape(EXTRA, width)])
        wide_own = jnp.concatenate(
            [
                shards[4].reshape(rows_at, chunks, width).transpose(1, 0, 2),
                shards[5].reshape(chunks, rows_at, width),
            ],
            axis=1,
        )
        square, wide_all = gather_weights(square_own, wide_own, shard_size // 2)
        small = square[:, 4 * rows_at :, :].reshape(shard_size, EXTRA * width)
    else:
        wq, wk, wv, wo, we, wr = [lax.all_gather(m, "shard", axis=0, tiled=True) for m in shards[:6]]
        square = jnp.concatenate(
            [m.reshape(UNITS, rows_at, width) for m in (wq, wk, wv, wo)]
            + [jnp.zeros((UNITS, EXTRA, width), BF16)],
            axis=1,
        )
        wide_all = jnp.concatenate(
            [
                we.reshape(UNITS, rows_at, chunks, width).transpose(0, 2, 1, 3),
                wr.reshape(UNITS, chunks, rows_at, width),
            ],
            axis=2,
        )
        small = lax.all_gather(small[None], "shard", axis=0, tiled=True)
    vectors, at = [], 0
    for member in shards[6:]:
        n = member.shape[0]
        vectors.append(small[:, at : at + n].reshape(1, n * shard_size).astype(F32))
        at += n
    bq, bv, bo, be, br, gain1, shift1, gain2, shift2 = vectors

    own = to_sequences(tokens)
    cot = to_sequences(cotangent)
    other = swap(own)
    swapped_ids = swap(segment_ids)
    ids = jnp.where(rep // 2 == core, segment_ids, swapped_ids)
    segments = lax.dynamic_index_in_dim(ids, odd, 0, keepdims=False)
    blocks = segments.reshape(-1, BLOCK)
    begin = jnp.sum((segments[None, :] < blocks[:, :1]).astype(jnp.int32), axis=1)
    end = jnp.sum((segments[None, :] <= blocks[:, -1:]).astype(jnp.int32), axis=1)
    seg_col = segments[:, None]

    q, k, v = project(core_arg, own, other, square, bq, bv)
    attended, lse = attend(begin, end, q, k, v, seg_col)
    rows = own.shape[0]
    mine = lax.dynamic_slice_in_dim(attended, core * rows, rows)
    theirs = swap(lax.dynamic_slice_in_dim(attended, (1 - core) * rows, rows))
    table = jnp.concatenate([bo, br, gain1, shift1, gain2, shift2, bo, bo])
    out, ga_mine, ga_theirs, residual, act, ge, first_low, gr, gb, sums, sum_e = row_local(
        core_arg, own, mine, theirs, cot, square, wide_all, table, be
    )
    ga_other = swap(ga_theirs)
    if not tuned:
        dwr = weight_grad(act, gr, F32)
        dwe = weight_grad(first_low, ge, F32)
        dwo_mine, dwo_theirs = weight_grad(mine, gb, F32), weight_grad(theirs, gb, F32)
        dq, dk, dv = attend_back(
            core_arg, begin, end, q, k, v, attended, ga_mine, ga_other, lse, seg_col
        )
        dw, sum_qkv, dx_own, dx_other = input_grad(
            core_arg, own, other, jnp.stack([dq, dk, dv]), square, F32
        )
        dx = (residual + dx_own + swap(dx_other.astype(BF16)).astype(F32)).astype(BF16)

        def place(part, dim):
            zero = jnp.zeros_like(part)
            return jnp.where(
                core == 0,
                jnp.concatenate([part, zero], axis=dim),
                jnp.concatenate([zero, part], axis=dim),
            )

        dwo = jnp.where(
            core == 0,
            jnp.concatenate([dwo_mine, dwo_theirs]),
            jnp.concatenate([dwo_theirs, dwo_mine]),
        )
        totals = (
            place(dw[0], 1),
            place(dw[1], 1),
            place(dw[2], 1),
            dwo,
            dwe,
            dwr,
            place(sum_qkv[0, 0], 0),
            place(sum_qkv[2, 0], 0),
            sums[0],
            sum_e[0],
            sums[1],
            sums[2],
            sums[3],
            sums[4],
            sums[5],
        )
        summed = lax.psum_scatter(totals, "shard", scatter_dimension=0, tiled=True)
        final = [part.astype(F32) for part in lax.psum([p.astype(BF16) for p in summed], "rep")]
        return (from_sequences(out), from_sequences(dx)) + tuple(final)

    z = shard // 2
    nz = shard_size // 2

    def plane_send(array, k):
        pairs = [(flat(r, s), flat(r ^ k, s)) for r in range(4) for s in range(shard_size)]
        return lax.ppermute(array, both, pairs)

    def line_send(array, k):
        pairs = [(flat(r, s), flat(r, s ^ (2 * k))) for r in range(4) for s in range(shard_size)]
        return lax.ppermute(array, both, pairs)

    def pick(array, n):
        return lax.dynamic_index_in_dim(array, n, 0, keepdims=False)

    def scatter_plane(pieces):
        got = [plane_send(pieces(rep ^ k).astype(BF16), k) for k in (1, 2, 3)]
        total = pieces(rep)
        for part in got:
            total = total + part.astype(F32)
        return total

    def scatter_line(array):
        got = [line_send(pick(array, z ^ k).astype(BF16), k) for k in range(1, nz)]
        total = pick(array, z)
        for part in got:
            total = total + part.astype(F32)
        return total

    def gather_plane(part):
        got = [part] + [plane_send(part, k) for k in (1, 2, 3)]
        result = jnp.zeros((4,) + part.shape, part.dtype)
        for k in range(4):
            result = lax.dynamic_update_index_in_dim(result, got[k], rep ^ k, 0)
        return result.astype(F32)

    feed_keep, feed_send = feed_grads(core_arg, first_low, ge, act, gr)
    wo_keep, wo_send = output_grad(core_arg, mine, theirs, gb)
    feed_got = swap(feed_send)
    wo_got = swap(wo_send)
    feed_parts = [
        pick(feed_keep, rep ^ hop).astype(F32) + pick(feed_got, rep ^ hop).astype(F32)
        for hop in range(4)
    ]
    feed_sent = [part.astype(BF16) for part in feed_parts[1:]]
    feed_sent, ga_other = lax.optimization_barrier((feed_sent, ga_other))
    feed = feed_parts[0]
    for hop in (1, 2, 3):
        feed = feed + plane_send(feed_sent[hop - 1], hop).astype(F32)
    dq, dk, dv = attend_back(
        core_arg, begin, end, q, k, v, attended, ga_mine, ga_other, lse, seg_col
    )
    line_sent = [pick(feed, z ^ hop).astype(BF16) for hop in range(1, nz)]
    line_sent, dq = lax.optimization_barrier((line_sent, dq))
    feed = pick(feed, z)
    for hop in range(1, nz):
        feed = feed + line_send(line_sent[hop - 1], hop).astype(F32)
    feed = feed.astype(BF16)
    qkv_keep, qkv_send, sum_qkv, dx_own, dx_other = packed_input_grad(
        core_arg, own, other, jnp.stack([dq, dk, dv]), square
    )
    dx = (residual + dx_own + swap(dx_other.astype(BF16)).astype(F32)).astype(BF16)
    qkv_got = swap(qkv_send)
    qkv = jnp.where(
        core == 0,
        jnp.concatenate([qkv_keep, qkv_got], axis=3),
        jnp.concatenate([qkv_got, qkv_keep], axis=3),
    )
    unit = width // shard_size
    wide_unit = sum_e.shape[1] // shard_size

    def place(part):
        zero = jnp.zeros_like(part)
        return jnp.where(
            core == 0, jnp.concatenate([part, zero]), jnp.concatenate([zero, part])
        )

    rows_of = [place(sum_qkv[0, 0]), place(sum_qkv[2, 0])] + [sums[n] for n in range(6)]
    table = jnp.concatenate(
        [vector.reshape(shard_size, unit) for vector in rows_of]
        + [
            sum_e.reshape(shard_size, wide_unit),
            jnp.zeros((shard_size, 2 * width - 8 * unit - wide_unit), F32),
        ],
        axis=1,
    ).reshape(nz, 2, 2, width)
    mine_table = lax.dynamic_index_in_dim(table, core, 1, keepdims=False)
    other_table = lax.dynamic_index_in_dim(table, 1 - core, 1, keepdims=False)
    mine_table = mine_table + swap(other_table)
    wo_sum = wo_keep.astype(F32) + wo_got.astype(F32)
    fourth = jnp.concatenate([wo_sum, mine_table, jnp.zeros((nz, 6, width), F32)], axis=1)
    rest = jnp.concatenate(
        [
            jnp.concatenate([qkv, jnp.zeros((3, nz, 8, width), BF16)], axis=2),
            fourth.astype(BF16)[None],
        ]
    )
    rest = scatter_line(scatter_plane(lambda n: pick(rest, n).astype(F32))).astype(BF16)
    result = gather_plane(jnp.concatenate([feed.reshape(2 * unit, width), rest]))
    dwe = result[:, :unit].transpose(1, 0, 2).reshape(unit, 4 * width)
    dwr = result[:, unit : 2 * unit].reshape(4 * unit, width)
    dwq, dwk, dwv, dwo = [result[n, 2 * unit : 3 * unit] for n in range(4)]
    small = result[3, 3 * unit : 3 * unit + 2].reshape(-1)
    dbq, dbv, dbo, dbr, dg1, ds1, dg2, ds2 = [small[n * unit : (n + 1) * unit] for n in range(8)]
    dbe = small[8 * unit : 8 * unit + wide_unit]
    return (
        from_sequences(out),
        from_sequences(dx),
        dwq,
        dwk,
        dwv,
        dwo,
        dwe,
        dwr,
        dbq,
        dbv,
        dbo,
        dbe,
        dbr,
        dg1,
        ds1,
        dg2,
        ds2,
    )


def solution(mesh):
    row = P("shard", "rep", None)
    in_specs = (row, P("shard", None), row) + (P("shard", None),) * 6 + (P("shard"),) * 9
    out_specs = (row, row) + (P("shard", None),) * 6 + (P("shard"),) * 9
    return jax.shard_map(local, mesh=mesh, in_specs=in_specs, out_specs=out_specs, check_vma=False)
```

time: 778 us -> 446 us (0.57)
  waiting for transfers between devices: 388 us -> 56 us
  blocking collectives: 54.8 us -> 0 us
  starting transfers between devices: 34.6 us -> 66.2 us
  Pallas kernels: 216 us -> 246 us
  local copies, waits for them, and re-layouts: 14.9 us -> 33.8 us
  other arithmetic: 54.2 us -> 36.2 us
  between operations: 15.6 us -> 1.79 us
    reduce_scatter x6 -> x0, waiting for transfers between devices: 265 us -> none  [local(): summed = lax.psum_scatter(totals, 'shard', scatter_dimension=0, tiled=True)]
    all_gather x6 -> x0, waiting for transfers between devices: 77.3 us -> none  [local(): lax.all_gather(m, 'shard', axis=0, tiled=True)]
    pallas_call x5, Pallas kernels: 45.1 us -> 111 us  [the longest x1 70.7 us: gather_weights(): pl.pallas_call(functools.partial(gather_kernel, nz), out_shape=[jax.Shape...]
    ppermute x0 -> x15, waiting for transfers between devices: none -> 50.2 us  [the longest x9 36.6 us: plane_send(): return lax.ppermute(array, both, pairs)]
    ppermute x0 -> x15, starting transfers between devices: none -> 34.7 us  [the longest x6 20.7 us: line_send(): return lax.ppermute(array, both, pairs)]
    unnamed x1 -> x0, blocking collectives: 28.8 us -> none
    pallas_call x1, Pallas kernels: 57.2 us -> 31.6 us  [attend(): pl.pallas_call(attend_kernel, out_shape=[jax.ShapeDtypeStruct((rows, widt...]
    psum x1 -> x0, waiting for transfers between devices: 25.4 us -> none  [local(): lax.psum([p.astype(BF16) for p in summed], 'rep')]
  transfers between devices with their start and end apart: 26 -> 32, of which waited for: 9 -> 9; matrix products, arithmetic and copies ran while one was open for 8% -> 14% of each run, Pallas kernels for 23% -> 43%
where the time goes in v2:
time: 446 us; the launch traced here: 440 us
  Pallas kernels  246 us (55%)
  starting transfers between devices  66.2 us (15%)
  waiting for transfers between devices  56 us (13%)
  other arithmetic  36.2 us (8%)
  local copies, waits for them, and re-layouts  33.8 us (8%)
    pallas_call x1, Pallas kernels, gather_weights(): pl.pallas_call(functools.partial(gather_kernel, nz), out_shape=[jax.Shape...  70.7 us
    pallas_call x1, Pallas kernels, attend_back(): pl.pallas_call(attend_back_kernel, out_shape=[jax.ShapeDtypeStruct((rows,...  53.7 us
    pallas_call x1, Pallas kernels, row_local(): pl.pallas_call(rows_kernel, out_shape=[shape(width, BF16), shape(half, BF...  39.6 us
    ppermute x9, waiting for transfers between devices, plane_send(): return lax.ppermute(array, both, pairs)  36.6 us
    pallas_call x1, Pallas kernels, attend(): pl.pallas_call(attend_kernel, out_shape=[jax.ShapeDtypeStruct((rows, widt...  31.6 us
    ppermute x6, starting transfers between devices, line_send(): return lax.ppermute(array, both, pairs)  20.7 us
    pallas_call x1, Pallas kernels, packed_input_grad(): pl.pallas_call(packed_input_grad_kernel, out_shape=[shape, shape, jax.Sha...  17.6 us
    ppermute x9, starting transfers between devices, plane_send(): return lax.ppermute(array, both, pairs)  14 us
  transfers between devices with their start and end apart: 32, of which 9 were waited for; matrix products, arithmetic and copies ran while one was open for 14% of the time, Pallas kernels for 43%

profile of v2, /device:TPU:0, one launch (start us, length us, event | category | flops | bytes accessed | tf_op | source)
XLA Modules:
  0.0 440.2 jit_solution(14446772847822745497)
XLA Ops:
  0.7 2.5 select_bitcast_fusion.7
  3.2 1.9 collective-permute-start
  5.2 2.9 collective-permute-start.1
  10.7 7.4 %collective-permute-start.5 = (bf16[512,768]{1,0:T(8,128)(2,1)}, bf16[512,768]{1,0:T(8,128)(2,1)}, u32[]{:S(2)}, u32[]{:S(2)}) collective-permute-start(bf16[512,768]{1,0:T(8,128)(2,1)} %get-tuple-element.134), channel_id=1, source_target_pairs={{0,0},{1,16},{2,2},{3,18},{4,4},{5,20},{6,6},{7,22},{8,8},{9,24},{... | collective-permute-start | bytes 2359304 | tf_op jit(solution)/shard_map/ppermute | solution.py:940
  20.7 4.8 %collective-permute-done.1 = bf16[512,768]{1,0:T(8,128)(2,1)} collective-permute-done((bf16[512,768]{1,0:T(8,128)(2,1)S(1)}, bf16[512,768]{1,0:T(8,128)(2,1)}, u32[]{:S(2)}, u32[]{:S(2)}) %collective-permute-start.1) | collective-permute-done | bytes 786464 | tf_op jit(solution)/shard_map/ppermute | solution.py:941
  26.9 3.9 collective-permute-start.3
  34.6 70.7 %gather_weights.1 = (bf16[8,392,768]{2,1,0:T(8,128)(2,1)}, bf16[8,4,192,768]{3,2,1,0:T(8,128)(2,1)}) custom-call(bf16[392,768]{1,0:T(8,128)(2,1)} %constant_dynamic-update-slice_fusion.square, bf16[4,192,768]{2,1,0:T(8,128)(2,1)} %pad_maximum_fusion.5.wide), custom_call_target="tpu_custom_call" | custom-call | bytes 157286400 | tf_op jit(solution)/shard_map/gather_weights/pallas_call | solution.py:187
  112.3 9.8 %project.1 = (bf16[2048,384]{1,0:T(8,128)(2,1)}, bf16[2048,384]{1,0:T(8,128)(2,1)}, bf16[2048,384]{1,0:T(8,128)(2,1)}) custom-call(s32[1]{0:T(128)} %bitcast.core, bf16[1024,768]{1,0:T(8,128)(2,1)} %copy-done.1, bf16[1024,768]{1,0:T(8,128)(2,1)} %copy-done.6, bf16[8,392,768]{2,1,0:T(8,128)(2,1)} %get-tuple-element.57.wq.wk.wv.wo_mine_ref.wo_theirs_ref.w_ref, ...), custom_call_target="tpu_custom_call" | custom-call | flops 3623878656 | bytes 10485760 | tf_op jit(solution)/shard_map/project/pallas_call | solution.py:238
  122.1 31.6 %attend.1 = (bf16[2048,384]{1,0:T(8,128)(2,1)}, f32[6,2048]{1,0:T(8,128)}) custom-call(s32[8]{0:T(128)} %get-tuple-element.165.low, s32[8]{0:T(128)} %get-tuple-element.162.high, bf16[2048,384]{1,0:T(8,128)(2,1)} %get-tuple-element.58.q_ref, bf16[2048,384]{1,0:T(8,128)(2,1)} %get-tuple-element.59.k_ref, bf16[2048,384]{1,0:T(8,128)(2,1)} %get-tuple-element.60.v_ref, ...), custom_call_target="tpu_custom_call" | custom-call | flops 6442450944 | bytes 8388608 | tf_op jit(solution)/shard_map/attend/pallas_call | solution.py:348
  153.7 2.4 constant_dynamic-slice_fusion
  162.0 39.6 %row_local.1 = (bf16[1024,768]{1,0:T(8,128)(2,1)}, bf16[1024,384]{1,0:T(8,128)(2,1)}, bf16[1024,384]{1,0:T(8,128)(2,1)}, f32[1024,768]{1,0:T(8,128)}, bf16[1024,...) custom-call(s32[1]{0:T(128)} %bitcast.core, ...), custom_call_target="tpu_custom_call" | custom-call | flops 21743271936 | bytes 41943040 | tf_op jit(solution)/shard_map/row_local/pallas_call | solution.py:607
  201.6 9.5 %expand_grad.1 = (bf16[4,4,2,96,768]{4,3,2,1,0:T(8,128)(2,1)}, bf16[4,4,2,96,768]{4,3,2,1,0:T(8,128)(2,1)}) custom-call(s32[1]{0:T(128)} %bitcast.core, bf16[1024,768]{1,0:T(8,128)(2,1)} %get-tuple-element.67.low, bf16[1024,3072]{1,0:T(8,128)(2,1)} %get-tuple-element.68.ge), custom_call_target="tpu_custom_call" | custom-call | flops 4831838208 | bytes 14680064 | tf_op jit(solution)/shard_map/expand_grad/pallas_call | solution.py:716
  211.0 9.2 %reduce_grad.1 = (bf16[4,4,2,96,768]{4,3,2,1,0:T(8,128)(2,1)}, bf16[4,4,2,96,768]{4,3,2,1,0:T(8,128)(2,1)}) custom-call(s32[1]{0:T(128)} %bitcast.core, bf16[1024,3072]{1,0:T(8,128)(2,1)} %get-tuple-element.65.act, bf16[1024,768]{1,0:T(8,128)(2,1)} %get-tuple-element.66.gr, ...), custom_call_target="tpu_custom_call", output_to_operand_aliasing={{0}: (3, {}), {1}: (4, {})} | custom-call | flops 4831838208 | bytes 14680064 | tf_op jit(solution)/shard_map/reduce_grad/pallas_call | solution.py:732
  221.4 4.5 %output_grad.1 = (bf16[4,96,768]{2,1,0:T(8,128)(2,1)}, bf16[4,96,768]{2,1,0:T(8,128)(2,1)}) custom-call(s32[1]{0:T(128)} %bitcast.core, bf16[1024,384]{1,0:T(8,128)(2,1)} %get-tuple-element.137.mine, bf16[1024,384]{1,0:T(8,128)(2,1)} %copy-done.42, bf16[1024,768]{1,0:T(8,128)(2,1)} %get-tuple-element.91.gb), custom_call_target="tpu_custom_call" | custom-call | flops 1207959552 | bytes 5242880 | tf_op jit(solution)/shard_map/output_grad/pallas_call | solution.py:769
  233.1 7.4 %collective-permute-start.7 = (bf16[512,768]{1,0:T(8,128)(2,1)}, bf16[512,768]{1,0:T(8,128)(2,1)}, u32[]{:S(2)}, u32[]{:S(2)}) collective-permute-start(bf16[512,768]{1,0:T(8,128)(2,1)} %get-tuple-element.130), channel_id=1, source_target_pairs={{0,0},{16,1},{2,2},{18,3},{4,4},{20,5},{6,6},{22,7},{8,8},{24,9},{... | collective-permute-start | bytes 2359304 | tf_op jit(solution)/shard_map/ppermute | solution.py:949
  240.5 5.2 %fusion.8 = (bf16[4,2,96,768]{3,2,1,0:T(8,128)(2,1)S(1)}, bf16[4,2,96,768]{3,2,1,0:T(8,128)(2,1)S(1)}, bf16[4,2,96,768]{3,2,1,0:T(8,128)(2,1)}) fusion(bf16[4,4,2,96,768]{4,3,2,1,0:T(8,128)(2,1)} %collective-permute-done.9, s32[]{:T(128)S(6)} %select_n.235, bf16[4,4,2,96,768]{4,3,2,1,0:T(8,128)(2,1)} %get-tuple-element.71, s32[]{:T(128)S(6)} %select_n.234, ...), kind=kLoop, calls=%fused_computation.21 | loop fusion | flops 7077888 | bytes 10616844 | tf_op jit(solution)/shard_map/convert_element_type | solution.py:1103
  248.2 2.0 collective-permute-start.13
  250.2 53.7 %attend_back.1 = (bf16[2048,384]{1,0:T(8,128)(2,1)}, bf16[2048,384]{1,0:T(8,128)(2,1)}, bf16[2048,384]{1,0:T(8,128)(2,1)}) custom-call(s32[1]{0:T(128)} %bitcast.core, s32[8]{0:T(128)} %get-tuple-element.166.low, s32[8]{0:T(128)} %get-tuple-element.161.high, bf16[2048,384]{1,0:T(8,128)(2,1)} %get-tuple-element.58.q_ref, ...), custom_call_target="tpu_custom_call" | custom-call | flops 16106127360 | bytes 16777216 | tf_op jit(solution)/shard_map/attend_back/pallas_call | solution.py:476
  305.4 3.2 fusion.3
  311.8 2.5 pad_maximum_fusion.d_ref
  314.3 17.6 %input_grad.1 = (bf16[3,4,96,384]{3,2,1,0:T(8,128)(2,1)}, bf16[3,4,96,384]{3,2,1,0:T(8,128)(2,1)}, f32[3,8,384]{2,1,0:T(8,128)}, f32[1024,768]{1,0:T(8,128)}, f32[1024,768]{1,0:T(8,128)}) custom-call(s32[1]{0:T(128)} %bitcast.core, bf16[1024,768]{1,0:T(8,128)(2,1)} %copy-done.1, bf16[1024,768]{1,0:T(8,128)(2,1)} %copy-done.6, ...), custom_call_target="tpu_custom_call" | custom-call | flops 7247757312 | bytes 20971520 | tf_op jit(solution)/shard_map/input_grad/pallas_call | solution.py:820
  332.0 2.0 collective-permute-start.20
  346.4 9.8 %collective-permute-done.23 = bf16[4,104,768]{2,1,0:T(8,128)(2,1)S(1)} collective-permute-done((bf16[4,104,768]{2,1,0:T(8,128)(2,1)}, bf16[4,104,768]{2,1,0:T(8,128)(2,1)S(1)}, u32[]{:S(2)}, u32[]{:S(2)}) %collective-permute-start.23) | collective-permute-done | bytes 639008 | tf_op jit(solution)/shard_map/ppermute | solution.py:1065
  356.2 16.3 %collective-permute-start.19 = (bf16[2,96,768]{2,1,0:T(8,128)(2,1)S(1)}, bf16[2,96,768]{2,1,0:T(8,128)(2,1)S(1)}, u32[]{:S(2)}, u32[]{:S(2)}) collective-permute-start(bf16[2,96,768]{2,1,0:T(8,128)(2,1)S(1)} %copy-done.15), channel_id=1, source_target_pairs={{0,6},{1,7},{2,4},{3,5},{4,2},{5,3},{6,0},{7,1},{8,14},{9,15},{10,... | collective-permute-start | bytes 884744 | tf_op jit(solution)/shard_map/ppermute | solution.py:1069
  375.0 3.8 collective-permute-start.28
  383.4 10.2 %collective-permute-done.27 = bf16[104,768]{1,0:T(8,128)(2,1)S(1)} collective-permute-done((bf16[104,768]{1,0:T(8,128)(2,1)S(1)}, bf16[104,768]{1,0:T(8,128)(2,1)S(1)}, u32[]{:S(2)}, u32[]{:S(2)}) %collective-permute-start.27) | collective-permute-done | bytes 159776 | tf_op jit(solution)/shard_map/ppermute | solution.py:1069
  395.3 2.1 add_convert_fusion
  398.9 5.3 %collective-permute-start.31 = (bf16[296,768]{1,0:T(8,128)(2,1)S(1)}, bf16[296,768]{1,0:T(8,128)(2,1)S(1)}, u32[]{:S(2)}, u32[]{:S(2)}) collective-permute-start(bf16[296,768]{1,0:T(8,128)(2,1)S(1)} %pad_maximum_fusion.6), channel_id=1, source_target_pairs={{0,24},{1,25},{2,26},{3,27},{4,28},{5,29},{6,30},{7,31},{8,16},{9,... | collective-permute-start | bytes 1363976 | tf_op jit(solution)/shard_map/ppermute | solution.py:1065
  404.4 2.7 collective-permute-done.29
  407.2 5.1 %collective-permute-done.30 = bf16[296,768]{1,0:T(8,128)(2,1)S(1)} collective-permute-done((bf16[296,768]{1,0:T(8,128)(2,1)S(1)}, bf16[296,768]{1,0:T(8,128)(2,1)S(1)}, u32[]{:S(2)}, u32[]{:S(2)}) %collective-permute-start.30) | collective-permute-done | bytes 454688 | tf_op jit(solution)/shard_map/ppermute | solution.py:1065
  412.3 18.9 %collective-permute-done.31 = bf16[296,768]{1,0:T(8,128)(2,1)S(1)} collective-permute-done((bf16[296,768]{1,0:T(8,128)(2,1)S(1)}, bf16[296,768]{1,0:T(8,128)(2,1)S(1)}, u32[]{:S(2)}, u32[]{:S(2)}) %collective-permute-start.31) | collective-permute-done | bytes 454688 | tf_op jit(solution)/shard_map/ppermute | solution.py:1065
  436.1 2.3 slice_bitcast_fusion.1
  (225 shorter events, 67.6 us)
Async XLA Ops:
  3.2 17.5 %collective-permute-start = (bf16[512,768]{1,0:T(8,128)(2,1)}, bf16[512,768]{1,0:T(8,128)(2,1)S(1)}, u32[]{:S(2)}, u32[]{:S(2)}) collective-permute-start(bf16[512,768]{1,0:T(8,128)(2,1)} %get-tuple-element.140), channel_id=1, source_target_pairs={{0,0},{1,16},{2,2},{3,18},{4,4},{5,20},{6,6},{7,22},{8,8},{9,24},{... | collective-permute-start | bytes 2359304 | tf_op jit(solution)/shard_map/ppermute | solution.py:940
  5.2 20.3 %collective-permute-start.1 = (bf16[512,768]{1,0:T(8,128)(2,1)S(1)}, bf16[512,768]{1,0:T(8,128)(2,1)}, u32[]{:S(2)}, u32[]{:S(2)}) collective-permute-start(bf16[512,768]{1,0:T(8,128)(2,1)S(1)} %get-tuple-element.141), channel_id=1, source_target_pairs={{0,8},{1,24},{2,10},{3,26},{4,12},{5,28},{6,14},{7,30},{8,0},{9,16... | collective-permute-start | bytes 2359304 | tf_op jit(solution)/shard_map/ppermute | solution.py:941
  8.1 99.5 %collective-permute-start.2 = (s32[2,2048]{1,0:T(2,128)S(1)}, s32[2,2048]{1,0:T(2,128)S(1)}, u32[]{:S(2)}, u32[]{:S(2)}) collective-permute-start(s32[2,2048]{1,0:T(2,128)S(1)} %copy-done.32), channel_id=1, source_target_pairs={{0,1},{1,0},{2,3},{3,2},{4,5},{5,4},{6,7},{7,6},{8,9},{9,8},{10,11... | collective-permute-start | bytes 49160 | tf_op jit(solution)/shard_map/ppermute | solution.py:934
  10.7 147.7 %collective-permute-start.5 = (bf16[512,768]{1,0:T(8,128)(2,1)}, bf16[512,768]{1,0:T(8,128)(2,1)}, u32[]{:S(2)}, u32[]{:S(2)}) collective-permute-start(bf16[512,768]{1,0:T(8,128)(2,1)} %get-tuple-element.134), channel_id=1, source_target_pairs={{0,0},{1,16},{2,2},{3,18},{4,4},{5,20},{6,6},{7,22},{8,8},{9,24},{... | collective-permute-start | bytes 2359304 | tf_op jit(solution)/shard_map/ppermute | solution.py:940
  18.1 140.3 %collective-permute-start.6 = (bf16[512,768]{1,0:T(8,128)(2,1)}, bf16[512,768]{1,0:T(8,128)(2,1)}, u32[]{:S(2)}, u32[]{:S(2)}) collective-permute-start(bf16[512,768]{1,0:T(8,128)(2,1)} %get-tuple-element.135), channel_id=1, source_target_pairs={{0,8},{1,24},{2,10},{3,26},{4,12},{5,28},{6,14},{7,30},{8,0},{9,16... | collective-permute-start | bytes 2359304 | tf_op jit(solution)/shard_map/ppermute | solution.py:941
  26.9 84.2 %collective-permute-start.3 = (bf16[1024,768]{1,0:T(8,128)(2,1)S(1)}, bf16[1024,768]{1,0:T(8,128)(2,1)S(1)}, u32[]{:S(2)}, u32[]{:S(2)}) collective-permute-start(bf16[1024,768]{1,0:T(8,128)(2,1)S(1)} %pad_maximum_fusion.1.own.x_ref), channel_id=1, source_target_pairs={{0,1},{1,0},{2,3},{3,2},{4,5},{5,4},{6,7},{7,6},{8,9},{9,8},{10,11... | collective-permute-start | bytes 4718600 | tf_op jit(solution)/shard_map/ppermute | solution.py:934
  156.1 5.0 %collective-permute-start.4 = (bf16[1024,384]{1,0:T(8,128)(2,1)S(1)}, bf16[1024,384]{1,0:T(8,128)(2,1)S(1)}, u32[]{:S(2)}, u32[]{:S(2)}) collective-permute-start(bf16[1024,384]{1,0:T(8,128)(2,1)S(1)} %get-tuple-element.136), channel_id=1, source_target_pairs={{0,1},{1,0},{2,3},{3,2},{4,5},{5,4},{6,7},{7,6},{8,9},{9,8},{10,11... | collective-permute-start | bytes 2359304 | tf_op jit(solution)/shard_map/ppermute | solution.py:934
  220.2 20.4 %collective-permute-start.9 = (bf16[4,4,2,96,768]{4,3,2,1,0:T(8,128)(2,1)}, bf16[4,4,2,96,768]{4,3,2,1,0:T(8,128)(2,1)}, u32[]{:S(2)}, u32[]{:S(2)}) collective-permute-start(bf16[4,4,2,96,768]{4,3,2,1,0:T(8,128)(2,1)} %get-tuple-element.72), channel_id=1, source_target_pairs={{0,1},{1,0},{2,3},{3,2},{4,5},{5,4},{6,7},{7,6},{8,9},{9,8},{10,11... | collective-permute-start | bytes 14155784 | tf_op jit(solution)/shard_map/ppermute | solution.py:934
  220.3 25.5 %collective-permute-start.10 = (bf16[1024,384]{1,0:T(8,128)(2,1)}, bf16[1024,384]{1,0:T(8,128)(2,1)S(1)}, u32[]{:S(2)}, u32[]{:S(2)}) collective-permute-start(bf16[1024,384]{1,0:T(8,128)(2,1)} %get-tuple-element.73), channel_id=1, source_target_pairs={{0,1},{1,0},{2,3},{3,2},{4,5},{5,4},{6,7},{7,6},{8,9},{9,8},{10,11... | collective-permute-start | bytes 2359304 | tf_op jit(solution)/shard_map/ppermute | solution.py:934
  225.8 109.4 %collective-permute-start.21 = (bf16[4,96,768]{2,1,0:T(8,128)(2,1)}, bf16[4,96,768]{2,1,0:T(8,128)(2,1)S(1)}, u32[]{:S(2)}, u32[]{:S(2)}) collective-permute-start(bf16[4,96,768]{2,1,0:T(8,128)(2,1)} %get-tuple-element.93), channel_id=1, source_target_pairs={{0,1},{1,0},{2,3},{3,2},{4,5},{5,4},{6,7},{7,6},{8,9},{9,8},{10,11... | collective-permute-start | bytes 1769480 | tf_op jit(solution)/shard_map/ppermute | solution.py:934
  233.1 110.4 %collective-permute-start.7 = (bf16[512,768]{1,0:T(8,128)(2,1)}, bf16[512,768]{1,0:T(8,128)(2,1)}, u32[]{:S(2)}, u32[]{:S(2)}) collective-permute-start(bf16[512,768]{1,0:T(8,128)(2,1)} %get-tuple-element.130), channel_id=1, source_target_pairs={{0,0},{16,1},{2,2},{18,3},{4,4},{20,5},{6,6},{22,7},{8,8},{24,9},{... | collective-permute-start | bytes 2359304 | tf_op jit(solution)/shard_map/ppermute | solution.py:949
  246.7 57.2 %collective-permute-start.11 = (bf16[4,2,96,768]{3,2,1,0:T(8,128)(2,1)}, bf16[4,2,96,768]{3,2,1,0:T(8,128)(2,1)S(1)}, u32[]{:S(2)}, u32[]{:S(2)}) collective-permute-start(bf16[4,2,96,768]{3,2,1,0:T(8,128)(2,1)} %get-tuple-element.74), channel_id=1, source_target_pairs={{0,8},{1,9},{2,10},{3,11},{4,12},{5,13},{6,14},{7,15},{8,0},{9,1},... | collective-permute-start | bytes 3538952 | tf_op jit(solution)/shard_map/ppermute | solution.py:1065
  248.2 57.2 %collective-permute-start.12 = (bf16[4,2,96,768]{3,2,1,0:T(8,128)(2,1)S(1)}, bf16[4,2,96,768]{3,2,1,0:T(8,128)(2,1)}, u32[]{:S(2)}, u32[]{:S(2)}) collective-permute-start(bf16[4,2,96,768]{3,2,1,0:T(8,128)(2,1)S(1)} %get-tuple-element.75), channel_id=1, source_target_pairs={{0,16},{1,17},{2,18},{3,19},{4,20},{5,21},{6,22},{7,23},{8,24},{9,... | collective-permute-start | bytes 3538952 | tf_op jit(solution)/shard_map/ppermute | solution.py:1065
  248.2 57.2 %collective-permute-start.13 = (bf16[4,2,96,768]{3,2,1,0:T(8,128)(2,1)S(1)}, bf16[4,2,96,768]{3,2,1,0:T(8,128)(2,1)}, u32[]{:S(2)}, u32[]{:S(2)}) collective-permute-start(bf16[4,2,96,768]{3,2,1,0:T(8,128)(2,1)S(1)} %get-tuple-element.76), channel_id=1, source_target_pairs={{0,24},{1,25},{2,26},{3,27},{4,28},{5,29},{6,30},{7,31},{8,16},{9,... | collective-permute-start | bytes 3538952 | tf_op jit(solution)/shard_map/ppermute | solution.py:1065
  303.8 39.7 %collective-permute-start.8 = (bf16[512,768]{1,0:T(8,128)(2,1)}, bf16[512,768]{1,0:T(8,128)(2,1)}, u32[]{:S(2)}, u32[]{:S(2)}) collective-permute-start(bf16[512,768]{1,0:T(8,128)(2,1)} %get-tuple-element.131), channel_id=1, source_target_pairs={{8,0},{24,1},{10,2},{26,3},{12,4},{28,5},{14,6},{30,7},{0,8},{16,9... | collective-permute-start | bytes 2359304 | tf_op jit(solution)/shard_map/ppermute | solution.py:950
  332.0 4.4 %collective-permute-start.20 = (bf16[3,4,96,384]{3,2,1,0:T(8,128)(2,1)}, bf16[3,4,96,384]{3,2,1,0:T(8,128)(2,1)S(1)}, u32[]{:S(2)}, u32[]{:S(2)}) collective-permute-start(bf16[3,4,96,384]{3,2,1,0:T(8,128)(2,1)} %get-tuple-element.90), channel_id=1, source_target_pairs={{0,1},{1,0},{2,3},{3,2},{4,5},{5,4},{6,7},{7,6},{8,9},{9,8},{10,11... | collective-permute-start | bytes 2654216 | tf_op jit(solution)/shard_map/ppermute | solution.py:934
  335.1 1.3 collective-permute-start.22
  338.8 17.4 %collective-permute-start.23 = (bf16[4,104,768]{2,1,0:T(8,128)(2,1)}, bf16[4,104,768]{2,1,0:T(8,128)(2,1)S(1)}, u32[]{:S(2)}, u32[]{:S(2)}) collective-permute-start(bf16[4,104,768]{2,1,0:T(8,128)(2,1)} %get-tuple-element.118), channel_id=1, source_target_pairs={{0,8},{1,9},{2,10},{3,11},{4,12},{5,13},{6,14},{7,15},{8,0},{9,1},... | collective-permute-start | bytes 1916936 | tf_op jit(solution)/shard_map/ppermute | solution.py:1065
  338.8 17.4 %collective-permute-start.24 = (bf16[4,104,768]{2,1,0:T(8,128)(2,1)}, bf16[4,104,768]{2,1,0:T(8,128)(2,1)}, u32[]{:S(2)}, u32[]{:S(2)}) collective-permute-start(bf16[4,104,768]{2,1,0:T(8,128)(2,1)} %get-tuple-element.120), channel_id=1, source_target_pairs={{0,16},{1,17},{2,18},{3,19},{4,20},{5,21},{6,22},{7,23},{8,24},{9,... | collective-permute-start | bytes 1916936 | tf_op jit(solution)/shard_map/ppermute | solution.py:1065
  340.4 32.1 %collective-permute-start.25 = (bf16[4,104,768]{2,1,0:T(8,128)(2,1)}, bf16[4,104,768]{2,1,0:T(8,128)(2,1)}, u32[]{:S(2)}, u32[]{:S(2)}) collective-permute-start(bf16[4,104,768]{2,1,0:T(8,128)(2,1)} %get-tuple-element.119), channel_id=1, source_target_pairs={{0,24},{1,25},{2,26},{3,27},{4,28},{5,29},{6,30},{7,31},{8,16},{9,... | collective-permute-start | bytes 1916936 | tf_op jit(solution)/shard_map/ppermute | solution.py:1065
  343.5 51.8 %collective-permute-start.14 = (bf16[1024,768]{1,0:T(8,128)(2,1)}, bf16[1024,768]{1,0:T(8,128)(2,1)}, u32[]{:S(2)}, u32[]{:S(2)}) collective-permute-start(bf16[1024,768]{1,0:T(8,128)(2,1)} %convert_element_type.296), channel_id=1, source_target_pairs={{0,1},{1,0},{2,3},{3,2},{4,5},{5,4},{6,7},{7,6},{8,9},{9,8},{10,11... | collective-permute-start | bytes 4718600 | tf_op jit(solution)/shard_map/ppermute | solution.py:934
  346.4 28.0 %collective-permute-start.17 = (bf16[2,96,768]{2,1,0:T(8,128)(2,1)S(1)}, bf16[2,96,768]{2,1,0:T(8,128)(2,1)S(1)}, u32[]{:S(2)}, u32[]{:S(2)}) collective-permute-start(bf16[2,96,768]{2,1,0:T(8,128)(2,1)S(1)} %copy-done.17), channel_id=1, source_target_pairs={{0,2},{1,3},{2,0},{3,1},{4,6},{5,7},{6,4},{7,5},{8,10},{9,11},{10,... | collective-permute-start | bytes 884744 | tf_op jit(solution)/shard_map/ppermute | solution.py:1069
  356.2 18.8 %collective-permute-start.18 = (bf16[2,96,768]{2,1,0:T(8,128)(2,1)S(1)}, bf16[2,96,768]{2,1,0:T(8,128)(2,1)S(1)}, u32[]{:S(2)}, u32[]{:S(2)}) collective-permute-start(bf16[2,96,768]{2,1,0:T(8,128)(2,1)S(1)} %copy-done.16), channel_id=1, source_target_pairs={{0,4},{1,5},{2,6},{3,7},{4,0},{5,1},{6,2},{7,3},{8,12},{9,13},{10,... | collective-permute-start | bytes 884744 | tf_op jit(solution)/shard_map/ppermute | solution.py:1069
  356.2 24.2 %collective-permute-start.19 = (bf16[2,96,768]{2,1,0:T(8,128)(2,1)S(1)}, bf16[2,96,768]{2,1,0:T(8,128)(2,1)S(1)}, u32[]{:S(2)}, u32[]{:S(2)}) collective-permute-start(bf16[2,96,768]{2,1,0:T(8,128)(2,1)S(1)} %copy-done.15), channel_id=1, source_target_pairs={{0,6},{1,7},{2,4},{3,5},{4,2},{5,3},{6,0},{7,1},{8,14},{9,15},{10,... | collective-permute-start | bytes 884744 | tf_op jit(solution)/shard_map/ppermute | solution.py:1069
  374.3 9.1 %collective-permute-start.26 = (bf16[104,768]{1,0:T(8,128)(2,1)S(1)}, bf16[104,768]{1,0:T(8,128)(2,1)S(1)}, u32[]{:S(2)}, u32[]{:S(2)}) collective-permute-start(bf16[104,768]{1,0:T(8,128)(2,1)S(1)} %get-tuple-element.142), channel_id=1, source_target_pairs={{0,2},{1,3},{2,0},{3,1},{4,6},{5,7},{6,4},{7,5},{8,10},{9,11},{10,... | collective-permute-start | bytes 479240 | tf_op jit(solution)/shard_map/ppermute | solution.py:1069
  374.4 19.2 %collective-permute-start.27 = (bf16[104,768]{1,0:T(8,128)(2,1)S(1)}, bf16[104,768]{1,0:T(8,128)(2,1)S(1)}, u32[]{:S(2)}, u32[]{:S(2)}) collective-permute-start(bf16[104,768]{1,0:T(8,128)(2,1)S(1)} %get-tuple-element.144), channel_id=1, source_target_pairs={{0,4},{1,5},{2,6},{3,7},{4,0},{5,1},{6,2},{7,3},{8,12},{9,13},{10,... | collective-permute-start | bytes 479240 | tf_op jit(solution)/shard_map/ppermute | solution.py:1069
  375.0 18.7 %collective-permute-start.28 = (bf16[104,768]{1,0:T(8,128)(2,1)S(1)}, bf16[104,768]{1,0:T(8,128)(2,1)S(1)}, u32[]{:S(2)}, u32[]{:S(2)}) collective-permute-start(bf16[104,768]{1,0:T(8,128)(2,1)S(1)} %get-tuple-element.143), channel_id=1, source_target_pairs={{0,6},{1,7},{2,4},{3,5},{4,2},{5,3},{6,0},{7,1},{8,14},{9,15},{10,... | collective-permute-start | bytes 479240 | tf_op jit(solution)/shard_map/ppermute | solution.py:1069
  393.7 13.4 %collective-permute-start.29 = (bf16[296,768]{1,0:T(8,128)(2,1)S(1)}, bf16[296,768]{1,0:T(8,128)(2,1)S(1)}, u32[]{:S(2)}, u32[]{:S(2)}) collective-permute-start(bf16[296,768]{1,0:T(8,128)(2,1)S(1)} %pad_maximum_fusion.6), channel_id=1, source_target_pairs={{0,8},{1,9},{2,10},{3,11},{4,12},{5,13},{6,14},{7,15},{8,0},{9,1},... | collective-permute-start | bytes 1363976 | tf_op jit(solution)/shard_map/ppermute | solution.py:1065
  397.4 14.9 %collective-permute-start.30 = (bf16[296,768]{1,0:T(8,128)(2,1)S(1)}, bf16[296,768]{1,0:T(8,128)(2,1)S(1)}, u32[]{:S(2)}, u32[]{:S(2)}) collective-permute-start(bf16[296,768]{1,0:T(8,128)(2,1)S(1)} %pad_maximum_fusion.6), channel_id=1, source_target_pairs={{0,16},{1,17},{2,18},{3,19},{4,20},{5,21},{6,22},{7,23},{8,24},{9,... | collective-permute-start | bytes 1363976 | tf_op jit(solution)/shard_map/ppermute | solution.py:1065
  397.6 40.7 %collective-permute-start.15 = (bf16[512,768]{1,0:T(8,128)(2,1)S(1)}, bf16[512,768]{1,0:T(8,128)(2,1)S(1)}, u32[]{:S(2)}, u32[]{:S(2)}) collective-permute-start(bf16[512,768]{1,0:T(8,128)(2,1)S(1)} %get-tuple-element.126), channel_id=1, source_target_pairs={{0,0},{16,1},{2,2},{18,3},{4,4},{20,5},{6,6},{22,7},{8,8},{24,9},{... | collective-permute-start | bytes 2359304 | tf_op jit(solution)/shard_map/ppermute | solution.py:949
  398.4 40.0 %collective-permute-start.16 = (bf16[512,768]{1,0:T(8,128)(2,1)S(1)}, bf16[512,768]{1,0:T(8,128)(2,1)S(1)}, u32[]{:S(2)}, u32[]{:S(2)}) collective-permute-start(bf16[512,768]{1,0:T(8,128)(2,1)S(1)} %get-tuple-element.127), channel_id=1, source_target_pairs={{8,0},{24,1},{10,2},{26,3},{12,4},{28,5},{14,6},{30,7},{0,8},{16,9... | collective-permute-start | bytes 2359304 | tf_op jit(solution)/shard_map/ppermute | solution.py:950
  398.9 32.3 %collective-permute-start.31 = (bf16[296,768]{1,0:T(8,128)(2,1)S(1)}, bf16[296,768]{1,0:T(8,128)(2,1)S(1)}, u32[]{:S(2)}, u32[]{:S(2)}) collective-permute-start(bf16[296,768]{1,0:T(8,128)(2,1)S(1)} %pad_maximum_fusion.6), channel_id=1, source_target_pairs={{0,24},{1,25},{2,26},{3,27},{4,28},{5,29},{6,30},{7,31},{8,16},{9,... | collective-permute-start | bytes 1363976 | tf_op jit(solution)/shard_map/ppermute | solution.py:1065
  (44 other events, 557.0 us)

commit v3 on v2

--- a/solution.py
+++ b/solution.py
@@ -384,7 +384,7 @@
 
 def attend_back_kernel(
     core, low, high, q_ref, k_ref, v_ref, out_ref, own, other, lse, seg_col,
-    dq_out, dk_out, dv_out, grad, qx, kx, vx, gx, dq, dk, dv, weights, slopes,
+    dq_out, dk_out, dv_out, sums, grad, qx, kx, vx, gx, dq, dk, dv, weights, slopes,
 ):
     rows, width = q_ref.shape
     heads = width // HEAD_DIM
@@ -466,6 +466,9 @@
         dv_out[k_rows, :] = dv[...].astype(BF16)
 
     dq_out[...] = (dq[...] * SCALE).astype(BF16)
+    ones = jnp.ones((8, rows), BF16)
+    sums[0] = dot(ones, dq_out[...])
+    sums[1] = dot(ones, dv_out[...])
 
 
 def attend_back(core, begin, end, q, k, v, out, own, other, lse, seg_col):
@@ -475,14 +478,15 @@
     wide = pltpu.VMEM((heads, rows, 2 * HEAD_DIM), BF16)
     return pl.pallas_call(
         attend_back_kernel,
-        out_shape=[jax.ShapeDtypeStruct((rows, width), BF16)] * 3,
+        out_shape=[jax.ShapeDtypeStruct((rows, width), BF16)] * 3
+        + [jax.ShapeDtypeStruct((2, 8, width), F32)],
         grid_spec=pltpu.PrefetchScalarGridSpec(
             num_scalar_prefetch=3,
             grid=(1,),
             in_specs=[whole((rows, width))] * 4
             + [whole((rows // 2, width))] * 2
             + [whole((heads, rows)), whole((rows, 1))],
-            out_specs=[whole((rows, width))] * 3,
+            out_specs=[whole((rows, width))] * 3 + [whole((2, 8, width))],
             scratch_shapes=[
                 pltpu.VMEM((rows, width), BF16),
                 wide,
@@ -691,7 +695,7 @@
 
 
 def expand_grad_kernel(core, low, ge, keep, send):
-    nz, unit = keep.shape[1], keep.shape[3]
+    nz, unit = keep.shape[1], keep.shape[2]
     whole = dot_left(low[...], ge[...]).reshape(nz, 2, unit, -1)
     kept, sent = split_cores(core[0], whole, 1)
     keep[...] = kept.reshape(keep.shape)
@@ -699,156 +703,414 @@
 
 
 def reduce_grad_kernel(core, act, gr, keep_in, send_in, keep, send):
-    unit = keep.shape[3]
+    unit = keep.shape[2]
     whole = dot_left(act[...], gr[...]).reshape(2, 4, unit, -1)
     kept, sent = split_cores(core[0], whole, 0)
     keep[...] = kept.reshape(keep.shape)
     send[...] = sent.reshape(send.shape)
 
 
-def feed_grads(core, low, ge, act, gr):
+def output_grad_kernel(core, mine, theirs, gb, keep_in, send_in, keep, send):
+    quarter = keep.shape[2]
+    from_mine, from_theirs = dot_left(mine[...], gb[...]), dot_left(theirs[...], gb[...])
+    first = jnp.where(core[0] == 0, from_mine, from_theirs)
+    second = jnp.where(core[0] == 0, from_theirs, from_mine)
+    whole = jnp.concatenate([first, second]).reshape(keep.shape[1], 2, 4, quarter, -1)
+    kept, sent = split_cores(core[0], whole, 1)
+    for part in range(4):
+        keep[part] = kept[:, 0, part]
+        send[part] = sent[:, 0, part]
+
+
+def feed_grads(core, low, ge, act, gr, mine, theirs, gb):
     rows, width = low.shape
     wide = ge.shape[1]
     chunks = wide // width
-    unit = width // 8
-    shape = jax.ShapeDtypeStruct((4, 4, 2, unit, width), BF16)
+    unit = width // UNITS
+    quarter = unit // 4
+    nz = UNITS // 2
+    shape = jax.ShapeDtypeStruct((4, nz, 2 * unit + quarter, width), BF16)
+    anywhere = pl.BlockSpec(memory_space=pl.ANY)
+    whole = lambda a: pl.BlockSpec(a.shape, lambda i, *_: (0,) * a.ndim)
+    chunk = pl.BlockSpec((rows, width), lambda i, *_: (0, i))
     flops = 2 * rows * width * wide
-    keep, send = pl.pallas_call(
+
+    def call(kernel, grid, in_specs, out_spec, name, flops, *operands, aliases={}):
+        return pl.pallas_call(
+            kernel,
+            out_shape=[shape, shape],
+            grid_spec=pltpu.PrefetchScalarGridSpec(
+                num_scalar_prefetch=1, grid=(grid,), in_specs=in_specs, out_specs=[out_spec] * 2
+            ),
+            input_output_aliases=aliases,
+            compiler_params=params(),
+            cost_estimate=pl.CostEstimate(flops=flops, bytes_accessed=14 << 20, transcendentals=0),
+            name=name,
+        )(core, *operands)
+
+    keep, send = call(
         expand_grad_kernel,
-        out_shape=[shape, shape],
-        grid_spec=pltpu.PrefetchScalarGridSpec(
-            num_scalar_prefetch=1,
-            grid=(chunks,),
-            in_specs=[
-                pl.BlockSpec((rows, width), lambda i, *_: (0, 0)),
-                pl.BlockSpec((rows, width), lambda i, *_: (0, i)),
-            ],
-            out_specs=[pl.BlockSpec((1, 4, 1, unit, width), lambda i, *_: (i, 0, 0, 0, 0))] * 2,
-        ),
-        compiler_params=params(),
-        cost_estimate=pl.CostEstimate(flops=flops, bytes_accessed=14 << 20, transcendentals=0),
-        name="expand_grad",
-    )(core, low, ge)
-    return pl.pallas_call(
+        chunks,
+        [whole(low), chunk],
+        pl.BlockSpec((1, nz, unit, width), lambda i, *_: (i, 0, 0, 0)),
+        "expand_grad",
+        flops,
+        low,
+        ge,
+    )
+    keep, send = call(
         reduce_grad_kernel,
-        out_shape=[shape, shape],
-        grid_spec=pltpu.PrefetchScalarGridSpec(
-            num_scalar_prefetch=1,
-            grid=(chunks,),
-            in_specs=[
-                pl.BlockSpec((rows, width), lambda i, *_: (0, i)),
-                pl.BlockSpec((rows, width), lambda i, *_: (0, 0)),
-                pl.BlockSpec(memory_space=pl.ANY),
-                pl.BlockSpec(memory_space=pl.ANY),
-            ],
-            out_specs=[pl.BlockSpec((4, 1, 1, unit, width), lambda i, *_: (0, i, 1, 0, 0))] * 2,
-        ),
-        input_output_aliases={3: 0, 4: 1},
-        compiler_params=params(),
-        cost_estimate=pl.CostEstimate(flops=flops, bytes_accessed=14 << 20, transcendentals=0),
-        name="reduce_grad",
-    )(core, act, gr, keep, send)
-
-
-def output_grad_kernel(core, mine, theirs, gb, keep, send):
-    nz, unit = keep.shape[:2]
-    from_mine, from_theirs = dot_left(mine[...], gb[...]), dot_left(theirs[...], gb[...])
-    first = jnp.where(core[0] == 0, from_mine, from_theirs)
-    second = jnp.where(core[0] == 0, from_theirs, from_mine)
-    whole = jnp.concatenate([first, second]).reshape(nz, 2, unit, -1)
-    kept, sent = split_cores(core[0], whole, 1)
-    keep[...] = kept.reshape(keep.shape)
-    send[...] = sent.reshape(send.shape)
-
-
-def output_grad(core, mine, theirs, gb):
-    rows = mine.shape[0]
-    width = gb.shape[1]
-    shape = jax.ShapeDtypeStruct((4, width // 8, width), BF16)
-    whole = lambda a: pl.BlockSpec(a.shape, lambda i, *_: (0,) * a.ndim)
-    return pl.pallas_call(
+        chunks,
+        [chunk, whole(gr), anywhere, anywhere],
+        pl.BlockSpec((4, 1, unit, width), lambda i, *_: (0, i, 1, 0)),
+        "reduce_grad",
+        flops,
+        act,
+        gr,
+        keep,
+        send,
+        aliases={3: 0, 4: 1},
+    )
+    return call(
         output_grad_kernel,
-        out_shape=[shape, shape],
-        grid_spec=pltpu.PrefetchScalarGridSpec(
-            num_scalar_prefetch=1,
-            grid=(1,),
-            in_specs=[whole(mine), whole(theirs), whole(gb)],
-            out_specs=[whole(shape)] * 2,
-        ),
-        compiler_params=params(),
-        cost_estimate=pl.CostEstimate(
-            flops=2 * rows * width * width, bytes_accessed=5 << 20, transcendentals=0
-        ),
-        name="output_grad",
-    )(core, mine, theirs, gb)
-
-
-def packed_input_grad_kernel(
-    core, own, other, d_ref, w_ref, keep, send, sums, dx_own, dx_other
+        1,
+        [whole(mine), whole(theirs), whole(gb), anywhere, anywhere],
+        pl.BlockSpec((4, nz, quarter, width), lambda i, *_: (0, 0, UNITS, 0)),
+        "output_grad",
+        flops // chunks,
+        mine,
+        theirs,
+        gb,
+        keep,
+        send,
+        aliases={4: 0, 5: 1},
+    )
+
+
+def finish_kernel(
+    own, other, dq, dk, dv, square, residual, feed, small_keep, small_send,
+    dx_out, qkv_out, expand_out, reduce_out, output_out, small_out,
+    x, d, w, res, keep, send, twin_part, plane_got, line_part, line_got, around,
+    feed_mine, feed_got, feed_around, to_twin, from_twin, ready,
+    small_got, small_plane, small_line,
+    loads, core_s, core_r, dx_s, dx_r, move_s, move_r, moved, plane_s, plane_r, line_s, line_r, ring_s, ring_r,
+    feed_s, feed_r, feed_ring_s, feed_ring_r, small_s, small_r,
 ):
-    part = pl.program_id(0)
+    r, s = lax.axis_index("rep"), lax.axis_index("shard")
+    z, core = s // 2, s % 2
+    half = dq.shape[1]
     rows = own.shape[0]
-    nz, unit = keep.shape[1], keep.shape[2]
-    mine = pl.multiple_of(core[0] * rows, rows)
-    theirs = pl.multiple_of((1 - core[0]) * rows, rows)
-    d_own, d_other = d_ref[0, pl.ds(mine, rows), :], d_ref[0, pl.ds(theirs, rows), :]
-    whole = (dot_left(own[...], d_own) + dot_left(other[...], d_other)).reshape(nz, 2, unit, -1)
-    kept, sent = split_cores(core[0], whole, 1)
-    keep[...] = kept.reshape(keep.shape)
-    send[...] = sent.reshape(send.shape)
-    sums[0] = jnp.broadcast_to(column_sum(d_own) + column_sum(d_other), sums.shape[1:])
-    to_own, to_other = dot_right(d_own, stacked(w_ref)), dot_right(d_other, stacked(w_ref))
-
-    @pl.when(part == 0)
+    block = rows // 2
+    unit = qkv_out.shape[1]
+    quarter = unit // 4
+    nz = feed.shape[0]
+    odd = r % 2
+    home = r // 2 == core
+    twin = (r, s ^ 1)
+    plane = lambda k: (r ^ k, s)
+    line = lambda k: (r, s ^ (2 * k))
+    barrier = pltpu.get_barrier_semaphore()
+    mesh_id = pl.DeviceIdType.MESH
+    friends = [twin, (r ^ 2, s ^ 1), (r ^ 3, s ^ 1)] + [plane(k) for k in (1, 2, 3)]
+    friends += [line(k) for k in range(1, nz)]
+    for device in friends:
+        pl.semaphore_signal(barrier, 1, device_id=device, device_id_type=mesh_id)
+    pl.semaphore_wait(barrier, len(friends))
+
+    def copy(source, target, sent, got, device):
+        return pltpu.make_async_remote_copy(
+            source, target, sent, got, device_id=device, device_id_type=mesh_id
+        )
+
+    local = [
+        pltpu.make_async_copy(own, x.at[0], loads.at[0]),
+        pltpu.make_async_copy(other, x.at[1], loads.at[1]),
+        pltpu.make_async_copy(dq, d.at[0], loads.at[2]),
+        pltpu.make_async_copy(dk, d.at[1], loads.at[3]),
+        pltpu.make_async_copy(dv, d.at[2], loads.at[4]),
+        pltpu.make_async_copy(residual, res, loads.at[5]),
+        pltpu.make_async_copy(feed.at[z], feed_mine, loads.at[6]),
+    ] + [
+        pltpu.make_async_copy(
+            square.at[:, pl.ds(m * unit, unit), pl.ds(pl.multiple_of(core * half, half), half)],
+            w.at[m],
+            loads.at[7 + m],
+        )
+        for m in range(3)
+    ]
+    for c in local:
+        c.start()
+    feed_line = [
+        copy(feed.at[z ^ k], feed_got.at[k - 1], feed_s.at[k - 1], feed_r.at[k - 1], line(k))
+        for k in range(1, nz)
+    ]
+    small_core = copy(small_send, small_got, small_s.at[0], small_r.at[0], twin)
+    for c in feed_line + [small_core]:
+        c.start()
+    for c in local[:5]:
+        c.wait()
+
+    def cross(m):
+        return copy(send.at[m], twin_part.at[m], core_s.at[m], core_r.at[m], twin)
+
+    def spread(m, side, k):
+        source = keep if side == 0 else twin_part
+        return copy(
+            source.at[m, r ^ k],
+            plane_got.at[k - 1, m, side],
+            plane_s.at[k - 1, m, side],
+            plane_r.at[k - 1, m, side],
+            plane(k),
+        )
+
+    mine, theirs = rows_at(core, rows), rows_at(1 - core, rows)
+
+    def weight(m, carry):
+        whole = dot_left(x[0], d[m, mine, :]) + dot_left(x[1], d[m, theirs, :])
+        kept, sent = split_cores(core, whole.reshape(nz, 2, 4, quarter, half), 1)
+        for part in range(4):
+            keep[m, part] = kept[:, 0, part]
+            send[m, part] = sent[:, 0, part]
+        cross(m).start()
+        for k in (1, 2, 3):
+            spread(m, 0, k).start()
+        return carry
+
+    lax.fori_loop(0, 3, weight, 0)
+    for c in local[7:]:
+        c.wait()
+
+    def share(at):
+        total = dot_right(d[0, at, :], w[0].reshape(-1, half))
+        for m in (1, 2):
+            total = total + dot_right(d[m, at, :], w[m].reshape(-1, half))
+        return total
+
+    def give(t):
+        return copy(to_twin.at[t], from_twin.at[t], dx_s.at[t], dx_r.at[t], twin)
+
+    def away(t, carry):
+        at = pl.ds(pl.multiple_of((1 - core) * rows + t * block, block), block)
+        to_twin[t] = share(at).astype(BF16)
+        give(t).start()
+        return carry
+
+    lax.fori_loop(0, 2, away, 0)
+
+    def take(m, carry):
+        cross(m).wait_recv()
+        for k in (1, 2, 3):
+            spread(m, 1, k).start()
+        return carry
+
+    lax.fori_loop(0, 3, take, 0)
+    local[5].wait()
+
+    def stay(turn):
+        return pltpu.make_async_copy(ready.at[odd ^ turn], dx_out.at[odd], moved.at[turn])
+
+    def leave(turn, device):
+        return copy(ready.at[odd ^ turn], dx_out.at[odd], move_s.at[turn], move_r.at[turn], device)
+
+    for turn in (0, 1):
+        t = odd ^ turn
+        at = pl.ds(pl.multiple_of(core * rows + t * block, block), block)
+        total = share(at) + res[rows_at(t, block), :]
+        give(t).wait_recv()
+        ready[t] = (total + from_twin[t].astype(F32)).astype(BF16)
+        if turn == 0:
+
+            @pl.when(home)
+            def _():
+                stay(0).start()
+
+            @pl.when(jnp.logical_not(home))
+            def _():
+                leave(0, (r ^ 2, s ^ 1)).start()
+
+        else:
+
+            @pl.when(home)
+            def _():
+                leave(1, (r ^ 1, s)).start()
+
+            @pl.when(jnp.logical_not(home))
+            def _():
+                leave(1, (r ^ 3, s ^ 1)).start()
+
+    small_core.wait()
+    small_mine = small_keep[...] + small_got[...]
+    small_got[...] = small_mine
+    small_around = [
+        copy(small_got, small_plane.at[k - 1], small_s.at[k], small_r.at[k], plane(k))
+        for k in (1, 2, 3)
+    ]
+    for c in small_around:
+        c.start()
+    local[6].wait()
+    total = feed_mine[...].astype(F32)
+    for n, c in enumerate(feed_line):
+        c.wait_recv()
+        total = total + feed_got[n].astype(F32)
+    feed_around[0] = total.astype(BF16)
+    feed_ring = [
+        copy(
+            feed_around.at[0], feed_around.at[k], feed_ring_s.at[k - 1], feed_ring_r.at[k - 1], plane(k)
+        )
+        for k in (1, 2, 3)
+    ]
+    for c in feed_ring:
+        c.start()
+    small_total = small_mine
+    for n, c in enumerate(small_around):
+        c.wait()
+        small_total = small_total + small_plane[n]
+    small_got[...] = small_total
+    small_along = [
+        copy(small_got.at[z ^ k], small_line.at[k - 1], small_s.at[3 + k], small_r.at[3 + k], line(k))
+        for k in range(1, nz)
+    ]
+    for c in small_along:
+        c.start()
+    for m in range(3):
+        for side in (0, 1):
+            source = keep if side == 0 else twin_part
+            total = source[m, r].astype(F32)
+            for k in (1, 2, 3):
+                spread(m, side, k).wait_recv()
+                total = total + plane_got[k - 1, m, side].astype(F32)
+            for n in range(nz):
+                line_part[n, m, side] = total[n].astype(BF16)
+    qkv_line = [
+        copy(line_part.at[z ^ k], line_got.at[k - 1], line_s.at[k - 1], line_r.at[k - 1], line(k))
+        for k in range(1, nz)
+    ]
+    for c in qkv_line:
+        c.start()
+    total = line_part[z].astype(F32)
+    for n, c in enumerate(qkv_line):
+        c.wait_recv()
+        total = total + line_got[n].astype(F32)
+    around[0] = total.astype(BF16)
+    qkv_ring = [
+        copy(around.at[0], around.at[k], ring_s.at[k - 1], ring_r.at[k - 1], plane(k)) for k in (1, 2, 3)
+    ]
+    for c in qkv_ring:
+        c.start()
+    total = small_got[z]
+    for n, c in enumerate(small_along):
+        c.wait()
+        total = total + small_line[n]
+    small_out[...] = total
+    width = qkv_out.shape[2]
+    for k in range(4):
+        if k > 0:
+            feed_ring[k - 1].wait()
+        part = r ^ k
+        expand_out[:, rows_at(part, width)] = feed_around[k, :unit, :].astype(F32)
+        reduce_out[rows_at(part, unit), :] = feed_around[k, unit : 2 * unit, :].astype(F32)
+        output_out[rows_at(part, quarter), :] = feed_around[k, 2 * unit :, :].astype(F32)
+    for k in range(4):
+        if k > 0:
+            qkv_ring[k - 1].wait()
+        at = rows_at(r ^ k, quarter)
+        qkv_out[:, at, rows_at(core, half)] = around[k, :, 0].astype(F32)
+        qkv_out[:, at, rows_at(1 - core, half)] = around[k, :, 1].astype(F32)
+
+    @pl.when(home)
     def _():
-        dx_own[...] = to_own
-        dx_other[...] = to_other
-
-    @pl.when(part > 0)
+        stay(0).wait()
+        leave(1, (r ^ 1, s)).wait()
+
+    @pl.when(jnp.logical_not(home))
     def _():
-        dx_own[...] += to_own
-        dx_other[...] += to_other
-
-
-def packed_input_grad(core, own, other, grads, weights):
+        leave(0, (r ^ 2, s ^ 1)).wait()
+        leave(1, (r ^ 3, s ^ 1)).wait()
+
+    for c in feed_line + qkv_line:
+        c.wait_send()
+    for m in range(3):
+        cross(m).wait_send()
+        for side in (0, 1):
+            for k in (1, 2, 3):
+                spread(m, side, k).wait_send()
+    for t in (0, 1):
+        give(t).wait_send()
+
+
+def finish(own, other, dq, dk, dv, square, residual, feed, small_keep, small_send, wide):
     rows, width = own.shape
     half = width // 2
-    unit = width // 8
-    shape = jax.ShapeDtypeStruct((3, 4, unit, half), BF16)
-    whole = lambda shape: pl.BlockSpec(shape, lambda i, *_: (0,) * len(shape))
-    packed = pl.BlockSpec((1, 4, unit, half), lambda i, core: (i, 0, 0, 0))
+    nz = feed.shape[0]
+    unit = width // UNITS
+    quarter = unit // 4
+    block = rows // 2
+    anywhere = pl.BlockSpec(memory_space=pl.ANY)
+    vmem = pl.BlockSpec(memory_space=pltpu.VMEM)
+    sems = lambda *shape: pltpu.SemaphoreType.DMA(shape)
+    low = lambda *shape: pltpu.VMEM(shape, BF16)
+    high = lambda *shape: pltpu.VMEM(shape, F32)
+    part = (quarter, half)
     return pl.pallas_call(
-        packed_input_grad_kernel,
+        finish_kernel,
         out_shape=[
-            shape,
-            shape,
-            jax.ShapeDtypeStruct((3, 8, half), F32),
-            jax.ShapeDtypeStruct((rows, width), F32),
-            jax.ShapeDtypeStruct((rows, width), F32),
+            jax.ShapeDtypeStruct((2, block, width), BF16),
+            jax.ShapeDtypeStruct((3, unit, width), F32),
+            jax.ShapeDtypeStruct((unit, wide), F32),
+            jax.ShapeDtypeStruct((4 * unit, width), F32),
+            jax.ShapeDtypeStruct((unit, width), F32),
+            jax.ShapeDtypeStruct(small_keep.shape[1:], F32),
         ],
-        grid_spec=pltpu.PrefetchScalarGridSpec(
-            num_scalar_prefetch=1,
-            grid=(3,),
-            in_specs=[
-                whole((rows, width)),
-                whole((rows, width)),
-                pl.BlockSpec((1, 2 * rows, half), lambda i, core: (i, 0, 0)),
-                pl.BlockSpec((UNITS, width // UNITS, half), lambda i, core: (0, i, core[0])),
-            ],
-            out_specs=[
-                packed,
-                packed,
-                pl.BlockSpec((1, 8, half), lambda i, core: (i, 0, 0)),
-                whole((rows, width)),
-                whole((rows, width)),
-            ],
+        in_specs=[anywhere] * 8 + [vmem] * 2,
+        out_specs=[anywhere] + [vmem] * 5,
+        scratch_shapes=[
+            low(2, rows, width),
+            low(3, 2 * rows, half),
+            low(3, UNITS, unit, half),
+            high(rows, width),
+            low(3, 4, nz, *part),
+            low(3, 4, nz, *part),
+            low(3, 4, nz, *part),
+            low(3, 3, 2, nz, *part),
+            low(nz, 3, 2, *part),
+            low(nz - 1, 3, 2, *part),
+            low(4, 3, 2, *part),
+            low(*feed.shape[1:]),
+            low(nz - 1, *feed.shape[1:]),
+            low(4, *feed.shape[1:]),
+            low(2, block, width),
+            low(2, block, width),
+            low(2, block, width),
+            high(*small_keep.shape),
+            high(3, *small_keep.shape),
+            high(nz - 1, *small_keep.shape[1:]),
+            sems(10),
+            sems(3),
+            sems(3),
+            sems(2),
+            sems(2),
+            sems(2),
+            sems(2),
+            sems(2),
+            sems(3, 3, 2),
+            sems(3, 3, 2),
+            sems(nz - 1),
+            sems(nz - 1),
+            sems(3),
+            sems(3),
+            sems(nz - 1),
+            sems(nz - 1),
+            sems(3),
+            sems(3),
+            sems(3 + nz),
+            sems(3 + nz),
+        ],
+        compiler_params=params(collective_id=1, has_side_effects=True),
+        cost_estimate=pl.CostEstimate(
+            flops=2 * 2 * 2 * rows * width * 3 * half, bytes_accessed=150 << 20, transcendentals=0
         ),
-        compiler_params=params(),
-        cost_estimate=pl.CostEstimate(
-            flops=2 * 2 * 2 * rows * width * 3 * half, bytes_accessed=20 << 20, transcendentals=0
-        ),
-        name="input_grad",
-    )(core, own, other, grads, weights)
+        name="finish",
+    )(own, other, dq, dk, dv, square, residual, feed, small_keep, small_send)
 
 
 def input_grad_kernel(core, own, other, d_ref, w_ref, dw, sums, dx_own, dx_other):
@@ -1015,7 +1277,7 @@
         dwr = weight_grad(act, gr, F32)
         dwe = weight_grad(first_low, ge, F32)
         dwo_mine, dwo_theirs = weight_grad(mine, gb, F32), weight_grad(theirs, gb, F32)
-        dq, dk, dv = attend_back(
+        dq, dk, dv, sum_qv = attend_back(
             core_arg, begin, end, q, k, v, attended, ga_mine, ga_other, lse, seg_col
         )
         dw, sum_qkv, dx_own, dx_other = input_grad(
@@ -1057,45 +1319,17 @@
         final = [part.astype(F32) for part in lax.psum([p.astype(BF16) for p in summed], "rep")]
         return (from_sequences(out), from_sequences(dx)) + tuple(final)
 
-    z = shard // 2
     nz = shard_size // 2
 
-    def plane_send(array, k):
-        pairs = [(flat(r, s), flat(r ^ k, s)) for r in range(4) for s in range(shard_size)]
-        return lax.ppermute(array, both, pairs)
-
-    def line_send(array, k):
-        pairs = [(flat(r, s), flat(r, s ^ (2 * k))) for r in range(4) for s in range(shard_size)]
+    def plane_send(array, hop):
+        pairs = [(flat(r, s), flat(r ^ hop, s)) for r in range(4) for s in range(shard_size)]
         return lax.ppermute(array, both, pairs)
 
     def pick(array, n):
         return lax.dynamic_index_in_dim(array, n, 0, keepdims=False)
 
-    def scatter_plane(pieces):
-        got = [plane_send(pieces(rep ^ k).astype(BF16), k) for k in (1, 2, 3)]
-        total = pieces(rep)
-        for part in got:
-            total = total + part.astype(F32)
-        return total
-
-    def scatter_line(array):
-        got = [line_send(pick(array, z ^ k).astype(BF16), k) for k in range(1, nz)]
-        total = pick(array, z)
-        for part in got:
-            total = total + part.astype(F32)
-        return total
-
-    def gather_plane(part):
-        got = [part] + [plane_send(part, k) for k in (1, 2, 3)]
-        result = jnp.zeros((4,) + part.shape, part.dtype)
-        for k in range(4):
-            result = lax.dynamic_update_index_in_dim(result, got[k], rep ^ k, 0)
-        return result.astype(F32)
-
-    feed_keep, feed_send = feed_grads(core_arg, first_low, ge, act, gr)
-    wo_keep, wo_send = output_grad(core_arg, mine, theirs, gb)
+    feed_keep, feed_send = feed_grads(core_arg, first_low, ge, act, gr, mine, theirs, gb)
     feed_got = swap(feed_send)
-    wo_got = swap(wo_send)
     feed_parts = [
         pick(feed_keep, rep ^ hop).astype(F32) + pick(feed_got, rep ^ hop).astype(F32)
         for hop in range(4)
@@ -1105,24 +1339,9 @@
     feed = feed_parts[0]
     for hop in (1, 2, 3):
         feed = feed + plane_send(feed_sent[hop - 1], hop).astype(F32)
-    dq, dk, dv = attend_back(
+    feed = feed.astype(BF16)
+    dq, dk, dv, sum_qv = attend_back(
         core_arg, begin, end, q, k, v, attended, ga_mine, ga_other, lse, seg_col
-    )
-    line_sent = [pick(feed, z ^ hop).astype(BF16) for hop in range(1, nz)]
-    line_sent, dq = lax.optimization_barrier((line_sent, dq))
-    feed = pick(feed, z)
-    for hop in range(1, nz):
-        feed = feed + line_send(line_sent[hop - 1], hop).astype(F32)
-    feed = feed.astype(BF16)
-    qkv_keep, qkv_send, sum_qkv, dx_own, dx_other = packed_input_grad(
-        core_arg, own, other, jnp.stack([dq, dk, dv]), square
-    )
-    dx = (residual + dx_own + swap(dx_other.astype(BF16)).astype(F32)).astype(BF16)
-    qkv_got = swap(qkv_send)
-    qkv = jnp.where(
-        core == 0,
-        jnp.concatenate([qkv_keep, qkv_got], axis=3),
-        jnp.concatenate([qkv_got, qkv_keep], axis=3),
     )
     unit = width // shard_size
     wide_unit = sum_e.shape[1] // shard_size
@@ -1133,40 +1352,29 @@
             core == 0, jnp.concatenate([part, zero]), jnp.concatenate([zero, part])
         )
 
-    rows_of = [place(sum_qkv[0, 0]), place(sum_qkv[2, 0])] + [sums[n] for n in range(6)]
+    rows_of = [place(sum_qv[0, 0]), place(sum_qv[1, 0])] + [sums[n] for n in range(6)]
     table = jnp.concatenate(
         [vector.reshape(shard_size, unit) for vector in rows_of]
         + [
             sum_e.reshape(shard_size, wide_unit),
-            jnp.zeros((shard_size, 2 * width - 8 * unit - wide_unit), F32),
+            jnp.zeros((shard_size, 8 * 256 - 8 * unit - wide_unit), F32),
         ],
         axis=1,
-    ).reshape(nz, 2, 2, width)
-    mine_table = lax.dynamic_index_in_dim(table, core, 1, keepdims=False)
-    other_table = lax.dynamic_index_in_dim(table, 1 - core, 1, keepdims=False)
-    mine_table = mine_table + swap(other_table)
-    wo_sum = wo_keep.astype(F32) + wo_got.astype(F32)
-    fourth = jnp.concatenate([wo_sum, mine_table, jnp.zeros((nz, 6, width), F32)], axis=1)
-    rest = jnp.concatenate(
-        [
-            jnp.concatenate([qkv, jnp.zeros((3, nz, 8, width), BF16)], axis=2),
-            fourth.astype(BF16)[None],
-        ]
+    ).reshape(nz, 2, 8, 256)
+    small_keep = lax.dynamic_index_in_dim(table, core, 1, keepdims=False)
+    small_send = lax.dynamic_index_in_dim(table, 1 - core, 1, keepdims=False)
+    dx, dqkv, dwe, dwr, dwo, small = finish(
+        own, other, dq, dk, dv, square, residual, feed, small_keep, small_send, be.shape[1]
     )
-    rest = scatter_line(scatter_plane(lambda n: pick(rest, n).astype(F32))).astype(BF16)
-    result = gather_plane(jnp.concatenate([feed.reshape(2 * unit, width), rest]))
-    dwe = result[:, :unit].transpose(1, 0, 2).reshape(unit, 4 * width)
-    dwr = result[:, unit : 2 * unit].reshape(4 * unit, width)
-    dwq, dwk, dwv, dwo = [result[n, 2 * unit : 3 * unit] for n in range(4)]
-    small = result[3, 3 * unit : 3 * unit + 2].reshape(-1)
+    small = small.reshape(-1)
     dbq, dbv, dbo, dbr, dg1, ds1, dg2, ds2 = [small[n * unit : (n + 1) * unit] for n in range(8)]
     dbe = small[8 * unit : 8 * unit + wide_unit]
     return (
         from_sequences(out),
-        from_sequences(dx),
-        dwq,
-        dwk,
-        dwv,
+        dx,
+        dqkv[0],
+        dqkv[1],
+        dqkv[2],
         dwo,
         dwe,
         dwr,

time: 446 us -> 395 us (0.89)
  Pallas kernels: 246 us -> 296 us
  waiting for transfers between devices: 56 us -> 17.5 us
  starting transfers between devices: 66.2 us -> 31 us
  other arithmetic: 36.2 us -> 20.3 us
  local copies, waits for them, and re-layouts: 33.8 us -> 27 us
    pallas_call x4, Pallas kernels: 40.8 us -> 91.1 us  [the longest x1 67.8 us: finish(): pl.pallas_call(finish_kernel, out_shape=[jax.ShapeDtypeStruct((2, block,...]
    ppermute x9 -> x3, waiting for transfers between devices: 36.6 us -> 2.52 us  [plane_send(): return lax.ppermute(array, both, pairs)]
    ppermute x6 -> x0, starting transfers between devices: 20.7 us -> none  [line_send(): return lax.ppermute(array, both, pairs)]
    ppermute x6 -> x0, waiting for transfers between devices: 13.7 us -> none  [line_send(): return lax.ppermute(array, both, pairs)]
    ppermute x2 -> x1, waiting for transfers between devices: 0.01 us -> 12.3 us  [from_sequences(): odd_part = lax.ppermute(jnp.where(odd == 0, b, a), both, route(1, True))]
    ppermute x9 -> x3, starting transfers between devices: 14 us -> 5.62 us  [plane_send(): return lax.ppermute(array, both, pairs)]
    ppermute x2 -> x1, starting transfers between devices: 8.14 us -> 0.71 us  [from_sequences(): even_part = lax.ppermute(jnp.where(odd == 0, a, b), both, route(0, True))]
    add x2 -> x0, other arithmetic: 4.9 us -> none  [the longest x1 3.19 us: local(): feed = feed + plane_send(feed_sent[hop - 1], hop).astype(F32)]
  transfers between devices with their start and end apart: 32 -> 14, of which waited for: 9 -> 3; matrix products, arithmetic and copies ran while one was open for 14% -> 7% of each run, Pallas kernels for 43% -> 42%
where the time goes in v3:
time: 395 us; the launch traced here: 393 us
  Pallas kernels  296 us (75%)
  starting transfers between devices  31 us (8%)
  local copies, waits for them, and re-layouts  27 us (7%)
  other arithmetic  20.3 us (5%)
  waiting for transfers between devices  17.5 us (4%)
    pallas_call x1, Pallas kernels, gather_weights(): pl.pallas_call(functools.partial(gather_kernel, nz), out_shape=[jax.Shape...  70.9 us
    pallas_call x1, Pallas kernels, finish(): pl.pallas_call(finish_kernel, out_shape=[jax.ShapeDtypeStruct((2, block,...  67.8 us
    pallas_call x1, Pallas kernels, attend_back(): pl.pallas_call(attend_back_kernel, out_shape=[jax.ShapeDtypeStruct((rows,...  53.5 us
    pallas_call x1, Pallas kernels, row_local(): pl.pallas_call(rows_kernel, out_shape=[shape(width, BF16), shape(half, BF...  39.5 us
    pallas_call x1, Pallas kernels, attend(): pl.pallas_call(attend_kernel, out_shape=[jax.ShapeDtypeStruct((rows, widt...  31.6 us
    pallas_call x3, Pallas kernels, call(): pl.pallas_call(kernel, out_shape=[shape, shape], grid_spec=pltpu.Prefetch...  23.3 us
    unnamed x67, local copies, waits for them, and re-layouts  13 us
    ppermute x1, waiting for transfers between devices, from_sequences(): odd_part = lax.ppermute(jnp.where(odd == 0, b, a), both, route(1, True))  12.3 us
  transfers between devices with their start and end apart: 14, of which 3 were waited for; matrix products, arithmetic and copies ran while one was open for 7% of the time, Pallas kernels for 42%

profile of v3, /device:TPU:0, one launch (start us, length us, event | category | flops | bytes accessed | tf_op | source)
XLA Modules:
  0.0 393.0 jit_solution(14418906130564584774)
XLA Ops:
  0.7 1.6 select_bitcast_fusion.5
  3.1 3.0 collective-permute-start.1
  6.1 2.3 collective-permute-start.2
  8.4 1.2 select_bitcast_fusion.3
  9.7 7.4 %collective-permute-start.5 = (bf16[512,768]{1,0:T(8,128)(2,1)}, bf16[512,768]{1,0:T(8,128)(2,1)}, u32[]{:S(2)}, u32[]{:S(2)}) collective-permute-start(bf16[512,768]{1,0:T(8,128)(2,1)} %get-tuple-element.116), channel_id=1, source_target_pairs={{0,0},{1,16},{2,2},{3,18},{4,4},{5,20},{6,6},{7,22},{8,8},{9,24},{... | collective-permute-start | bytes 2359304 | tf_op jit(solution)/shard_map/ppermute | solution.py:1202
  19.7 2.7 collective-permute-done.1
  22.7 5.7 %collective-permute-start.3 = (bf16[1024,768]{1,0:T(8,128)(2,1)S(1)}, bf16[1024,768]{1,0:T(8,128)(2,1)S(1)}, u32[]{:S(2)}, u32[]{:S(2)}) collective-permute-start(bf16[1024,768]{1,0:T(8,128)(2,1)S(1)} %pad_maximum_fusion.own.x_ref), channel_id=1, source_target_pairs={{0,1},{1,0},{2,3},{3,2},{4,5},{5,4},{6,7},{7,6},{8,9},{9,8},{10,11... | collective-permute-start | bytes 4718600 | tf_op jit(solution)/shard_map/ppermute | solution.py:1196
  32.1 70.9 %gather_weights.1 = (bf16[8,392,768]{2,1,0:T(8,128)(2,1)}, bf16[8,4,192,768]{3,2,1,0:T(8,128)(2,1)}) custom-call(bf16[392,768]{1,0:T(8,128)(2,1)} %constant_dynamic-update-slice_fusion.square, bf16[4,192,768]{2,1,0:T(8,128)(2,1)} %pad_maximum_fusion.3.wide), custom_call_target="tpu_custom_call" | custom-call | bytes 157286400 | tf_op jit(solution)/shard_map/gather_weights/pallas_call | solution.py:187
  106.5 1.3 copy.46.seg_col
  108.8 1.2 copy-done.2
  110.1 9.6 %project.1 = (bf16[2048,384]{1,0:T(8,128)(2,1)}, bf16[2048,384]{1,0:T(8,128)(2,1)}, bf16[2048,384]{1,0:T(8,128)(2,1)}) custom-call(s32[1]{0:T(128)} %bitcast.core, bf16[1024,768]{1,0:T(8,128)(2,1)} %copy-done.1, bf16[1024,768]{1,0:T(8,128)(2,1)} %copy-done.2, bf16[8,392,768]{2,1,0:T(8,128)(2,1)} %get-tuple-element.55.wq.wk.wv.wo_mine_ref.wo_theirs_ref.square, ...), custom_call_target="tpu_custom_call" | custom-call | flops 3623878656 | bytes 10485760 | tf_op jit(solution)/shard_map/project/pallas_call | solution.py:238
  119.7 31.6 %attend.1 = (bf16[2048,384]{1,0:T(8,128)(2,1)}, f32[6,2048]{1,0:T(8,128)}) custom-call(s32[8]{0:T(128)} %get-tuple-element.149.low, s32[8]{0:T(128)} %get-tuple-element.146.high, bf16[2048,384]{1,0:T(8,128)(2,1)} %get-tuple-element.56.q_ref, bf16[2048,384]{1,0:T(8,128)(2,1)} %get-tuple-element.57.k_ref, bf16[2048,384]{1,0:T(8,128)(2,1)} %get-tuple-element.58.v_ref, ...), custom_call_target="tpu_custom_call" | custom-call | flops 6442450944 | bytes 8388608 | tf_op jit(solution)/shard_map/attend/pallas_call | solution.py:348
  151.3 2.4 constant_dynamic-slice_fusion
  155.9 1.5 broadcast_select_fusion.3
  157.4 1.2 pad_maximum_fusion.1.cot
  159.6 39.5 %row_local.1 = (bf16[1024,768]{1,0:T(8,128)(2,1)}, bf16[1024,384]{1,0:T(8,128)(2,1)}, bf16[1024,384]{1,0:T(8,128)(2,1)}, f32[1024,768]{1,0:T(8,128)}, bf16[1024,...) custom-call(s32[1]{0:T(128)} %bitcast.core, ...), custom_call_target="tpu_custom_call" | custom-call | flops 21743271936 | bytes 41943040 | tf_op jit(solution)/shard_map/row_local/pallas_call | solution.py:611
  199.2 9.5 %expand_grad.1 = (bf16[4,4,216,768]{3,2,1,0:T(8,128)(2,1)}, bf16[4,4,216,768]{3,2,1,0:T(8,128)(2,1)}) custom-call(s32[1]{0:T(128)} %bitcast.core, bf16[1024,768]{1,0:T(8,128)(2,1)} %get-tuple-element.66.low, bf16[1024,3072]{1,0:T(8,128)(2,1)} %get-tuple-element.67.ge), custom_call_target="tpu_custom_call" | custom-call | flops 4831838208 | bytes 14680064 | tf_op jit(solution)/shard_map/expand_grad/pallas_call | solution.py:739
  208.7 9.2 %reduce_grad.1 = (bf16[4,4,216,768]{3,2,1,0:T(8,128)(2,1)}, bf16[4,4,216,768]{3,2,1,0:T(8,128)(2,1)}) custom-call(s32[1]{0:T(128)} %bitcast.core, bf16[1024,3072]{1,0:T(8,128)(2,1)} %get-tuple-element.64.act, bf16[1024,768]{1,0:T(8,128)(2,1)} %get-tuple-element.65.gr, ...), custom_call_target="tpu_custom_call", output_to_operand_aliasing={{0}: (3, {}), {1}: (4, {})} | custom-call | flops 4831838208 | bytes 14680064 | tf_op jit(solution)/shard_map/reduce_grad/pallas_call | solution.py:739
  217.9 4.5 %output_grad.1 = (bf16[4,4,216,768]{3,2,1,0:T(8,128)(2,1)}, bf16[4,4,216,768]{3,2,1,0:T(8,128)(2,1)}) custom-call(s32[1]{0:T(128)} %bitcast.core, bf16[1024,384]{1,0:T(8,128)(2,1)} %get-tuple-element.119.mine, bf16[1024,384]{1,0:T(8,128)(2,1)} %copy-done.8, bf16[1024,768]{1,0:T(8,128)(2,1)} %get-tuple-element.63.gb, ...), custom_call_target="tpu_custom_call", output_to_operand_aliasing={{0}: (4, {}), {1}: (5, {})} | custom-call | flops 1207959552 | bytes 14680064 | tf_op jit(solution)/shard_map/output_grad/pallas_call | solution.py:739
  223.4 1.6 collective-permute-start.8
  225.0 2.8 collective-permute-start.10
  229.5 12.3 %collective-permute-done.8 = bf16[512,768]{1,0:T(8,128)(2,1)S(1)} collective-permute-done((bf16[512,768]{1,0:T(8,128)(2,1)S(1)}, bf16[512,768]{1,0:T(8,128)(2,1)S(1)}, u32[]{:S(2)}, u32[]{:S(2)}) %collective-permute-start.8) | collective-permute-done | bytes 786464 | tf_op jit(solution)/shard_map/ppermute | solution.py:1212
  241.9 1.3 pad_maximum_fusion.2
  243.2 1.7 copy-done
  244.8 4.2 %fusion.5 = (bf16[4,216,768]{2,1,0:T(8,128)(2,1)}, bf16[4,216,768]{2,1,0:T(8,128)(2,1)S(1)}, bf16[4,216,768]{2,1,0:T(8,128)(2,1)S(1)}) fusion(bf16[4,4,216,768]{3,2,1,0:T(8,128)(2,1)} %collective-permute-done.9, s32[]{:T(128)S(6)} %select_n.181, bf16[4,4,216,768]{3,2,1,0:T(8,128)(2,1)S(1)} %copy-done, s32[]{:T(128)S(6)} %select_n.180, s32[]{:T(128)S(6)} %select_n.179), kind=kLoop, calls=%fused_computation.12 | loop fusion | flops 7962624 | bytes 11943948 | tf_op jit(solution)/shard_map/convert_element_type | solution.py:1337
  249.1 4.6 %collective-permute-start.13 = (bf16[4,216,768]{2,1,0:T(8,128)(2,1)}, bf16[4,216,768]{2,1,0:T(8,128)(2,1)}, u32[]{:S(2)}, u32[]{:S(2)}) collective-permute-start(bf16[4,216,768]{2,1,0:T(8,128)(2,1)} %get-tuple-element.83), channel_id=1, source_target_pairs={{0,24},{1,25},{2,26},{3,27},{4,28},{5,29},{6,30},{7,31},{8,16},{9,... | collective-permute-start | bytes 3981320 | tf_op jit(solution)/shard_map/ppermute | solution.py:1326
  254.7 53.5 %attend_back.1 = (bf16[2048,384]{1,0:T(8,128)(2,1)}, bf16[2048,384]{1,0:T(8,128)(2,1)}, bf16[2048,384]{1,0:T(8,128)(2,1)}, f32[2,8,384]{2,1,0:T(8,128)}) custom-call(s32[1]{0:T(128)} %bitcast.core, s32[8]{0:T(128)} %get-tuple-element.150.low, s32[8]{0:T(128)} %get-tuple-element.145.high, bf16[2048,384]{1,0:T(8,128)(2,1)} %get-tuple-element.56.q_ref, ...), custom_call_target="tpu_custom_call" | custom-call | flops 16106127360 | bytes 16777216 | tf_op jit(solution)/shard_map/attend_back/pallas_call | solution.py:479
  309.9 2.5 collective-permute-done.12
  312.4 4.8 %fusion.2.feed = bf16[4,216,768]{2,1,0:T(8,128)(2,1)} fusion(bf16[4,216,768]{2,1,0:T(8,128)(2,1)} %collective-permute-done.13, bf16[4,216,768]{2,1,0:T(8,128)(2,1)} %collective-permute-done.12, bf16[4,216,768]{2,1,0:T(8,128)(2,1)} %collective-permute-done.11, bf16[4,4,216,768]{3,2,1,0:T(8,128)(2,1)} %collective-permute-done.9, s32[]{:T(128)S(6)} %select_n.182, ...), kind=kLoop, calls=%fused_computation.3 | loop fusion | flops 6635520 | bytes 7962628 | tf_op jit(solution)/shard_map/convert_element_type | solution.py:1342
  317.2 67.8 %finish.1 = (bf16[2,512,768]{2,1,0:T(8,128)(2,1)}, f32[3,96,768]{2,1,0:T(8,128)}, f32[96,3072]{1,0:T(8,128)}, f32[384,768]{1,0:T(8,128)}, f32[96,768]{1,0:T(8,128)}, /*index=5*/f32[8,256]{1,0:T(8,128)}) custom-call(bf16[1024,768]{1,0:T(8,128)(2,1)} %copy-done.1, bf16[1024,768]{1,0:T(8,128)(2,1)} %copy-done.2, bf16[2048,384]{1,0:T(8,128)(2,1)} %get-tuple-element.77.dq, ...), custom_call_target="tpu_custom_call" | custom-call | flops 7247757312 | bytes 157286400 | tf_op jit(solution)/shard_map/finish/pallas_call | solution.py:1054
  387.0 2.1 slice_bitcast_fusion
  389.1 1.1 copy.67
  (130 shorter events, 25.2 us)
Async XLA Ops:
  0.7 5.5 %copy-start.17 = (s32[2,2048]{1,0:T(2,128)S(1)}, s32[2,2048]{1,0:T(2,128)}, u32[]{:S(2)}) copy-start(s32[2,2048]{1,0:T(2,128)} %param.19) | copy-start | bytes 49156
  0.7 7.7 %copy-start.4 = (bf16[2,512,768]{2,1,0:T(8,128)(2,1)S(1)}, bf16[2,512,768]{2,1,0:T(8,128)(2,1)}, u32[]{:S(2)}) copy-start(bf16[2,512,768]{2,1,0:T(8,128)(2,1)} %param.20) | copy-start | bytes 4718596
  2.3 17.4 %collective-permute-start = (bf16[512,768]{1,0:T(8,128)(2,1)S(1)}, bf16[512,768]{1,0:T(8,128)(2,1)S(1)}, u32[]{:S(2)}, u32[]{:S(2)}) collective-permute-start(bf16[512,768]{1,0:T(8,128)(2,1)S(1)} %get-tuple-element.122), channel_id=1, source_target_pairs={{0,0},{1,16},{2,2},{3,18},{4,4},{5,20},{6,6},{7,22},{8,8},{9,24},{... | collective-permute-start | bytes 2359304 | tf_op jit(solution)/shard_map/ppermute | solution.py:1202
  3.0 14.7 %copy-start.18 = (bf16[384]{0:T(512)(128)(2,1)S(1)}, bf16[384]{0:T(512)(128)(2,1)}, u32[]{:S(2)}) copy-start(bf16[384]{0:T(512)(128)(2,1)} %param.30) | copy-start | bytes 2308
  3.0 14.7 %copy-start.19 = (bf16[96]{0:T(256)(128)(2,1)S(1)}, bf16[96]{0:T(256)(128)(2,1)}, u32[]{:S(2)}) copy-start(bf16[96]{0:T(256)(128)(2,1)} %param.27) | copy-start | bytes 580
  3.0 14.7 %copy-start.20 = (bf16[96]{0:T(256)(128)(2,1)S(1)}, bf16[96]{0:T(256)(128)(2,1)}, u32[]{:S(2)}) copy-start(bf16[96]{0:T(256)(128)(2,1)} %param.28) | copy-start | bytes 580
  3.0 14.7 %copy-start.21 = (bf16[96]{0:T(256)(128)(2,1)S(1)}, bf16[96]{0:T(256)(128)(2,1)}, u32[]{:S(2)}) copy-start(bf16[96]{0:T(256)(128)(2,1)} %param.29) | copy-start | bytes 580
  3.1 14.7 %copy-start.22 = (bf16[96]{0:T(256)(128)(2,1)S(1)}, bf16[96]{0:T(256)(128)(2,1)}, u32[]{:S(2)}) copy-start(bf16[96]{0:T(256)(128)(2,1)} %param.31) | copy-start | bytes 580
  3.1 14.7 %copy-start.23 = (bf16[96]{0:T(256)(128)(2,1)S(1)}, bf16[96]{0:T(256)(128)(2,1)}, u32[]{:S(2)}) copy-start(bf16[96]{0:T(256)(128)(2,1)} %param.32) | copy-start | bytes 580
  3.1 14.7 %copy-start.24 = (bf16[96]{0:T(256)(128)(2,1)S(1)}, bf16[96]{0:T(256)(128)(2,1)}, u32[]{:S(2)}) copy-start(bf16[96]{0:T(256)(128)(2,1)} %param.33) | copy-start | bytes 580
  3.1 14.7 %copy-start.25 = (bf16[96]{0:T(256)(128)(2,1)S(1)}, bf16[96]{0:T(256)(128)(2,1)}, u32[]{:S(2)}) copy-start(bf16[96]{0:T(256)(128)(2,1)} %param.34) | copy-start | bytes 580
  3.1 14.7 %copy-start.26 = (bf16[96]{0:T(256)(128)(2,1)S(1)}, bf16[96]{0:T(256)(128)(2,1)}, u32[]{:S(2)}) copy-start(bf16[96]{0:T(256)(128)(2,1)} %param.35) | copy-start | bytes 580
  3.1 15.9 %copy-start.11 = (bf16[96,768]{1,0:T(8,128)(2,1)S(1)}, bf16[96,768]{1,0:T(8,128)(2,1)}, u32[]{:S(2)}) copy-start(bf16[96,768]{1,0:T(8,128)(2,1)} %param.21) | copy-start | bytes 442372
  3.1 19.3 %collective-permute-start.1 = (bf16[512,768]{1,0:T(8,128)(2,1)S(1)}, bf16[512,768]{1,0:T(8,128)(2,1)S(1)}, u32[]{:S(2)}, u32[]{:S(2)}) collective-permute-start(bf16[512,768]{1,0:T(8,128)(2,1)S(1)} %get-tuple-element.123), channel_id=1, source_target_pairs={{0,8},{1,24},{2,10},{3,26},{4,12},{5,28},{6,14},{7,30},{8,0},{9,16... | collective-permute-start | bytes 2359304 | tf_op jit(solution)/shard_map/ppermute | solution.py:1203
  6.1 99.2 %collective-permute-start.2 = (s32[2,2048]{1,0:T(2,128)S(1)}, s32[2,2048]{1,0:T(2,128)S(1)}, u32[]{:S(2)}, u32[]{:S(2)}) collective-permute-start(s32[2,2048]{1,0:T(2,128)S(1)} %copy-done.17), channel_id=1, source_target_pairs={{0,1},{1,0},{2,3},{3,2},{4,5},{5,4},{6,7},{7,6},{8,9},{9,8},{10,11... | collective-permute-start | bytes 49160 | tf_op jit(solution)/shard_map/ppermute | solution.py:1196
  9.7 146.3 %collective-permute-start.5 = (bf16[512,768]{1,0:T(8,128)(2,1)}, bf16[512,768]{1,0:T(8,128)(2,1)}, u32[]{:S(2)}, u32[]{:S(2)}) collective-permute-start(bf16[512,768]{1,0:T(8,128)(2,1)} %get-tuple-element.116), channel_id=1, source_target_pairs={{0,0},{1,16},{2,2},{3,18},{4,4},{5,20},{6,6},{7,22},{8,8},{9,24},{... | collective-permute-start | bytes 2359304 | tf_op jit(solution)/shard_map/ppermute | solution.py:1202
  17.1 138.9 %collective-permute-start.6 = (bf16[512,768]{1,0:T(8,128)(2,1)}, bf16[512,768]{1,0:T(8,128)(2,1)}, u32[]{:S(2)}, u32[]{:S(2)}) collective-permute-start(bf16[512,768]{1,0:T(8,128)(2,1)} %get-tuple-element.117), channel_id=1, source_target_pairs={{0,8},{1,24},{2,10},{3,26},{4,12},{5,28},{6,14},{7,30},{8,0},{9,16... | collective-permute-start | bytes 2359304 | tf_op jit(solution)/shard_map/ppermute | solution.py:1203
  22.5 5.9 %copy-start.12 = (bf16[96,768]{1,0:T(8,128)(2,1)S(1)}, bf16[96,768]{1,0:T(8,128)(2,1)}, u32[]{:S(2)}) copy-start(bf16[96,768]{1,0:T(8,128)(2,1)} %param.22) | copy-start | bytes 442372
  22.5 6.6 %copy-start.13 = (bf16[96,768]{1,0:T(8,128)(2,1)S(1)}, bf16[96,768]{1,0:T(8,128)(2,1)}, u32[]{:S(2)}) copy-start(bf16[96,768]{1,0:T(8,128)(2,1)} %param.23) | copy-start | bytes 442372
  22.5 7.2 %copy-start.14 = (bf16[96,768]{1,0:T(8,128)(2,1)S(1)}, bf16[96,768]{1,0:T(8,128)(2,1)}, u32[]{:S(2)}) copy-start(bf16[96,768]{1,0:T(8,128)(2,1)} %param.24) | copy-start | bytes 442372
  22.6 8.5 %copy-start.9 = (bf16[384,768]{1,0:T(8,128)(2,1)S(1)}, bf16[384,768]{1,0:T(8,128)(2,1)}, u32[]{:S(2)}) copy-start(bf16[384,768]{1,0:T(8,128)(2,1)} %param.26) | copy-start | bytes 1769476
  22.7 9.4 %copy-start.1 = (bf16[1024,768]{1,0:T(8,128)(2,1)}, bf16[1024,768]{1,0:T(8,128)(2,1)S(1)}, u32[]{:S(2)}) copy-start(bf16[1024,768]{1,0:T(8,128)(2,1)S(1)} %pad_maximum_fusion.own.x_ref) | copy-start | bytes 4718596
  22.7 86.1 %collective-permute-start.3 = (bf16[1024,768]{1,0:T(8,128)(2,1)S(1)}, bf16[1024,768]{1,0:T(8,128)(2,1)S(1)}, u32[]{:S(2)}, u32[]{:S(2)}) collective-permute-start(bf16[1024,768]{1,0:T(8,128)(2,1)S(1)} %pad_maximum_fusion.own.x_ref), channel_id=1, source_target_pairs={{0,1},{1,0},{2,3},{3,2},{4,5},{5,4},{6,7},{7,6},{8,9},{9,8},{10,11... | collective-permute-start | bytes 4718600 | tf_op jit(solution)/shard_map/ppermute | solution.py:1196
  153.7 5.0 %collective-permute-start.4 = (bf16[1024,384]{1,0:T(8,128)(2,1)S(1)}, bf16[1024,384]{1,0:T(8,128)(2,1)S(1)}, u32[]{:S(2)}, u32[]{:S(2)}) collective-permute-start(bf16[1024,384]{1,0:T(8,128)(2,1)S(1)} %get-tuple-element.118), channel_id=1, source_target_pairs={{0,1},{1,0},{2,3},{3,2},{4,5},{5,4},{6,7},{7,6},{8,9},{9,8},{10,11... | collective-permute-start | bytes 2359304 | tf_op jit(solution)/shard_map/ppermute | solution.py:1196
  222.4 20.7 %collective-permute-start.9 = (bf16[4,4,216,768]{3,2,1,0:T(8,128)(2,1)}, bf16[4,4,216,768]{3,2,1,0:T(8,128)(2,1)}, u32[]{:S(2)}, u32[]{:S(2)}) collective-permute-start(bf16[4,4,216,768]{3,2,1,0:T(8,128)(2,1)} %get-tuple-element.73), channel_id=1, source_target_pairs={{0,1},{1,0},{2,3},{3,2},{4,5},{5,4},{6,7},{7,6},{8,9},{9,8},{10,11... | collective-permute-start | bytes 15925256 | tf_op jit(solution)/shard_map/ppermute | solution.py:1196
  222.6 6.2 %copy-start.16 = (f32[1,3072]{1,0:T(1,128)S(1)}, f32[1,3072]{1,0:T(1,128)}, u32[]{:S(2)}) copy-start(f32[1,3072]{1,0:T(1,128)} %get-tuple-element.86) | copy-start | bytes 36868
  222.7 6.8 %collective-permute-start.7 = (bf16[512,768]{1,0:T(8,128)(2,1)S(1)}, bf16[512,768]{1,0:T(8,128)(2,1)S(1)}, u32[]{:S(2)}, u32[]{:S(2)}) collective-permute-start(bf16[512,768]{1,0:T(8,128)(2,1)S(1)} %get-tuple-element.112), channel_id=1, source_target_pairs={{0,0},{16,1},{2,2},{18,3},{4,4},{20,5},{6,6},{22,7},{8,8},{24,9},{... | collective-permute-start | bytes 2359304 | tf_op jit(solution)/shard_map/ppermute | solution.py:1211
  223.4 18.4 %collective-permute-start.8 = (bf16[512,768]{1,0:T(8,128)(2,1)S(1)}, bf16[512,768]{1,0:T(8,128)(2,1)S(1)}, u32[]{:S(2)}, u32[]{:S(2)}) collective-permute-start(bf16[512,768]{1,0:T(8,128)(2,1)S(1)} %get-tuple-element.113), channel_id=1, source_target_pairs={{8,0},{24,1},{10,2},{26,3},{12,4},{28,5},{14,6},{30,7},{0,8},{16,9... | collective-permute-start | bytes 2359304 | tf_op jit(solution)/shard_map/ppermute | solution.py:1212
  225.0 24.1 %collective-permute-start.10 = (bf16[1024,384]{1,0:T(8,128)(2,1)}, bf16[1024,384]{1,0:T(8,128)(2,1)}, u32[]{:S(2)}, u32[]{:S(2)}) collective-permute-start(bf16[1024,384]{1,0:T(8,128)(2,1)} %get-tuple-element.74), channel_id=1, source_target_pairs={{0,1},{1,0},{2,3},{3,2},{4,5},{5,4},{6,7},{7,6},{8,9},{9,8},{10,11... | collective-permute-start | bytes 2359304 | tf_op jit(solution)/shard_map/ppermute | solution.py:1196
  249.1 60.8 %collective-permute-start.13 = (bf16[4,216,768]{2,1,0:T(8,128)(2,1)}, bf16[4,216,768]{2,1,0:T(8,128)(2,1)}, u32[]{:S(2)}, u32[]{:S(2)}) collective-permute-start(bf16[4,216,768]{2,1,0:T(8,128)(2,1)} %get-tuple-element.83), channel_id=1, source_target_pairs={{0,24},{1,25},{2,26},{3,27},{4,28},{5,29},{6,30},{7,31},{8,16},{9,... | collective-permute-start | bytes 3981320 | tf_op jit(solution)/shard_map/ppermute | solution.py:1326
  253.6 58.7 %collective-permute-start.12 = (bf16[4,216,768]{2,1,0:T(8,128)(2,1)S(1)}, bf16[4,216,768]{2,1,0:T(8,128)(2,1)}, u32[]{:S(2)}, u32[]{:S(2)}) collective-permute-start(bf16[4,216,768]{2,1,0:T(8,128)(2,1)S(1)} %get-tuple-element.82), channel_id=1, source_target_pairs={{0,16},{1,17},{2,18},{3,19},{4,20},{5,21},{6,22},{7,23},{8,24},{9,... | collective-permute-start | bytes 3981320 | tf_op jit(solution)/shard_map/ppermute | solution.py:1326
  253.7 58.7 %collective-permute-start.11 = (bf16[4,216,768]{2,1,0:T(8,128)(2,1)S(1)}, bf16[4,216,768]{2,1,0:T(8,128)(2,1)}, u32[]{:S(2)}, u32[]{:S(2)}) collective-permute-start(bf16[4,216,768]{2,1,0:T(8,128)(2,1)S(1)} %get-tuple-element.81), channel_id=1, source_target_pairs={{0,8},{1,9},{2,10},{3,11},{4,12},{5,13},{6,14},{7,15},{8,0},{9,1},... | collective-permute-start | bytes 3981320 | tf_op jit(solution)/shard_map/ppermute | solution.py:1326
  (9 other events, 24.1 us)

commit v4 on v3

--- a/solution.py
+++ b/solution.py
@@ -14,6 +14,7 @@
 PREPARE = 512
 DOCS = 8
 ROWS = 256
+WIDE_ROWS = 512
 MASKED = -1e30
 EPS = 1e-05
 UNITS = 8
@@ -48,38 +49,59 @@
 
 
 def gather_kernel(
-    nz, square, wide, square_all, wide_all,
+    nz, wq, wk, wv, wo, expand, reduce, small, tokens, cotangent, ids,
+    square_all, wide_all, own, other, cot, segments,
     z_send, z_recv, p_send, p_recv, c_send, c_recv, own_send, own_recv, copied,
+    row_send, row_recv, row_kept, twin_send, twin_recv, id_sems,
+    square_here, wide_here, rows_here, ids_here, brought,
 ):
     r, s = lax.axis_index("rep"), lax.axis_index("shard")
-    z = s // 2
+    z, core = s // 2, s % 2
+    odd = r % 2
+    home = r // 2 == core
     twin = (r, s ^ 1)
     barrier = pltpu.get_barrier_semaphore()
+    mesh_id = pl.DeviceIdType.MESH
 
     def greet(device):
-        pl.semaphore_signal(barrier, 1, device_id=device, device_id_type=pl.DeviceIdType.MESH)
-
-    greet(twin)
-    for k in (1, 2, 3):
-        greet((r ^ k, s))
+        pl.semaphore_signal(barrier, 1, device_id=device, device_id_type=mesh_id)
+
+    for device in [twin, (r ^ 2, s ^ 1), (r ^ 3, s ^ 1)] + [(r ^ k, s) for k in (1, 2, 3)]:
+        greet(device)
     for step in (1, -1):
 
         @pl.when((z + step >= 0) & (z + step < nz))
         def _(step=step):
             greet((r, s + 2 * step))
 
-    pl.semaphore_wait(barrier, 4 + jnp.where(z > 0, 1, 0) + jnp.where(z < nz - 1, 1, 0))
+    pl.semaphore_wait(barrier, 6 + jnp.where(z > 0, 1, 0) + jnp.where(z < nz - 1, 1, 0))
 
     def copy(source, target, sent, got, device):
         return pltpu.make_async_remote_copy(
-            source, target, sent, got, device_id=device, device_id_type=pl.DeviceIdType.MESH
-        )
-
+            source, target, sent, got, device_id=device, device_id_type=mesh_id
+        )
+
+    block = tokens.shape[1]
+    unit, width = wq.shape
+    square, wide = square_here, wide_here
+    pairs = [(small, square.at[pl.ds(4 * unit, EXTRA)])]
+    pairs += [(m, square.at[pl.ds(n * unit, unit)]) for n, m in enumerate((wq, wk, wv, wo))]
+    for n in range(wide.shape[0]):
+        pairs.append((expand.at[:, pl.ds(n * width, width)], wide.at[n, pl.ds(0, unit)]))
+        pairs.append((reduce.at[pl.ds(n * unit, unit)], wide.at[n, pl.ds(unit, unit)]))
+    weights = len(pairs)
+    pairs.append((tokens.at[odd], rows_here.at[0]))
+    pairs.append((cotangent.at[odd], rows_here.at[1]))
+    pairs.append((ids.at[odd], ids_here))
+    fetched = [
+        pltpu.make_async_copy(source, target, brought.at[n])
+        for n, (source, target) in enumerate(pairs)
+    ]
     kept = [
-        pltpu.make_async_copy(square, square_all.at[s], copied.at[0]),
-        pltpu.make_async_copy(wide, wide_all.at[s], copied.at[1]),
+        pltpu.make_async_copy(square_here, square_all.at[s], copied.at[0]),
+        pltpu.make_async_copy(wide_here, wide_all.at[s], copied.at[1]),
     ]
-    own = [
+    mine = [
         copy(square, square_all.at[s], own_send.at[0], own_recv.at[0], twin),
         copy(wide, wide_all.at[s], own_send.at[1], own_recv.at[1], twin),
     ]
@@ -95,10 +117,15 @@
             target = wide_all.at[at, r]
         return copy(source, target, z_send.at[n, d, part], z_recv.at[n, d, part], (r, s + 2 * step))
 
-    def sideways(n, d, k):
+    turns = [(0, 0, 1), (0, 0, 2), (0, 1, 2), (1, 0, 2), (1, 0, 1), (1, 2, 1)]
+
+    def sideways(n, d, which):
         at = s - 2 * (1 - 2 * n) * d
-        part = wide_all.at[at, r]
-        return copy(part, part, p_send.at[n, d - 1, k - 1], p_recv.at[n, d - 1, k - 1], (r ^ k, s))
+        half, whose, to = turns[which]
+        part = wide_all.at[at, r ^ whose, pl.ds(half * unit, unit)]
+        return copy(
+            part, part, p_send.at[n, d - 1, which], p_recv.at[n, d - 1, which], (r ^ to, s)
+        )
 
     def across(n, d, k):
         at = s - 2 * (1 - 2 * n) * d
@@ -113,6 +140,38 @@
         at = z + 1 - 2 * n
         return (at >= 0) & (at < nz)
 
+    def stay(target, which):
+        at = pl.ds(pl.multiple_of(odd * block, block), block)
+        return pltpu.make_async_copy(rows_here.at[which], target.at[at], row_kept.at[which])
+
+    def move(source, target, which, turn, device):
+        at = pl.ds(pl.multiple_of(odd * block, block), block)
+        return copy(
+            source.at[odd ^ turn],
+            target.at[at],
+            row_send.at[which, turn],
+            row_recv.at[which, turn],
+            device,
+        )
+
+    def rows_act(source, target, which, act_kept, act_moved):
+        @pl.when(home)
+        def _():
+            if act_kept:
+                act_kept(stay(target, which))
+            act_moved(move(source, target, which, 1, (r ^ 1, s)))
+
+        @pl.when(jnp.logical_not(home))
+        def _():
+            act_moved(move(source, target, which, 0, (r ^ 2, s ^ 1)))
+            act_moved(move(source, target, which, 1, (r ^ 3, s ^ 1)))
+
+    begin = lambda c: c.start()
+    for c in fetched:
+        c.start()
+    rows_act(tokens, own, 0, None, begin)
+    for c in fetched[:weights]:
+        c.wait()
     for n in (0, 1):
 
         @pl.when(goes(n))
@@ -120,13 +179,29 @@
             onward(n, 0, 1).start()
             onward(n, 0, 0).start()
 
-    for c in own + kept:
+    id_kept = pltpu.make_async_copy(ids_here, segments, id_sems.at[0])
+    id_sent = copy(ids.at[odd], segments, id_sems.at[1], id_sems.at[2], twin)
+
+    @pl.when(home)
+    def _():
+        id_sent.start()
+
+    for c in mine + kept:
         c.start()
-    for d in range(1, nz):
+    for c in fetched[weights:]:
+        c.wait()
+
+    @pl.when(home)
+    def _():
+        id_kept.start()
+        stay(own, 0).start()
+        stay(cot, 1).start()
+
+    def arrivals(d):
         for n in (0, 1):
 
             @pl.when(has(n, d))
-            def _(n=n, d=d):
+            def _(n=n):
                 onward(n, d - 1, 1).wait_recv()
                 if d < nz - 1:
 
@@ -134,8 +209,8 @@
                     def _():
                         onward(n, d, 1).start()
 
-                for k in (1, 2, 3):
-                    sideways(n, d, k).start()
+                for which in (0, 3, 1, 4):
+                    sideways(n, d, which).start()
                 across(n, d, 0).start()
                 onward(n, d - 1, 0).wait_recv()
                 if d < nz - 1:
@@ -146,17 +221,68 @@
 
                 across(n, d, 4).start()
 
+    def hand_on(turn):
+        at = pl.ds(pl.multiple_of((odd ^ turn) * block, block), block)
+        return copy(own.at[at], other.at[at], twin_send.at[turn], twin_recv.at[turn], twin)
+
+    def relays(d):
+        for n in (0, 1):
+
+            @pl.when(has(n, d))
+            def _(n=n):
+                sideways(n, d, 0).wait_recv()
+                sideways(n, d, 2).start()
+                sideways(n, d, 3).wait_recv()
+                sideways(n, d, 5).start()
+                sideways(n, d, 4).wait_recv()
+                across(n, d, 1).start()
+                sideways(n, d, 1).wait_recv()
+                across(n, d, 2).start()
+
+    arrivals(1)
+
+    @pl.when(home)
+    def _():
+        stay(own, 0).wait()
+
+    @pl.when(jnp.logical_not(home))
+    def _():
+        move(tokens, own, 0, 0, (r ^ 2, s ^ 1)).wait_recv()
+
+    hand_on(0).start()
+    move(tokens, own, 0, 1, (r ^ 1, s)).wait_recv()
+    hand_on(1).start()
+    relays(1)
+    rows_act(cotangent, cot, 1, None, begin)
+    for d in range(2, nz):
+        arrivals(d)
+        relays(d)
     for d in range(1, nz):
         for n in (0, 1):
 
             @pl.when(has(n, d))
             def _(n=n, d=d):
-                for k in (1, 2, 3):
-                    sideways(n, d, k).wait_recv()
-                    across(n, d, k).start()
-
-    for c in own + kept:
+                sideways(n, d, 2).wait_recv()
+                sideways(n, d, 5).wait_recv()
+                across(n, d, 3).start()
+
+    def sent(c):
+        c.wait_send()
+
+    rows_act(tokens, own, 0, None, sent)
+    rows_act(cotangent, cot, 1, lambda c: c.wait(), lambda c: c.wait())
+    for c in mine + kept + [hand_on(0), hand_on(1)]:
         c.wait()
+
+    @pl.when(home)
+    def _():
+        id_kept.wait()
+        id_sent.wait_send()
+
+    @pl.when(jnp.logical_not(home))
+    def _():
+        id_sent.wait_recv()
+
     for n in (0, 1):
 
         @pl.when(goes(n))
@@ -169,8 +295,8 @@
 
             @pl.when(has(n, d))
             def _(n=n, d=d):
-                for k in (1, 2, 3):
-                    sideways(n, d, k).wait_send()
+                for which in range(6):
+                    sideways(n, d, which).wait_send()
                 for k in range(5):
                     across(n, d, k).wait()
                 if d < nz - 1:
@@ -181,47 +307,66 @@
                         onward(n, d, 0).wait_send()
 
 
-def gather_weights(square, wide, nz):
+def gather(matrices, small, tokens, cotangent, ids, nz):
     anywhere = pl.BlockSpec(memory_space=pl.ANY)
     sems = lambda *shape: pltpu.SemaphoreType.DMA(shape)
+    unit, width = matrices[0].shape
+    chunks = matrices[4].shape[1] // width
+    square, wide = (4 * unit + EXTRA, width), (chunks, 2 * unit, width)
+    rows = jax.ShapeDtypeStruct((2 * tokens.shape[1], tokens.shape[2]), BF16)
     return pl.pallas_call(
         functools.partial(gather_kernel, nz),
         out_shape=[
-            jax.ShapeDtypeStruct((2 * nz,) + square.shape, BF16),
-            jax.ShapeDtypeStruct((2 * nz,) + wide.shape, BF16),
+            jax.ShapeDtypeStruct((2 * nz,) + square, BF16),
+            jax.ShapeDtypeStruct((2 * nz,) + wide, BF16),
+            rows,
+            rows,
+            rows,
+            jax.ShapeDtypeStruct(ids.shape[1:], jnp.int32),
         ],
-        in_specs=[anywhere] * 2,
-        out_specs=[anywhere] * 2,
+        in_specs=[anywhere] * 10,
+        out_specs=[anywhere] * 6,
         scratch_shapes=[
             sems(2, nz - 1, 2),
             sems(2, nz - 1, 2),
-            sems(2, nz - 1, 3),
-            sems(2, nz - 1, 3),
+            sems(2, nz - 1, 6),
+            sems(2, nz - 1, 6),
             sems(2, nz - 1, 5),
             sems(2, nz - 1, 5),
             sems(2),
             sems(2),
             sems(2),
+            sems(2, 2),
+            sems(2, 2),
+            sems(2),
+            sems(2),
+            sems(2),
+            sems(3),
+            pltpu.VMEM(square, BF16),
+            pltpu.VMEM(wide, BF16),
+            pltpu.VMEM((2,) + tokens.shape[1:], BF16),
+            pltpu.VMEM(ids.shape[1:], jnp.int32),
+            sems(8 + 2 * chunks),
         ],
         compiler_params=params(collective_id=0, has_side_effects=True),
         cost_estimate=pl.CostEstimate(flops=0, bytes_accessed=150 << 20, transcendentals=0),
-        name="gather_weights",
-    )(square, wide)
-
-
-def qkv_kernel(core, own, other, wq, wk, wv, bq, bv, q_out, k_out, v_out):
+        name="gather",
+    )(*matrices, small, tokens, cotangent, ids)
+
+
+def qkv_kernel(core, own, other, wq, wk, wv, vectors, q_out, k_out, v_out):
     per_core = pl.num_programs(0) // 2
     mine = pl.program_id(0) // per_core == core[0]
     rows = jnp.where(mine, own[...], other[...])
-    q_out[...] = (dot(rows, stacked(wq)) + bq[...]).astype(BF16)
+    q_out[...] = (dot(rows, stacked(wq)) + vectors[0:1, :]).astype(BF16)
     k_out[...] = dot(rows, stacked(wk)).astype(BF16)
-    v_out[...] = (dot(rows, stacked(wv)) + bv[...]).astype(BF16)
-
-
-def project(core, own, other, square, bq, bv):
+    v_out[...] = (dot(rows, stacked(wv)) + vectors[1:2, :]).astype(BF16)
+
+
+def project(core, own, other, square, vectors):
     rows, width = own.shape
     half = width // 2
-    steps = rows // ROWS
+    steps = rows // WIDE_ROWS
 
     def side(flip):
         def index(i, core):
@@ -233,8 +378,8 @@
     weight = lambda m: pl.BlockSpec(
         (UNITS, width // UNITS, half), lambda i, core: (0, m, core[0])
     )
-    bias = pl.BlockSpec((1, half), lambda i, core: (0, core[0]))
-    result = pl.BlockSpec((ROWS, half), lambda i, core: (i, 0))
+    bias = pl.BlockSpec((8, half), lambda i, core: (0, core[0]))
+    result = pl.BlockSpec((WIDE_ROWS, half), lambda i, core: (i, 0))
     return pl.pallas_call(
         qkv_kernel,
         out_shape=[jax.ShapeDtypeStruct((2 * rows, half), BF16)] * 3,
@@ -242,12 +387,11 @@
             num_scalar_prefetch=1,
             grid=(2 * steps,),
             in_specs=[
-                pl.BlockSpec((ROWS, width), side(0)),
-                pl.BlockSpec((ROWS, width), side(1)),
+                pl.BlockSpec((WIDE_ROWS, width), side(0)),
+                pl.BlockSpec((WIDE_ROWS, width), side(1)),
                 weight(0),
                 weight(1),
                 weight(2),
-                bias,
                 bias,
             ],
             out_specs=[result] * 3,
@@ -257,7 +401,7 @@
             flops=2 * 2 * rows * width * 3 * half, bytes_accessed=10 << 20, transcendentals=0
         ),
         name="project",
-    )(core, own, other, square, square, square, bq, bv)
+    )(core, own, other, square, square, square, vectors)
 
 
 def halves(pair):
@@ -276,23 +420,28 @@
 
 
 def same_document(ids, extra_lanes):
-    slot = lax.broadcasted_iota(jnp.int32, (ids.shape[0], 2 * HEAD_DIM), 1) % HEAD_DIM
-    hit = slot == ids
+    size = ids.shape[1]
+    number = lax.broadcasted_iota(jnp.int32, (2 * DOCS, size), 0)
+    hit = jnp.where(number == ids, 1.0, 0.0).astype(BF16)
+    lane = lax.broadcasted_iota(jnp.int32, (2 * DOCS, 2 * HEAD_DIM), 1) % HEAD_DIM
+    spread = lane == lax.broadcasted_iota(jnp.int32, (2 * DOCS, 2 * HEAD_DIM), 0)
+    for_queries = dot_left(hit, jnp.where(spread, 1.0, 0.0).astype(BF16))
+    slot = lax.broadcasted_iota(jnp.int32, (size, 2 * HEAD_DIM), 1) % HEAD_DIM
     for_keys = jnp.where(
-        (slot < DOCS) & ~hit,
+        (slot < DOCS) & (for_queries == 0.0),
         MASKED,
         jnp.where((slot >= DOCS) & (slot < DOCS + extra_lanes), 1.0, 0.0),
     )
-    return jnp.where(hit, 1.0, 0.0), for_keys.astype(BF16)
-
-
-def attend_kernel(low, high, q_ref, k_ref, v_ref, seg_col, out, lse, qx, kx, v_turned, top, mix, kept):
+    return for_queries, for_keys.astype(BF16)
+
+
+def attend_kernel(low, high, q_ref, k_ref, v_ref, segments, out, lse, qx, kx, v_turned, top, mix, kept):
     rows, width = q_ref.shape
     heads = width // HEAD_DIM
     pairs = heads // 2
     for at in range(0, rows, PREPARE):
         part = pl.ds(at, PREPARE)
-        for_queries, for_keys = same_document(seg_col[part, :], 0)
+        for_queries, for_keys = same_document(segments[:, part], 0)
         for_queries = for_queries.astype(BF16)
         for pair in range(pairs):
             cols = pl.ds(pair * 2 * HEAD_DIM, 2 * HEAD_DIM)
@@ -340,7 +489,7 @@
     return begin // size, (end + size - 1) // size
 
 
-def attend(begin, end, q, k, v, seg_col):
+def attend(begin, end, q, k, v, segments):
     rows, width = q.shape
     heads = width // HEAD_DIM
     whole = lambda shape: pl.BlockSpec(shape, lambda i, *_: (0,) * len(shape))
@@ -354,7 +503,7 @@
         grid_spec=pltpu.PrefetchScalarGridSpec(
             num_scalar_prefetch=2,
             grid=(1,),
-            in_specs=[whole((rows, width))] * 3 + [whole((rows, 1))],
+            in_specs=[whole((rows, width))] * 3 + [whole((1, rows))],
             out_specs=[whole((rows, width)), whole((heads, rows))],
             scratch_shapes=[
                 wide,
@@ -372,7 +521,7 @@
             transcendentals=rows * rows * heads // 2,
         ),
         name="attend",
-    )(*spans(begin, end, KEYS), q, k, v, seg_col)
+    )(*spans(begin, end, KEYS), q, k, v, segments)
 
 
 def three_parts(values):
@@ -383,7 +532,7 @@
 
 
 def attend_back_kernel(
-    core, low, high, q_ref, k_ref, v_ref, out_ref, own, other, lse, seg_col,
+    core, low, high, q_ref, k_ref, v_ref, out_ref, own, other, lse, segments,
     dq_out, dk_out, dv_out, sums, grad, qx, kx, vx, gx, dq, dk, dv, weights, slopes,
 ):
     rows, width = q_ref.shape
@@ -410,7 +559,7 @@
     ).astype(BF16)
     for at in range(0, rows, PREPARE):
         part = pl.ds(at, PREPARE)
-        for_queries, for_keys = same_document(seg_col[part, :], 3)
+        for_queries, for_keys = same_document(segments[:, part], 3)
         ones = jnp.where(for_keys == 1.0, for_keys, jnp.zeros_like(for_keys))
         level = jnp.concatenate(
             [lse[:, part] * (-1.0 / SCALE2), jnp.zeros((8 - heads, PREPARE), F32)]
@@ -471,7 +620,7 @@
     sums[1] = dot(ones, dv_out[...])
 
 
-def attend_back(core, begin, end, q, k, v, out, own, other, lse, seg_col):
+def attend_back(core, begin, end, q, k, v, out, own, other, lse, segments):
     rows, width = q.shape
     heads = width // HEAD_DIM
     whole = lambda shape: pl.BlockSpec(shape, lambda i, *_: (0,) * len(shape))
@@ -485,7 +634,7 @@
             grid=(1,),
             in_specs=[whole((rows, width))] * 4
             + [whole((rows // 2, width))] * 2
-            + [whole((heads, rows)), whole((rows, 1))],
+            + [whole((heads, rows)), whole((1, rows))],
             out_specs=[whole((rows, width))] * 3 + [whole((2, 8, width))],
             scratch_shapes=[
                 pltpu.VMEM((rows, width), BF16),
@@ -507,7 +656,7 @@
             transcendentals=rows * rows * heads // 2,
         ),
         name="attend_back",
-    )(core, *spans(begin, end, BLOCK), q, k, v, out, own, other, lse, seg_col)
+    )(core, *spans(begin, end, BLOCK), q, k, v, out, own, other, lse, segments)
 
 
 def row_mean(values):
@@ -539,8 +688,8 @@
     each = UNITS // chunks
     we = lambda j: wide_ref[:, j, :unit, :].reshape(width, width)
     wr = lambda j: wide_ref[each * j : each * (j + 1), :, unit:, :].reshape(width, width)
-    bo, br = vectors[0:1, :], vectors[1:2, :]
-    gain1, shift1, gain2, shift2 = [vectors[n : n + 1, :] for n in range(2, 6)]
+    bo, br = vectors[2:3, :], vectors[3:4, :]
+    gain1, shift1, gain2, shift2 = [vectors[n : n + 1, :] for n in range(4, 8)]
     wo_mine, wo_theirs = stacked(wo_mine_ref), stacked(wo_theirs_ref)
 
     @pl.when(pl.program_id(0) == 0)
@@ -694,116 +843,166 @@
     return keep.astype(BF16), send.astype(BF16)
 
 
-def expand_grad_kernel(core, low, ge, keep, send):
-    nz, unit = keep.shape[1], keep.shape[2]
-    whole = dot_left(low[...], ge[...]).reshape(nz, 2, unit, -1)
-    kept, sent = split_cores(core[0], whole, 1)
-    keep[...] = kept.reshape(keep.shape)
-    send[...] = sent.reshape(send.shape)
-
-
-def reduce_grad_kernel(core, act, gr, keep_in, send_in, keep, send):
-    unit = keep.shape[2]
-    whole = dot_left(act[...], gr[...]).reshape(2, 4, unit, -1)
-    kept, sent = split_cores(core[0], whole, 0)
-    keep[...] = kept.reshape(keep.shape)
-    send[...] = sent.reshape(send.shape)
-
-
-def output_grad_kernel(core, mine, theirs, gb, keep_in, send_in, keep, send):
-    quarter = keep.shape[2]
-    from_mine, from_theirs = dot_left(mine[...], gb[...]), dot_left(theirs[...], gb[...])
-    first = jnp.where(core[0] == 0, from_mine, from_theirs)
-    second = jnp.where(core[0] == 0, from_theirs, from_mine)
-    whole = jnp.concatenate([first, second]).reshape(keep.shape[1], 2, 4, quarter, -1)
-    kept, sent = split_cores(core[0], whole, 1)
+def feed_kernel(
+    low, ge, act, gr, mine, theirs, gb, part0, part1, part2, part3,
+    left, wide_left, wide_right, right, narrow, keep, send, got, keep_o, send_o, got_o,
+    loads, core_s, core_r,
+):
+    r, s = lax.axis_index("rep"), lax.axis_index("shard")
+    core = s % 2
+    twin = (r, s ^ 1)
+    rows, width = low.shape
+    chunks = wide_left.shape[0]
+    nz, unit, quarter = keep.shape[1], keep.shape[2] // 2, keep_o.shape[2]
+    half = width // 2
+    load = lambda source, target, n: pltpu.make_async_copy(source, target, loads.at[n])
+    chunk = lambda ref, u: ref.at[:, pl.ds(pl.multiple_of(u * width, width), width)]
+    act_load = lambda u: load(chunk(act, u), wide_left.at[u], u)
+    ge_load = lambda u: load(chunk(ge, u), wide_right.at[u], chunks + u)
+    others = [
+        load(gr, right.at[0], 2 * chunks),
+        load(low, left, 2 * chunks + 1),
+        load(mine, narrow.at[0], 2 * chunks + 2),
+        load(theirs, narrow.at[1], 2 * chunks + 3),
+        load(gb, right.at[1], 2 * chunks + 4),
+    ]
+    others[0].start()
+    for u in range(chunks):
+        act_load(u).start()
+    others[1].start()
+    for u in range(chunks):
+        ge_load(u).start()
+    for c in others[2:]:
+        c.start()
+    barrier = pltpu.get_barrier_semaphore()
+    pl.semaphore_signal(barrier, 1, device_id=twin, device_id_type=pl.DeviceIdType.MESH)
+    pl.semaphore_wait(barrier, 1)
+
+    def swap(source, target, n):
+        return pltpu.make_async_remote_copy(
+            source,
+            target,
+            core_s.at[n],
+            core_r.at[n],
+            device_id=twin,
+            device_id_type=pl.DeviceIdType.MESH,
+        )
+
+    lower, upper = pl.ds(0, unit), pl.ds(unit, unit)
+    reduce_swap = lambda u: swap(send.at[:, u, upper], got.at[:, u, upper], u)
+    expand_swap = lambda u: swap(send.at[u, :, lower], got.at[u, :, lower], chunks + u)
+    output_swap = swap(send_o, got_o, 2 * chunks)
+    others[0].wait()
+
+    def reduce_step(u, carry):
+        act_load(u).wait()
+        whole = dot_left(wide_left[u], right[0]).reshape(2, 4, unit, width)
+        kept, sent = split_cores(core, whole, 0)
+        for part in range(4):
+            keep[part, u, upper] = kept[0, part]
+            send[part, u, upper] = sent[0, part]
+        reduce_swap(u).start()
+        return carry
+
+    lax.fori_loop(0, chunks, reduce_step, 0)
+    others[1].wait()
+
+    def expand_step(u, carry):
+        ge_load(u).wait()
+        whole = dot_left(left[...], wide_right[u]).reshape(nz, 2, unit, width)
+        kept, sent = split_cores(core, whole, 1)
+        for n in range(nz):
+            keep[u, n, lower] = kept[n, 0]
+            send[u, n, lower] = sent[n, 0]
+        expand_swap(u).start()
+        return carry
+
+    lax.fori_loop(0, chunks, expand_step, 0)
+    for c in others[2:]:
+        c.wait()
+    from_mine, from_theirs = dot_left(narrow[0], right[1]), dot_left(narrow[1], right[1])
+    first = jnp.where(core == 0, from_mine, from_theirs)
+    second = jnp.where(core == 0, from_theirs, from_mine)
+    whole = jnp.concatenate([first, second]).reshape(nz, 2, 4, quarter, width)
+    kept, sent = split_cores(core, whole, 1)
     for part in range(4):
-        keep[part] = kept[:, 0, part]
-        send[part] = sent[:, 0, part]
-
-
-def feed_grads(core, low, ge, act, gr, mine, theirs, gb):
+        keep_o[part] = kept[:, 0, part]
+        send_o[part] = sent[:, 0, part]
+    output_swap.start()
+    for u in range(chunks):
+        reduce_swap(u).wait_recv()
+        expand_swap(u).wait_recv()
+    for k, out in enumerate((part0, part1, part2, part3)):
+        part = r ^ k
+        for n in range(nz):
+            total = keep[part, n].astype(F32) + got[part, n].astype(F32)
+            out[n, : 2 * unit, :] = total.astype(BF16)
+    output_swap.wait_recv()
+    for k, out in enumerate((part0, part1, part2, part3)):
+        part = r ^ k
+        total = keep_o[part].astype(F32) + got_o[part].astype(F32)
+        out[:, 2 * unit :, :] = total.astype(BF16)
+    for u in range(chunks):
+        reduce_swap(u).wait_send()
+        expand_swap(u).wait_send()
+    output_swap.wait_send()
+
+
+def feed_grads(low, ge, act, gr, mine, theirs, gb):
     rows, width = low.shape
     wide = ge.shape[1]
     chunks = wide // width
     unit = width // UNITS
     quarter = unit // 4
     nz = UNITS // 2
-    shape = jax.ShapeDtypeStruct((4, nz, 2 * unit + quarter, width), BF16)
-    anywhere = pl.BlockSpec(memory_space=pl.ANY)
-    whole = lambda a: pl.BlockSpec(a.shape, lambda i, *_: (0,) * a.ndim)
-    chunk = pl.BlockSpec((rows, width), lambda i, *_: (0, i))
-    flops = 2 * rows * width * wide
-
-    def call(kernel, grid, in_specs, out_spec, name, flops, *operands, aliases={}):
-        return pl.pallas_call(
-            kernel,
-            out_shape=[shape, shape],
-            grid_spec=pltpu.PrefetchScalarGridSpec(
-                num_scalar_prefetch=1, grid=(grid,), in_specs=in_specs, out_specs=[out_spec] * 2
-            ),
-            input_output_aliases=aliases,
-            compiler_params=params(),
-            cost_estimate=pl.CostEstimate(flops=flops, bytes_accessed=14 << 20, transcendentals=0),
-            name=name,
-        )(core, *operands)
-
-    keep, send = call(
-        expand_grad_kernel,
-        chunks,
-        [whole(low), chunk],
-        pl.BlockSpec((1, nz, unit, width), lambda i, *_: (i, 0, 0, 0)),
-        "expand_grad",
-        flops,
-        low,
-        ge,
-    )
-    keep, send = call(
-        reduce_grad_kernel,
-        chunks,
-        [chunk, whole(gr), anywhere, anywhere],
-        pl.BlockSpec((4, 1, unit, width), lambda i, *_: (0, i, 1, 0)),
-        "reduce_grad",
-        flops,
-        act,
-        gr,
-        keep,
-        send,
-        aliases={3: 0, 4: 1},
-    )
-    return call(
-        output_grad_kernel,
-        1,
-        [whole(mine), whole(theirs), whole(gb), anywhere, anywhere],
-        pl.BlockSpec((4, nz, quarter, width), lambda i, *_: (0, 0, UNITS, 0)),
-        "output_grad",
-        flops // chunks,
-        mine,
-        theirs,
-        gb,
-        keep,
-        send,
-        aliases={4: 0, 5: 1},
-    )
+    vmem = lambda *shape: pltpu.VMEM(shape, BF16)
+    sems = lambda *shape: pltpu.SemaphoreType.DMA(shape)
+    return pl.pallas_call(
+        feed_kernel,
+        out_shape=[jax.ShapeDtypeStruct((nz, 2 * unit + quarter, width), BF16)] * 4,
+        in_specs=[pl.BlockSpec(memory_space=pl.ANY)] * 7,
+        out_specs=[pl.BlockSpec(memory_space=pltpu.VMEM)] * 4,
+        scratch_shapes=[
+            vmem(rows, width),
+            vmem(chunks, rows, width),
+            vmem(chunks, rows, width),
+            vmem(2, rows, width),
+            vmem(2, rows, width // 2),
+            vmem(4, nz, 2 * unit, width),
+            vmem(4, nz, 2 * unit, width),
+            vmem(4, nz, 2 * unit, width),
+            vmem(4, nz, quarter, width),
+            vmem(4, nz, quarter, width),
+            vmem(4, nz, quarter, width),
+            sems(2 * chunks + 5),
+            sems(2 * chunks + 1),
+            sems(2 * chunks + 1),
+        ],
+        compiler_params=params(collective_id=2, has_side_effects=True),
+        cost_estimate=pl.CostEstimate(
+            flops=2 * rows * width * (2 * wide + width), bytes_accessed=25 << 20, transcendentals=0
+        ),
+        name="feed_grads",
+    )(low, ge, act, gr, mine, theirs, gb)
 
 
 def finish_kernel(
-    own, other, dq, dk, dv, square, residual, feed, small_keep, small_send,
-    dx_out, qkv_out, expand_out, reduce_out, output_out, small_out,
-    x, d, w, res, keep, send, twin_part, plane_got, line_part, line_got, around,
-    feed_mine, feed_got, feed_around, to_twin, from_twin, ready,
+    own, other, dq, dk, dv, square, residual, feed0, feed1, feed2, feed3, small_keep, small_send,
+    dx_out, qkv_out, feed_out, small_out,
+    x, d, w, res, keep, send, twin_part, plane_got, plane_part, line_part, line_got, around,
+    feed_in, feed_line, feed_got, feed_around, to_twin, from_twin, ready,
     small_got, small_plane, small_line,
-    loads, core_s, core_r, dx_s, dx_r, move_s, move_r, moved, plane_s, plane_r, line_s, line_r, ring_s, ring_r,
-    feed_s, feed_r, feed_ring_s, feed_ring_r, small_s, small_r,
+    loads, feed_loads, stores, core_s, core_r, dx_s, dx_r, move_s, move_r, moved, plane_s, plane_r, line_s, line_r,
+    ring_s, ring_r, feed_s, feed_r, small_s, small_r,
 ):
     r, s = lax.axis_index("rep"), lax.axis_index("shard")
     z, core = s // 2, s % 2
     half = dq.shape[1]
     rows = own.shape[0]
     block = rows // 2
-    unit = qkv_out.shape[1]
+    unit = w.shape[1]
     quarter = unit // 4
-    nz = feed.shape[0]
+    nz, feed_rows = feed0.shape[:2]
     odd = r % 2
     home = r // 2 == core
     twin = (r, s ^ 1)
@@ -822,69 +1021,88 @@
             source, target, sent, got, device_id=device, device_id_type=mesh_id
         )
 
+    mine, theirs = rows_at(core, rows), rows_at(1 - core, rows)
     local = [
-        pltpu.make_async_copy(own, x.at[0], loads.at[0]),
-        pltpu.make_async_copy(other, x.at[1], loads.at[1]),
-        pltpu.make_async_copy(dq, d.at[0], loads.at[2]),
-        pltpu.make_async_copy(dk, d.at[1], loads.at[3]),
-        pltpu.make_async_copy(dv, d.at[2], loads.at[4]),
-        pltpu.make_async_copy(residual, res, loads.at[5]),
-        pltpu.make_async_copy(feed.at[z], feed_mine, loads.at[6]),
-    ] + [
+        pltpu.make_async_copy(own, x.at[mine], loads.at[0]),
+        pltpu.make_async_copy(other, x.at[theirs], loads.at[1]),
+    ]
+    for m, source in enumerate((dq, dk, dv)):
+        local.append(
+            pltpu.make_async_copy(source, d.at[:, pl.ds(m * half, half)], loads.at[2 + m])
+        )
+    late = [pltpu.make_async_copy(residual, res, loads.at[5])] + [
         pltpu.make_async_copy(
             square.at[:, pl.ds(m * unit, unit), pl.ds(pl.multiple_of(core * half, half), half)],
-            w.at[m],
-            loads.at[7 + m],
+            w.at[:, :, pl.ds(m * half, half)],
+            loads.at[6 + m],
         )
         for m in range(3)
     ]
+    feeds = [
+        pltpu.make_async_copy(source, feed_in.at[k], feed_loads.at[k])
+        for k, source in enumerate((feed0, feed1, feed2, feed3))
+    ]
+    for c in local + feeds + late:
+        c.start()
+    small_core = copy(small_send, small_got, small_s.at[0], small_r.at[0], twin)
+    small_core.start()
     for c in local:
-        c.start()
-    feed_line = [
-        copy(feed.at[z ^ k], feed_got.at[k - 1], feed_s.at[k - 1], feed_r.at[k - 1], line(k))
+        c.wait()
+
+    def cross(i):
+        return copy(send.at[i], twin_part.at[i], core_s.at[i], core_r.at[i], twin)
+
+    def spread(i, side, stage):
+        source = keep if side == 0 else twin_part
+        near, far = (1, 2) if side == 0 else (2, 1)
+        part = (source.at[i, r ^ near], source.at[i, r ^ 3], plane_part.at[i, side])[stage]
+        return copy(
+            part,
+            plane_got.at[stage, i, side],
+            plane_s.at[stage, i, side],
+            plane_r.at[stage, i, side],
+            plane(far if stage == 2 else near),
+        )
+
+    def pass_on(side):
+        source = keep if side == 0 else twin_part
+        far = 2 if side == 0 else 1
+        for i in (0, 1):
+            spread(i, side, 1).wait_recv()
+            total = source[i, r ^ far].astype(F32) + plane_got[1, i, side].astype(F32)
+            plane_part[i, side] = total.astype(BF16)
+            spread(i, side, 2).start()
+
+    for i in (0, 1):
+        whole = dot_left(x[:, i * half : (i + 1) * half], d[...])
+        kept, sent = split_cores(core, whole.reshape(nz // 2, 2, 4, quarter, 3 * half), 1)
+        for part in range(4):
+            keep[i, part] = kept[:, 0, part]
+            send[i, part] = sent[:, 0, part]
+        cross(i).start()
+        for stage in (1, 0):
+            spread(i, 0, stage).start()
+    for c in feeds:
+        c.wait()
+    feed_hops = [
+        copy(feed_line.at[z ^ k], feed_got.at[k - 1], feed_s.at[k - 1], feed_r.at[k - 1], line(k))
         for k in range(1, nz)
     ]
-    small_core = copy(small_send, small_got, small_s.at[0], small_r.at[0], twin)
-    for c in feed_line + [small_core]:
-        c.start()
-    for c in local[:5]:
-        c.wait()
-
-    def cross(m):
-        return copy(send.at[m], twin_part.at[m], core_s.at[m], core_r.at[m], twin)
-
-    def spread(m, side, k):
-        source = keep if side == 0 else twin_part
-        return copy(
-            source.at[m, r ^ k],
-            plane_got.at[k - 1, m, side],
-            plane_s.at[k - 1, m, side],
-            plane_r.at[k - 1, m, side],
-            plane(k),
-        )
-
-    mine, theirs = rows_at(core, rows), rows_at(1 - core, rows)
-
-    def weight(m, carry):
-        whole = dot_left(x[0], d[m, mine, :]) + dot_left(x[1], d[m, theirs, :])
-        kept, sent = split_cores(core, whole.reshape(nz, 2, 4, quarter, half), 1)
-        for part in range(4):
-            keep[m, part] = kept[:, 0, part]
-            send[m, part] = sent[:, 0, part]
-        cross(m).start()
-        for k in (1, 2, 3):
-            spread(m, 0, k).start()
-        return carry
-
-    lax.fori_loop(0, 3, weight, 0)
-    for c in local[7:]:
-        c.wait()
+    for k in range(nz - 1, -1, -1):
+        at = z ^ k
+        total = feed_in[0, at].astype(F32)
+        for n in (1, 2, 3):
+            total = total + feed_in[n, at].astype(F32)
+        feed_line[at] = total.astype(BF16)
+        if k > 0:
+            feed_hops[k - 1].start()
+    for i in (0, 1):
+        cross(i).wait_recv()
+        for stage in (1, 0):
+            spread(i, 1, stage).start()
 
     def share(at):
-        total = dot_right(d[0, at, :], w[0].reshape(-1, half))
-        for m in (1, 2):
-            total = total + dot_right(d[m, at, :], w[m].reshape(-1, half))
-        return total
+        return dot_right(d[at, :], w[...].reshape(-1, 3 * half))
 
     def give(t):
         return copy(to_twin.at[t], from_twin.at[t], dx_s.at[t], dx_r.at[t], twin)
@@ -895,16 +1113,9 @@
         give(t).start()
         return carry
 
+    for c in late:
+        c.wait()
     lax.fori_loop(0, 2, away, 0)
-
-    def take(m, carry):
-        cross(m).wait_recv()
-        for k in (1, 2, 3):
-            spread(m, 1, k).start()
-        return carry
-
-    lax.fori_loop(0, 3, take, 0)
-    local[5].wait()
 
     def stay(turn):
         return pltpu.make_async_copy(ready.at[odd ^ turn], dx_out.at[odd], moved.at[turn])
@@ -938,6 +1149,23 @@
             def _():
                 leave(1, (r ^ 3, s ^ 1)).start()
 
+    pass_on(0)
+    pass_on(1)
+    for i in (0, 1):
+        for side in (0, 1):
+            source = keep if side == 0 else twin_part
+            total = source[i, r].astype(F32)
+            for stage in (0, 2):
+                spread(i, side, stage).wait_recv()
+                total = total + plane_got[stage, i, side].astype(F32)
+            for n in range(nz // 2):
+                line_part[i * (nz // 2) + n, side] = total[n].astype(BF16)
+    qkv_line = [
+        copy(line_part.at[z ^ k], line_got.at[k - 1], line_s.at[k - 1], line_r.at[k - 1], line(k))
+        for k in range(1, nz)
+    ]
+    for c in qkv_line:
+        c.start()
     small_core.wait()
     small_mine = small_keep[...] + small_got[...]
     small_got[...] = small_mine
@@ -947,20 +1175,49 @@
     ]
     for c in small_around:
         c.start()
-    local[6].wait()
-    total = feed_mine[...].astype(F32)
-    for n, c in enumerate(feed_line):
+    total = feed_line[z].astype(F32)
+    for n, c in enumerate(feed_hops):
         c.wait_recv()
         total = total + feed_got[n].astype(F32)
-    feed_around[0] = total.astype(BF16)
-    feed_ring = [
-        copy(
-            feed_around.at[0], feed_around.at[k], feed_ring_s.at[k - 1], feed_ring_r.at[k - 1], plane(k)
-        )
-        for k in (1, 2, 3)
+    feed_around[...] = total.astype(BF16)
+
+    def ring(own_part, out, sent, got, number, pieces):
+        copies = []
+        for n, piece in enumerate(pieces):
+            near, far = (1, 2) if n == 0 else (2, 1)
+            here, there = own_part.at[piece], out.at[(r,) + piece]
+            passed = out.at[(r ^ near,) + piece]
+            at = lambda stage: (sent.at[number, n, stage], got.at[number, n, stage])
+            copies.append(
+                [
+                    copy(here, there, *at(0), plane(near)),
+                    copy(here, there, *at(1), plane(far)),
+                    copy(passed, passed, *at(2), plane(far)),
+                ]
+            )
+        return copies
+
+    def set_out(copies):
+        for one in copies:
+            one[0].start()
+            one[1].start()
+
+    def relay(copies):
+        for one in copies:
+            one[0].wait_recv()
+            one[2].start()
+
+    cut = (feed_rows // 2 + 15) // 16 * 16
+    feed_ring = ring(
+        feed_around, feed_out, ring_s, ring_r, 0, [(pl.ds(0, cut),), (pl.ds(cut, feed_rows - cut),)]
+    )
+    qkv_ring = ring(around, qkv_out, ring_s, ring_r, 1, [(0,), (1,)])
+    kept = [
+        pltpu.make_async_copy(feed_around, feed_out.at[r], stores.at[0]),
+        pltpu.make_async_copy(around, qkv_out.at[r], stores.at[1]),
     ]
-    for c in feed_ring:
-        c.start()
+    set_out(feed_ring)
+    kept[0].start()
     small_total = small_mine
     for n, c in enumerate(small_around):
         c.wait()
@@ -972,50 +1229,27 @@
     ]
     for c in small_along:
         c.start()
-    for m in range(3):
-        for side in (0, 1):
-            source = keep if side == 0 else twin_part
-            total = source[m, r].astype(F32)
-            for k in (1, 2, 3):
-                spread(m, side, k).wait_recv()
-                total = total + plane_got[k - 1, m, side].astype(F32)
-            for n in range(nz):
-                line_part[n, m, side] = total[n].astype(BF16)
-    qkv_line = [
-        copy(line_part.at[z ^ k], line_got.at[k - 1], line_s.at[k - 1], line_r.at[k - 1], line(k))
-        for k in range(1, nz)
-    ]
-    for c in qkv_line:
-        c.start()
+    relay(feed_ring)
     total = line_part[z].astype(F32)
     for n, c in enumerate(qkv_line):
         c.wait_recv()
         total = total + line_got[n].astype(F32)
-    around[0] = total.astype(BF16)
-    qkv_ring = [
-        copy(around.at[0], around.at[k], ring_s.at[k - 1], ring_r.at[k - 1], plane(k)) for k in (1, 2, 3)
-    ]
-    for c in qkv_ring:
-        c.start()
+    around[core] = total[0].astype(BF16)
+    around[1 - core] = total[1].astype(BF16)
+    set_out(qkv_ring)
+    kept[1].start()
     total = small_got[z]
     for n, c in enumerate(small_along):
         c.wait()
         total = total + small_line[n]
     small_out[...] = total
-    width = qkv_out.shape[2]
-    for k in range(4):
-        if k > 0:
-            feed_ring[k - 1].wait()
-        part = r ^ k
-        expand_out[:, rows_at(part, width)] = feed_around[k, :unit, :].astype(F32)
-        reduce_out[rows_at(part, unit), :] = feed_around[k, unit : 2 * unit, :].astype(F32)
-        output_out[rows_at(part, quarter), :] = feed_around[k, 2 * unit :, :].astype(F32)
-    for k in range(4):
-        if k > 0:
-            qkv_ring[k - 1].wait()
-        at = rows_at(r ^ k, quarter)
-        qkv_out[:, at, rows_at(core, half)] = around[k, :, 0].astype(F32)
-        qkv_out[:, at, rows_at(1 - core, half)] = around[k, :, 1].astype(F32)
+    relay(qkv_ring)
+    for c in kept:
+        c.wait()
+    for one in feed_ring + qkv_ring:
+        one[0].wait_send()
+        one[1].wait()
+        one[2].wait()
 
     @pl.when(home)
     def _():
@@ -1027,81 +1261,81 @@
         leave(0, (r ^ 2, s ^ 1)).wait()
         leave(1, (r ^ 3, s ^ 1)).wait()
 
-    for c in feed_line + qkv_line:
+    for c in feed_hops + qkv_line:
         c.wait_send()
-    for m in range(3):
-        cross(m).wait_send()
+    for i in (0, 1):
+        cross(i).wait_send()
         for side in (0, 1):
-            for k in (1, 2, 3):
-                spread(m, side, k).wait_send()
+            for stage in range(3):
+                spread(i, side, stage).wait_send()
     for t in (0, 1):
         give(t).wait_send()
 
 
-def finish(own, other, dq, dk, dv, square, residual, feed, small_keep, small_send, wide):
+def finish(own, other, dq, dk, dv, square, residual, feeds, small_keep, small_send):
     rows, width = own.shape
     half = width // 2
-    nz = feed.shape[0]
+    nz, feed_rows = feeds[0].shape[:2]
     unit = width // UNITS
-    quarter = unit // 4
     block = rows // 2
     anywhere = pl.BlockSpec(memory_space=pl.ANY)
     vmem = pl.BlockSpec(memory_space=pltpu.VMEM)
     sems = lambda *shape: pltpu.SemaphoreType.DMA(shape)
     low = lambda *shape: pltpu.VMEM(shape, BF16)
     high = lambda *shape: pltpu.VMEM(shape, F32)
-    part = (quarter, half)
+    part = (unit // 4, 3 * half)
+    twos = nz // 2
     return pl.pallas_call(
         finish_kernel,
         out_shape=[
             jax.ShapeDtypeStruct((2, block, width), BF16),
-            jax.ShapeDtypeStruct((3, unit, width), F32),
-            jax.ShapeDtypeStruct((unit, wide), F32),
-            jax.ShapeDtypeStruct((4 * unit, width), F32),
-            jax.ShapeDtypeStruct((unit, width), F32),
+            jax.ShapeDtypeStruct((4, 2) + part, BF16),
+            jax.ShapeDtypeStruct((4, feed_rows, width), BF16),
             jax.ShapeDtypeStruct(small_keep.shape[1:], F32),
         ],
-        in_specs=[anywhere] * 8 + [vmem] * 2,
-        out_specs=[anywhere] + [vmem] * 5,
+        in_specs=[anywhere] * 11 + [vmem] * 2,
+        out_specs=[anywhere] * 3 + [vmem],
         scratch_shapes=[
-            low(2, rows, width),
-            low(3, 2 * rows, half),
-            low(3, UNITS, unit, half),
+            low(2 * rows, width),
+            low(2 * rows, 3 * half),
+            low(UNITS, unit, 3 * half),
             high(rows, width),
-            low(3, 4, nz, *part),
-            low(3, 4, nz, *part),
-            low(3, 4, nz, *part),
-            low(3, 3, 2, nz, *part),
-            low(nz, 3, 2, *part),
-            low(nz - 1, 3, 2, *part),
-            low(4, 3, 2, *part),
-            low(*feed.shape[1:]),
-            low(nz - 1, *feed.shape[1:]),
-            low(4, *feed.shape[1:]),
+            low(2, 4, twos, *part),
+            low(2, 4, twos, *part),
+            low(2, 4, twos, *part),
+            low(3, 2, 2, twos, *part),
+            low(2, 2, twos, *part),
+            low(nz, 2, *part),
+            low(nz - 1, 2, *part),
+            low(2, *part),
+            low(4, nz, feed_rows, width),
+            low(nz, feed_rows, width),
+            low(nz - 1, feed_rows, width),
+            low(feed_rows, width),
             low(2, block, width),
             low(2, block, width),
             low(2, block, width),
             high(*small_keep.shape),
             high(3, *small_keep.shape),
             high(nz - 1, *small_keep.shape[1:]),
-            sems(10),
-            sems(3),
-            sems(3),
+            sems(9),
+            sems(4),
             sems(2),
             sems(2),
             sems(2),
             sems(2),
             sems(2),
-            sems(3, 3, 2),
-            sems(3, 3, 2),
+            sems(2),
+            sems(2),
+            sems(2),
+            sems(3, 2, 2),
+            sems(3, 2, 2),
             sems(nz - 1),
             sems(nz - 1),
-            sems(3),
-            sems(3),
+            sems(2, 2, 3),
+            sems(2, 2, 3),
             sems(nz - 1),
             sems(nz - 1),
-            sems(3),
-            sems(3),
             sems(3 + nz),
             sems(3 + nz),
         ],
@@ -1110,7 +1344,7 @@
             flops=2 * 2 * 2 * rows * width * 3 * half, bytes_accessed=150 << 20, transcendentals=0
         ),
         name="finish",
-    )(own, other, dq, dk, dv, square, residual, feed, small_keep, small_send)
+    )(own, other, dq, dk, dv, square, residual, *feeds, small_keep, small_send)
 
 
 def input_grad_kernel(core, own, other, d_ref, w_ref, dw, sums, dx_own, dx_other):
@@ -1170,6 +1404,32 @@
     )(core, own, other, grads, weights)
 
 
+def unpack_kernel(feed, qkv, dq, dk, dv, do, de, dr):
+    unit, width = dq.shape
+    quarter, half = unit // 4, width // 2
+    for part in range(4):
+        de[:, part * width : (part + 1) * width] = feed[part, :unit, :].astype(F32)
+        dr[part * unit : (part + 1) * unit, :] = feed[part, unit : 2 * unit, :].astype(F32)
+        rows = slice(part * quarter, (part + 1) * quarter)
+        do[rows, :] = feed[part, 2 * unit :, :].astype(F32)
+        for m, out in enumerate((dq, dk, dv)):
+            for side in (0, 1):
+                columns = qkv[part, side, :, m * half : (m + 1) * half]
+                out[rows, side * half : (side + 1) * half] = columns.astype(F32)
+
+
+def unpack(feed, qkv, unit, width):
+    shape = lambda *dims: jax.ShapeDtypeStruct(dims, F32)
+    return pl.pallas_call(
+        unpack_kernel,
+        out_shape=[shape(unit, width)] * 4 + [shape(unit, 4 * width), shape(4 * unit, width)],
+        in_specs=[pl.BlockSpec(memory_space=pltpu.VMEM)] * 2,
+        out_specs=[pl.BlockSpec(memory_space=pltpu.VMEM)] * 6,
+        compiler_params=params(),
+        name="unpack",
+    )(feed, qkv)
+
+
 def local(tokens, segment_ids, cotangent, *shards):
     rep_size, shard_size = lax.axis_size("rep"), lax.axis_size("shard")
     rep, shard = lax.axis_index("rep"), lax.axis_index("shard")
@@ -1215,60 +1475,52 @@
         )
 
     tuned = rep_size == 4 and shard_size == UNITS
-    rows_at = width // UNITS
+    unit = width // UNITS
     chunks = shards[4].shape[1] // width
-    small = jnp.concatenate(shards[6:])
+    short = jnp.stack(shards[6:9] + shards[10:])
+    small = jnp.pad(short, ((0, 0), (0, width - short.shape[1])))
+    small = small + jnp.pad(shards[9][None], ((0, EXTRA - 1), (half, half - shards[9].shape[0])))
     if tuned:
-        small_rows = jnp.concatenate([small, jnp.zeros((EXTRA * width - small.shape[0],), BF16)])
-        square_own = jnp.concatenate(list(shards[:4]) + [small_rows.reshape(EXTRA, width)])
-        wide_own = jnp.concatenate(
-            [
-                shards[4].reshape(rows_at, chunks, width).transpose(1, 0, 2),
-                shards[5].reshape(chunks, rows_at, width),
-            ],
-            axis=1,
-        )
-        square, wide_all = gather_weights(square_own, wide_own, shard_size // 2)
-        small = square[:, 4 * rows_at :, :].reshape(shard_size, EXTRA * width)
+        square, wide_all, own, other, cot, segments = gather(
+            shards[:6], small, tokens, cotangent, segment_ids.reshape(2, -1, 128), shard_size // 2
+        )
+        segments = segments.reshape(-1)
+        small = square[:, 4 * unit :, :]
     else:
         wq, wk, wv, wo, we, wr = [lax.all_gather(m, "shard", axis=0, tiled=True) for m in shards[:6]]
         square = jnp.concatenate(
-            [m.reshape(UNITS, rows_at, width) for m in (wq, wk, wv, wo)]
+            [m.reshape(UNITS, unit, width) for m in (wq, wk, wv, wo)]
             + [jnp.zeros((UNITS, EXTRA, width), BF16)],
             axis=1,
         )
         wide_all = jnp.concatenate(
             [
-                we.reshape(UNITS, rows_at, chunks, width).transpose(0, 2, 1, 3),
-                wr.reshape(UNITS, chunks, rows_at, width),
+                we.reshape(UNITS, unit, chunks, width).transpose(0, 2, 1, 3),
+                wr.reshape(UNITS, chunks, unit, width),
             ],
             axis=2,
         )
         small = lax.all_gather(small[None], "shard", axis=0, tiled=True)
-    vectors, at = [], 0
-    for member in shards[6:]:
-        n = member.shape[0]
-        vectors.append(small[:, at : at + n].reshape(1, n * shard_size).astype(F32))
-        at += n
-    bq, bv, bo, be, br, gain1, shift1, gain2, shift2 = vectors
-
-    own = to_sequences(tokens)
-    cot = to_sequences(cotangent)
-    other = swap(own)
-    swapped_ids = swap(segment_ids)
-    ids = jnp.where(rep // 2 == core, segment_ids, swapped_ids)
-    segments = lax.dynamic_index_in_dim(ids, odd, 0, keepdims=False)
+        own = to_sequences(tokens)
+        cot = to_sequences(cotangent)
+        other = swap(own)
+        swapped_ids = swap(segment_ids)
+        ids = jnp.where(rep // 2 == core, segment_ids, swapped_ids)
+        segments = lax.dynamic_index_in_dim(ids, odd, 0, keepdims=False)
+    each = width // shard_size
+    table = small[:, :, :each].transpose(1, 0, 2).reshape(8, width).astype(F32)
+    be = small[:, 0, half : half + shards[9].shape[0]].reshape(1, -1).astype(F32)
+
     blocks = segments.reshape(-1, BLOCK)
     begin = jnp.sum((segments[None, :] < blocks[:, :1]).astype(jnp.int32), axis=1)
     end = jnp.sum((segments[None, :] <= blocks[:, -1:]).astype(jnp.int32), axis=1)
-    seg_col = segments[:, None]
-
-    q, k, v = project(core_arg, own, other, square, bq, bv)
-    attended, lse = attend(begin, end, q, k, v, seg_col)
+    segments = segments[None, :]
+
+    q, k, v = project(core_arg, own, other, square, table)
+    attended, lse = attend(begin, end, q, k, v, segments)
     rows = own.shape[0]
     mine = lax.dynamic_slice_in_dim(attended, core * rows, rows)
     theirs = swap(lax.dynamic_slice_in_dim(attended, (1 - core) * rows, rows))
-    table = jnp.concatenate([bo, br, gain1, shift1, gain2, shift2, bo, bo])
     out, ga_mine, ga_theirs, residual, act, ge, first_low, gr, gb, sums, sum_e = row_local(
         core_arg, own, mine, theirs, cot, square, wide_all, table, be
     )
@@ -1278,7 +1530,7 @@
         dwe = weight_grad(first_low, ge, F32)
         dwo_mine, dwo_theirs = weight_grad(mine, gb, F32), weight_grad(theirs, gb, F32)
         dq, dk, dv, sum_qv = attend_back(
-            core_arg, begin, end, q, k, v, attended, ga_mine, ga_other, lse, seg_col
+            core_arg, begin, end, q, k, v, attended, ga_mine, ga_other, lse, segments
         )
         dw, sum_qkv, dx_own, dx_other = input_grad(
             core_arg, own, other, jnp.stack([dq, dk, dv]), square, F32
@@ -1325,25 +1577,12 @@
         pairs = [(flat(r, s), flat(r ^ hop, s)) for r in range(4) for s in range(shard_size)]
         return lax.ppermute(array, both, pairs)
 
-    def pick(array, n):
-        return lax.dynamic_index_in_dim(array, n, 0, keepdims=False)
-
-    feed_keep, feed_send = feed_grads(core_arg, first_low, ge, act, gr, mine, theirs, gb)
-    feed_got = swap(feed_send)
-    feed_parts = [
-        pick(feed_keep, rep ^ hop).astype(F32) + pick(feed_got, rep ^ hop).astype(F32)
-        for hop in range(4)
-    ]
-    feed_sent = [part.astype(BF16) for part in feed_parts[1:]]
-    feed_sent, ga_other = lax.optimization_barrier((feed_sent, ga_other))
-    feed = feed_parts[0]
-    for hop in (1, 2, 3):
-        feed = feed + plane_send(feed_sent[hop - 1], hop).astype(F32)
-    feed = feed.astype(BF16)
+    feeds = feed_grads(first_low, ge, act, gr, mine, theirs, gb)
+    feeds, ga_other = lax.optimization_barrier((feeds, ga_other))
+    feeds = [feeds[0]] + [plane_send(feeds[hop], hop) for hop in (1, 2, 3)]
     dq, dk, dv, sum_qv = attend_back(
-        core_arg, begin, end, q, k, v, attended, ga_mine, ga_other, lse, seg_col
+        core_arg, begin, end, q, k, v, attended, ga_mine, ga_other, lse, segments
     )
-    unit = width // shard_size
     wide_unit = sum_e.shape[1] // shard_size
 
     def place(part):
@@ -1363,18 +1602,19 @@
     ).reshape(nz, 2, 8, 256)
     small_keep = lax.dynamic_index_in_dim(table, core, 1, keepdims=False)
     small_send = lax.dynamic_index_in_dim(table, 1 - core, 1, keepdims=False)
-    dx, dqkv, dwe, dwr, dwo, small = finish(
-        own, other, dq, dk, dv, square, residual, feed, small_keep, small_send, be.shape[1]
+    dx, dqkv, feed, small = finish(
+        own, other, dq, dk, dv, square, residual, feeds, small_keep, small_send
     )
+    dwq, dwk, dwv, dwo, dwe, dwr = unpack(feed, dqkv, unit, width)
     small = small.reshape(-1)
     dbq, dbv, dbo, dbr, dg1, ds1, dg2, ds2 = [small[n * unit : (n + 1) * unit] for n in range(8)]
     dbe = small[8 * unit : 8 * unit + wide_unit]
     return (
         from_sequences(out),
         dx,
-        dqkv[0],
-        dqkv[1],
-        dqkv[2],
+        dwq,
+        dwk,
+        dwv,
         dwo,
         dwe,
         dwr,

time: 395 us -> 330 us (0.84)
  starting transfers between devices: 31 us -> 6.6 us
  waiting for transfers between devices: 17.5 us -> 1.17 us
  other arithmetic: 20.3 us -> 7.67 us
  local copies, waits for them, and re-layouts: 27 us -> 15.3 us
    ppermute x1, waiting for transfers between devices: 12.3 us -> 0.01 us  [from_sequences(): odd_part = lax.ppermute(jnp.where(odd == 0, b, a), both, route(1, True))]
    ppermute x4 -> x0, starting transfers between devices: 11.8 us -> none  [the longest x2 8.14 us: to_sequences(): even_part = lax.ppermute(jnp.where(odd == 0, a, b), both, route(0))]
    ppermute x5 -> x2, starting transfers between devices: 11.3 us -> 0.82 us  [swap(): return lax.ppermute(array, both, swap_pairs)]
    unnamed x67 -> x10, local copies, waits for them, and re-layouts: 13 us -> 4.36 us
    convert_element_type x2, other arithmetic: 9.04 us -> 1.34 us  [the longest x1 0.72 us: local(): table = small[:, :, :each].transpose(1, 0, 2).reshape(8, width).astype(F32)]
    select_n x5 -> x0, other arithmetic: 5.09 us -> none  [the longest x2 2.82 us: to_sequences(): even_part = lax.ppermute(jnp.where(odd == 0, a, b), both, route(0))]
    pallas_call x4 -> x3, Pallas kernels: 94.1 us -> 99 us  [the longest x1 74.2 us: gather(): pl.pallas_call(functools.partial(gather_kernel, nz), out_shape=[jax.Shape...]
  transfers between devices with their start and end apart: 14 -> 7, of which waited for: 3 -> 2; matrix products, arithmetic and copies ran while one was open for 7% -> 3% of each run, Pallas kernels for 42% -> 23%
where the time goes in v4:
time: 330 us; the launch traced here: 329 us
  Pallas kernels  298 us (90%)
  local copies, waits for them, and re-layouts  15.3 us (5%)
  other arithmetic  7.67 us (2%)
  starting transfers between devices  6.6 us (2%)
    pallas_call x1, Pallas kernels, gather(): pl.pallas_call(functools.partial(gather_kernel, nz), out_shape=[jax.Shape...  74.2 us
    pallas_call x1, Pallas kernels, finish(): pl.pallas_call(finish_kernel, out_shape=[jax.ShapeDtypeStruct((2, block,...  66.7 us
    pallas_call x1, Pallas kernels, attend_back(): pl.pallas_call(attend_back_kernel, out_shape=[jax.ShapeDtypeStruct((rows,...  52.9 us
    pallas_call x1, Pallas kernels, row_local(): pl.pallas_call(rows_kernel, out_shape=[shape(width, BF16), shape(half, BF...  39.6 us
    pallas_call x1, Pallas kernels, attend(): pl.pallas_call(attend_kernel, out_shape=[jax.ShapeDtypeStruct((rows, widt...  31.1 us
    pallas_call x1, Pallas kernels, feed_grads(): pl.pallas_call(feed_kernel, out_shape=[jax.ShapeDtypeStruct((nz, 2 * unit...  21.6 us
    pallas_call x1, Pallas kernels, project(): pl.pallas_call(qkv_kernel, out_shape=[jax.ShapeDtypeStruct((2 * rows, hal...  8.61 us
  transfers between devices with their start and end apart: 7, of which 2 were waited for; matrix products, arithmetic and copies ran while one was open for 3% of the time, Pallas kernels for 23%

profile of v4, /device:TPU:0, one launch (start us, length us, event | category | flops | bytes accessed | tf_op | source)
XLA Modules:
  0.0 329.4 jit_solution(10446814316694413269)
XLA Ops:
  0.7 1.3 copy.50
  2.0 0.7 broadcast_in_dim.6
  2.7 0.8 stack.44
  4.1 74.2 %gather.1 = (bf16[8,392,768]{2,1,0:T(8,128)(2,1)}, bf16[8,4,192,768]{3,2,1,0:T(8,128)(2,1)}, bf16[1024,768]{1,0:T(8,128)(2,1)}, bf16[1024,768]{1,0:T(8,128)(2,1)...) custom-call(bf16[96,768]{1,0:T(8,128)(2,1)} %wq.1, bf16[96,768]{1,0:T(8,128)(2,1)} %wk.1, bf16[96,768]{1,0:T(8,128)(2,1)} %wv.1, ...), custom_call_target="tpu_custom_call" | custom-call | bytes 157286400 | tf_op jit(solution)/shard_map/gather/pallas_call | solution.py:317
  78.3 0.7 convert_bitcast_fusion
  79.0 0.7 reshape.80.vectors
  79.7 0.7 reshape_reshape.3
  80.6 0.9 convert_reduce_fusion
  82.1 8.6 %project.1 = (bf16[2048,384]{1,0:T(8,128)(2,1)}, bf16[2048,384]{1,0:T(8,128)(2,1)}, bf16[2048,384]{1,0:T(8,128)(2,1)}) custom-call(s32[1]{0:T(128)} %bitcast.core, bf16[1024,768]{1,0:T(8,128)(2,1)} %get-tuple-element.62.own.x_ref, bf16[1024,768]{1,0:T(8,128)(2,1)} %get-tuple-element.64.other, ...), custom_call_target="tpu_custom_call" | custom-call | flops 3623878656 | bytes 10485760 | tf_op jit(solution)/shard_map/project/pallas_call | solution.py:383
  90.7 31.1 %attend.1 = (bf16[2048,384]{1,0:T(8,128)(2,1)}, f32[6,2048]{1,0:T(8,128)}) custom-call(s32[8]{0:T(128)} %get-tuple-element.139.low, s32[8]{0:T(128)} %get-tuple-element.136.high, bf16[2048,384]{1,0:T(8,128)(2,1)} %get-tuple-element.66.q_ref, bf16[2048,384]{1,0:T(8,128)(2,1)} %get-tuple-element.67.k_ref, bf16[2048,384]{1,0:T(8,128)(2,1)} %get-tuple-element.68.v_ref, ...), custom_call_target="tpu_custom_call" | custom-call | flops 6442450944 | bytes 8388608 | tf_op jit(solution)/shard_map/attend/pallas_call | solution.py:497
  121.8 2.4 constant_dynamic-slice_fusion
  124.6 0.8 slice.75
  125.4 0.6 convert.3.be
  126.5 0.9 copy-done.1
  127.4 39.6 %row_local.1 = (bf16[1024,768]{1,0:T(8,128)(2,1)}, bf16[1024,384]{1,0:T(8,128)(2,1)}, bf16[1024,384]{1,0:T(8,128)(2,1)}, f32[1024,768]{1,0:T(8,128)}, bf16[1024,...) custom-call(s32[1]{0:T(128)} %bitcast.core, ...), custom_call_target="tpu_custom_call" | custom-call | flops 21743271936 | bytes 41943040 | tf_op jit(solution)/shard_map/row_local/pallas_call | solution.py:760
  167.4 1.0 slice_reduce_fusion
  169.4 1.4 reduce.20
  170.8 1.5 broadcast_select_fusion.1
  172.3 0.7 collective-permute-start.1
  173.0 1.5 collective-permute-start.2
  174.5 21.6 %feed_grads.1 = (bf16[4,216,768]{2,1,0:T(8,128)(2,1)}, bf16[4,216,768]{2,1,0:T(8,128)(2,1)}, bf16[4,216,768]{2,1,0:T(8,128)(2,1)}, bf16[4,216,768]{2,1,0:T(8,128)(2,1)}) custom-call(bf16[1024,768]{1,0:T(8,128)(2,1)} %get-tuple-element.74.low, bf16[1024,3072]{1,0:T(8,128)(2,1)} %get-tuple-element.75.ge, bf16[1024,3072]{1,0:T(8,128)(2,1)} %get-tuple-element.76.act, ...), custom_call_target="tpu_custom_call" | custom-call | flops 10871635968 | bytes 26214400 | tf_op jit(solution)/shard_map/feed_grads/pallas_call | solution.py:960
  196.1 0.6 collective-permute-start.4
  196.8 2.9 collective-permute-start.6
  199.7 52.9 %attend_back.1 = (bf16[2048,384]{1,0:T(8,128)(2,1)}, bf16[2048,384]{1,0:T(8,128)(2,1)}, bf16[2048,384]{1,0:T(8,128)(2,1)}, f32[2,8,384]{2,1,0:T(8,128)}) custom-call(s32[1]{0:T(128)} %bitcast.core, s32[8]{0:T(128)} %get-tuple-element.140.low, s32[8]{0:T(128)} %get-tuple-element.135.high, bf16[2048,384]{1,0:T(8,128)(2,1)} %get-tuple-element.66.q_ref, ...), custom_call_target="tpu_custom_call" | custom-call | flops 16106127360 | bytes 16777216 | tf_op jit(solution)/shard_map/attend_back/pallas_call | solution.py:628
  252.6 0.7 slice_reduce_fusion.6
  253.6 0.6 dynamic-slice_bitcast_fusion
  254.4 1.3 pad_maximum_fusion
  255.7 0.7 collective-permute-done.6.feed3
  256.4 66.7 %finish.1 = (bf16[2,512,768]{2,1,0:T(8,128)(2,1)}, bf16[4,2,24,1152]{3,2,1,0:T(8,128)(2,1)}, bf16[4,216,768]{2,1,0:T(8,128)(2,1)}, f32[8,256]{1,0:T(8,128)}) custom-call(bf16[1024,768]{1,0:T(8,128)(2,1)} %get-tuple-element.62.own.x_ref, bf16[1024,768]{1,0:T(8,128)(2,1)} %get-tuple-element.64.other, bf16[2048,384]{1,0:T(8,128)(2,1)} %get-tuple-element.86.dq, ...), custom_call_target="tpu_custom_call" | custom-call | flops 7247757312 | bytes 157286400 | tf_op jit(solution)/shard_map/finish/pallas_call | solution.py:1288
  323.0 0.8 copy.48
  325.0 3.2 unpack.1
  328.3 1.1 copy.52
  (36 shorter events, 5.2 us)
Async XLA Ops:
  124.2 2.3 collective-permute-start
  126.5 0.9 copy-start.1
  167.0 29.1 %collective-permute-start.3 = (bf16[1024,384]{1,0:T(8,128)(2,1)}, bf16[1024,384]{1,0:T(8,128)(2,1)}, u32[]{:S(2)}, u32[]{:S(2)}) collective-permute-start(bf16[1024,384]{1,0:T(8,128)(2,1)} %get-tuple-element.83), channel_id=1, source_target_pairs={{0,1},{1,0},{2,3},{3,2},{4,5},{5,4},{6,7},{7,6},{8,9},{9,8},{10,11... | collective-permute-start | bytes 2359304 | tf_op jit(solution)/shard_map/ppermute | solution.py:1456
  172.3 82.0 %collective-permute-start.1 = (bf16[512,768]{1,0:T(8,128)(2,1)S(1)}, bf16[512,768]{1,0:T(8,128)(2,1)S(1)}, u32[]{:S(2)}, u32[]{:S(2)}) collective-permute-start(bf16[512,768]{1,0:T(8,128)(2,1)S(1)} %get-tuple-element.119), channel_id=1, source_target_pairs={{0,0},{16,1},{2,2},{18,3},{4,4},{20,5},{6,6},{22,7},{8,8},{24,9},{... | collective-permute-start | bytes 2359304 | tf_op jit(solution)/shard_map/ppermute | solution.py:1471
  173.0 81.3 %collective-permute-start.2 = (bf16[512,768]{1,0:T(8,128)(2,1)S(1)}, bf16[512,768]{1,0:T(8,128)(2,1)S(1)}, u32[]{:S(2)}, u32[]{:S(2)}) collective-permute-start(bf16[512,768]{1,0:T(8,128)(2,1)S(1)} %get-tuple-element.120), channel_id=1, source_target_pairs={{8,0},{24,1},{10,2},{26,3},{12,4},{28,5},{14,6},{30,7},{0,8},{16,9... | collective-permute-start | bytes 2359304 | tf_op jit(solution)/shard_map/ppermute | solution.py:1472
  196.1 59.5 %collective-permute-start.4 = (bf16[4,216,768]{2,1,0:T(8,128)(2,1)}, bf16[4,216,768]{2,1,0:T(8,128)(2,1)}, u32[]{:S(2)}, u32[]{:S(2)}) collective-permute-start(bf16[4,216,768]{2,1,0:T(8,128)(2,1)} %get-tuple-element.91), channel_id=1, source_target_pairs={{0,8},{1,9},{2,10},{3,11},{4,12},{5,13},{6,14},{7,15},{8,0},{9,1},... | collective-permute-start | bytes 3981320 | tf_op jit(solution)/shard_map/ppermute | solution.py:1578
  196.8 58.9 %collective-permute-start.5 = (bf16[4,216,768]{2,1,0:T(8,128)(2,1)}, bf16[4,216,768]{2,1,0:T(8,128)(2,1)}, u32[]{:S(2)}, u32[]{:S(2)}) collective-permute-start(bf16[4,216,768]{2,1,0:T(8,128)(2,1)} %get-tuple-element.92), channel_id=1, source_target_pairs={{0,16},{1,17},{2,18},{3,19},{4,20},{5,21},{6,22},{7,23},{8,24},{9,... | collective-permute-start | bytes 3981320 | tf_op jit(solution)/shard_map/ppermute | solution.py:1578
  196.8 59.6 %collective-permute-start.6 = (bf16[4,216,768]{2,1,0:T(8,128)(2,1)}, bf16[4,216,768]{2,1,0:T(8,128)(2,1)}, u32[]{:S(2)}, u32[]{:S(2)}) collective-permute-start(bf16[4,216,768]{2,1,0:T(8,128)(2,1)} %get-tuple-element.93), channel_id=1, source_target_pairs={{0,24},{1,25},{2,26},{3,27},{4,28},{5,29},{6,30},{7,31},{8,16},{9,... | collective-permute-start | bytes 3981320 | tf_op jit(solution)/shard_map/ppermute | solution.py:1578
  323.0 5.2 %copy-start = (bf16[2,512,768]{2,1,0:T(8,128)(2,1)S(1)}, bf16[2,512,768]{2,1,0:T(8,128)(2,1)}, u32[]{:S(2)}) copy-start(bf16[2,512,768]{2,1,0:T(8,128)(2,1)} %get-tuple-element.159) | copy-start | bytes 4718596
